TPU v7x, 32 devices: a whole 2x2x4 slice. The times are simulated.
32 devices in a mesh: snap: 4 (over z), vert: 8 (over y, x, core).
Axes of the slice: x: 2, y: 2, z: 4, core: 2. Of those that a mesh axis runs over, the one named last changes fastest.
Arguments:
- features: bfloat16 [4, 6144, 128], P('snap', 'vert'), may hold values from -6 to 6
- adjacency_tiles: bfloat16 [4, 96, 128, 128], P('snap', 'vert'), may hold values from -0.375 to 0.375
- src_block: int32 [4, 96], P('snap', 'vert'), may hold values from 0 to 47, as said below
- dst_block: int32 [4, 96], P('snap', 'vert'), may hold values from 0 to 5
- block_count: int32 [4, 8], P('snap', 'vert'), may hold values from 6 to 12, as said below
- w_conv: bfloat16 [128, 512], replicated, may hold values from -0.5 to 0.5
- b_conv: float32 [512], replicated, may hold values from -3 to 3
- w_input: bfloat16 [512, 2048], replicated, may hold values from -0.25 to 0.25
- w_state: bfloat16 [512, 2048], replicated, may hold values from -0.25 to 0.25
- b_gates: float32 [2048], replicated, may hold values from -3 to 3
Outputs:
- hidden_seq: bfloat16 [4, 6144, 512], P('snap', 'vert')
Inputs may be any that keep to these rules, and one draw needn't show every extreme that they name: `src_block`: slot s of owner v names a column block held by owner v - 1, v or v + 1 (clipped to the owners that exist); its first slot names one of owner v - 1 and its second one of owner v + 1 where those exist. `block_count`: in every snapshot some owner has all 12 slots live.
All inputs are finite; a program needn't handle non-finite values.
Results may differ from a plain program's by a relative error of at most 0.0044.
Values may be sent and summed in bfloat16 or wider, within the bound.
No kernel may reach another device: no remote copies, remote signals or barrier semaphores. Data moves between devices by JAX's collectives and lax.ppermute only.
A program may use at most 64 MiB of HBM per device.

v0:
```python
import jax
import jax.numpy as jnp
from jax import lax
from jax.sharding import PartitionSpec as P

forget_bias = 2.0


def padded(cells, sides, width):
    for axis, dim in sides:
        count = lax.axis_size(axis)
        ends = count - 1
        head = lax.slice_in_dim(cells, 0, width, axis=dim)
        tail = lax.slice_in_dim(cells, cells.shape[dim] - width, cells.shape[dim], axis=dim)
        cells = jnp.concatenate(
            [
                lax.ppermute(tail, axis, [(i, (i + 1) % count) for i in range(ends)]),
                cells,
                lax.ppermute(head, axis, [((i + 1) % count, i) for i in range(ends)]),
            ],
            axis=dim,
        )
    return cells


def gate_step(hidden, cell, pre_gates, w_state, b_gates):
    width = w_state.shape[0]
    gates = pre_gates + jnp.dot(hidden, w_state, preferred_element_type=jnp.float32) + b_gates
    input_gate = jax.nn.sigmoid(gates[:, :width])
    forget_gate = jax.nn.sigmoid(gates[:, width : 2 * width] + forget_bias)
    candidate = jnp.tanh(gates[:, 2 * width : 3 * width])
    output_gate = jax.nn.sigmoid(gates[:, 3 * width :])
    new_cell = forget_gate * cell + input_gate * candidate
    new_hidden = (output_gate * jnp.tanh(new_cell)).astype(jnp.bfloat16)
    return (new_hidden, new_cell)


def shards(
    features,
    adjacency_tiles,
    src_block,
    dst_block,
    block_count,
    w_conv,
    b_conv,
    w_input,
    w_state,
    b_gates,
):
    vert_rows = features.shape[1]
    feat_width = features.shape[2]
    block_rows = adjacency_tiles.shape[2]
    slot_count = adjacency_tiles.shape[1]
    row_blocks = vert_rows // block_rows
    hid_width = w_state.shape[0]
    owner_index = lax.axis_index("vert")
    window = padded(features, (("vert", 1),), vert_rows)
    window_blocks = window[0].reshape(3 * row_blocks, block_rows, feat_width)
    local_index = src_block[0] - (owner_index - 1) * row_blocks
    picked = jnp.take(window_blocks, local_index, axis=0)
    product = jnp.einsum(
        "ebk,ekf->ebf", adjacency_tiles[0], picked, preferred_element_type=jnp.float32
    )
    alive = jnp.arange(slot_count, dtype=jnp.int32) < block_count[0, 0]
    selector = (
        (dst_block[0][None, :] == jnp.arange(row_blocks, dtype=jnp.int32)[:, None]) & alive[None, :]
    ).astype(jnp.float32)
    summed = jnp.einsum("re,ebf->rbf", selector, product, precision=lax.Precision.HIGHEST)
    summed = summed.reshape(vert_rows, feat_width).astype(jnp.bfloat16)
    conv = jax.nn.relu(jnp.dot(summed, w_conv, preferred_element_type=jnp.float32) + b_conv).astype(
        jnp.bfloat16
    )
    regrouped = lax.all_to_all(conv[None], "snap", split_axis=1, concat_axis=0, tiled=True)
    pre_all = jnp.einsum("tvp,pg->tvg", regrouped, w_input, preferred_element_type=jnp.float32)
    slice_rows = regrouped.shape[1]

    def advance(carry, pre_now):
        hidden, cell = carry
        new_hidden, new_cell = gate_step(hidden, cell, pre_now, w_state, b_gates)
        return ((new_hidden, new_cell), new_hidden)

    start_state = (
        jnp.zeros((slice_rows, hid_width), jnp.bfloat16),
        jnp.zeros((slice_rows, hid_width), jnp.float32),
    )
    _, sequence = lax.scan(advance, start_state, pre_all)
    return lax.all_to_all(sequence, "snap", split_axis=0, concat_axis=1, tiled=True)


def solution(mesh):
    placed = (
        P("snap", "vert", None),
        P("snap", "vert", None, None),
        P("snap", "vert"),
        P("snap", "vert"),
        P("snap", "vert"),
        P(),
        P(),
        P(),
        P(),
        P(),
    )
    return jax.shard_map(
        shards, mesh=mesh, in_specs=placed, out_specs=P("snap", "vert", None), check_vma=False
    )
```

profile of v0, /device:TPU:4, one launch (start us, length us, event | category | flops | bytes accessed | tf_op | source)
XLA Modules:
  0.0 96.3 jit_solution(7456984444435545295)
XLA Ops:
  0.0 2.0 %collective-permute-start = (bf16[1,768,128]{2,1,0:T(8,128)(2,1)}, bf16[1,768,128]{2,1,0:T(8,128)(2,1)S(1)}, u32[]{:S(2)}, u32[]{:S(2)}) collective-permute-start(bf16[1,768,128]{2,1,0:T(8,128)(2,1)} %param.12), channel_id=1, source_target_pairs={{0,1},{1,2},{2,3},{3,4},{4,5},{5,6},{6,7},{8,9},{9,10},{10,11},{11... | collective-permute-start | bytes 589832 | tf_op jit(solution)/shard_map/ppermute | solution.py:17
  2.1 4.5 %collective-permute-start.1 = (bf16[1,768,128]{2,1,0:T(8,128)(2,1)}, bf16[1,768,128]{2,1,0:T(8,128)(2,1)S(1)}, u32[]{:S(2)}, u32[]{:S(2)}) collective-permute-start(bf16[1,768,128]{2,1,0:T(8,128)(2,1)} %param.12), channel_id=1, source_target_pairs={{1,0},{2,1},{3,2},{4,3},{5,4},{6,5},{7,6},{9,8},{10,9},{11,10},{12... | collective-permute-start | bytes 589832 | tf_op jit(solution)/shard_map/ppermute | solution.py:19
  6.6 0.7 fusion.32
  7.9 0.7 compare_and_fusion
  8.6 1.5 %collective-permute-done.1 = bf16[1,768,128]{2,1,0:T(8,128)(2,1)S(1)} collective-permute-done((bf16[1,768,128]{2,1,0:T(8,128)(2,1)}, bf16[1,768,128]{2,1,0:T(8,128)(2,1)S(1)}, u32[]{:S(2)}, u32[]{:S(2)}) %collective-permute-start.1) | collective-permute-done | bytes 196640 | tf_op jit(solution)/shard_map/ppermute | solution.py:19
  10.1 1.0 %pad_maximum_fusion = bf16[1,2304,128]{2,1,0:T(8,128)(2,1)S(1)} fusion(bf16[1,768,128]{2,1,0:T(8,128)(2,1)S(1)} %collective-permute-done.1, bf16[1,768,128]{2,1,0:T(8,128)(2,1)} %param.12, bf16[1,768,128]{2,1,0:T(8,128)(2,1)S(1)} %collective-permute-done), kind=kLoop, calls=%fused_computation.33 | loop fusion | flops 1769472 | bytes 1179648 | tf_op jit(solution)/shard_map/concatenate | solution.py:15
  11.1 0.6 gather_fusion
  11.7 1.4 %convolution_bitcast_fusion = f32[12,128,128]{1,2,0:T(8,128)} fusion(bf16[1,12,128,128]{3,2,1,0:T(8,128)(2,1)S(1)} %copy-done.2, bf16[12,128,128]{2,1,0:T(8,128)(2,1)S(1)} %gather_fusion, pred[12]{0:T(512)(128)(4,1)S(1)} %compare_and_fusion), kind=kOutput, calls=%fused_computation.31 | convolution fusion | flops 50528256 | bytes 1572876 | tf_op jit(solution)/shard_map/ebk,ekf->ebf/dot_general | solution.py:61
  13.1 1.7 %copy.16 = f32[12,128,128]{2,0,1:T(8,128)S(1)} copy(f32[12,128,128]{1,2,0:T(8,128)} %convolution_bitcast_fusion) | data formatting | bytes 1572864 | tf_op jit(solution)/shard_map/ebk,ekf->ebf/dot_general | solution.py:61
  15.7 2.4 %copy.22 = bf16[1,768,512]{2,0,1:T(2,128)(2,1)} copy(bf16[1,768,512]{2,1,0:T(8,128)(2,1)S(1)} %fusion.22) | data formatting | bytes 1572864 | tf_op jit(solution)/shard_map/broadcast_in_dim | solution.py:73
  18.6 6.4 %reduce = bf16[768,512]{1,0:T(8,128)(2,1)S(1)} reduce(bf16[768,1,512]{2,1,0:T(2,128)(2,1)} %bitcast.45, bf16[]{:T(256)} %broadcast.89), dimensions={1}, to_apply=%bitcast.37.reduce_sub_computation | reduce | bytes 1572866
  25.0 1.4 %reshape.53 = bf16[4,2,49152]{2,1,0:T(2,128)(2,1)} reshape(bf16[768,512]{1,0:T(8,128)(2,1)S(1)} %reduce) | data formatting | bytes 1572864
  26.4 4.9 %all-to-all-start = ((bf16[4,2,49152]{2,1,0:T(2,128)(2,1)}), bf16[4,2,49152]{2,1,0:T(2,128)(2,1)S(1)}, u32[]{:S(2)}, u32[]{:S(2)}) async-start(bf16[4,2,49152]{2,1,0:T(2,128)(2,1)} %reshape.53), calls=%async_computation | async-start | bytes 1572864 | tf_op jit(solution)/shard_map/all_to_all | solution.py:73
  31.3 21.0 %all-to-all-done = bf16[4,2,49152]{2,1,0:T(2,128)(2,1)S(1)} async-done(((bf16[4,2,49152]{2,1,0:T(2,128)(2,1)}), bf16[4,2,49152]{2,1,0:T(2,128)(2,1)S(1)}, u32[]{:S(2)}, u32[]{:S(2)}) %all-to-all-start) | async-done | bytes 786464 | tf_op jit(solution)/shard_map/all_to_all | solution.py:73
  52.3 2.1 %reshape.54 = bf16[768,1,512]{2,1,0:T(2,128)(2,1)} reshape(bf16[4,2,49152]{2,1,0:T(2,128)(2,1)S(1)} %all-to-all-done) | data formatting | bytes 1572864
  54.4 1.6 %copy.20 = bf16[1,768,512]{2,1,0:T(8,128)(2,1)S(1)} copy(bf16[1,768,512]{2,0,1:T(2,128)(2,1)} %bitcast.46) | data formatting | bytes 1572864
  56.0 4.5 %fusion.20 = f32[4,192,2048]{2,1,0:T(8,128)} fusion(bf16[4,192,512]{2,1,0:T(8,128)(2,1)S(1)} %bitcast.47, bf16[512,2048]{1,0:T(8,128)(2,1)S(1)} %copy-done), kind=kOutput, calls=%fused_computation.27 | convolution fusion | flops 1610612736 | bytes 9175040 | tf_op jit(solution)/shard_map/tvp,pg->tvg/dot_general | solution.py:74
  60.5 12.3 %while.15 = (s32[]{:T(128)}, bf16[192,512]{1,0:T(8,128)(2,1)S(1)}, f32[192,512]{1,0:T(8,128)S(1)}, bf16[4,192,512]{2,1,0:T(8,128)(2,1)S(1)}, f32[4,192,2048]{2,1...) while((s32[]{:T(128)}, bf16[192,512]{1,0:T(8,128)(2,1)S(1)}, ...), condition=%wide.region_1.2_spmd.clone, body=%wide.region_0.1_spmd.clone.sunk | while | flops 405110784 | bytes 8200304 | solution.py:86
  60.5 2.6 %fusion.46 = f32[192,2048]{1,0:T(8,128)S(1)} fusion(bf16[512,2048]{1,0:T(8,128)(2,1)} %get-tuple-element.156, f32[4,192,2048]{2,1,0:T(8,128)} %get-tuple-element.155, s32[]{:T(128)} %get-tuple-element.142, f32[2048]{0:T(1024)S(1)} %get-tuple-element.157, bf16[192,512]{1,0:T(8,128)(2,1)S(1)} %get-tuple-element.143, pred[]{:T(512)S(6)} %compare.3), kind=kOutput, calls=%fused_computation.2.clone.1 | convolution fusion | flops 403537920 | bytes 5447685 | tf_op jit(solution)/shard_map/while/body/eval_jaxpr/dot_general | solution.py:28
  63.5 2.6 %fusion.46 = f32[192,2048]{1,0:T(8,128)S(1)} fusion(bf16[512,2048]{1,0:T(8,128)(2,1)} %get-tuple-element.156, f32[4,192,2048]{2,1,0:T(8,128)} %get-tuple-element.155, s32[]{:T(128)} %get-tuple-element.142, f32[2048]{0:T(1024)S(1)} %get-tuple-element.157, bf16[192,512]{1,0:T(8,128)(2,1)S(1)} %get-tuple-element.143, pred[]{:T(512)S(6)} %compare.3), kind=kOutput, calls=%fused_computation.2.clone.1 | convolution fusion | flops 403537920 | bytes 5447685 | tf_op jit(solution)/shard_map/while/body/eval_jaxpr/dot_general | solution.py:28
  66.6 2.6 %fusion.46 = f32[192,2048]{1,0:T(8,128)S(1)} fusion(bf16[512,2048]{1,0:T(8,128)(2,1)} %get-tuple-element.156, f32[4,192,2048]{2,1,0:T(8,128)} %get-tuple-element.155, s32[]{:T(128)} %get-tuple-element.142, f32[2048]{0:T(1024)S(1)} %get-tuple-element.157, bf16[192,512]{1,0:T(8,128)(2,1)S(1)} %get-tuple-element.143, pred[]{:T(512)S(6)} %compare.3), kind=kOutput, calls=%fused_computation.2.clone.1 | convolution fusion | flops 403537920 | bytes 5447685 | tf_op jit(solution)/shard_map/while/body/eval_jaxpr/dot_general | solution.py:28
  69.7 2.6 %fusion.46 = f32[192,2048]{1,0:T(8,128)S(1)} fusion(bf16[512,2048]{1,0:T(8,128)(2,1)} %get-tuple-element.156, f32[4,192,2048]{2,1,0:T(8,128)} %get-tuple-element.155, s32[]{:T(128)} %get-tuple-element.142, f32[2048]{0:T(1024)S(1)} %get-tuple-element.157, bf16[192,512]{1,0:T(8,128)(2,1)S(1)} %get-tuple-element.143, pred[]{:T(512)S(6)} %compare.3), kind=kOutput, calls=%fused_computation.2.clone.1 | convolution fusion | flops 403537920 | bytes 5447685 | tf_op jit(solution)/shard_map/while/body/eval_jaxpr/dot_general | solution.py:28
  72.8 22.6 %all_to_all.24 = bf16[4,192,512]{2,1,0:T(8,128)(2,1)S(1)} all-to-all(bf16[4,192,512]{2,1,0:T(8,128)(2,1)S(1)} %get-tuple-element.42), channel_id=1, replica_groups=mesh['snap'=4,'vert'=8] {'snap'}, dimensions={0} | all-to-all | bytes 1572864 | tf_op jit(solution)/shard_map/all_to_all | solution.py:87
  95.4 0.9 copy.38
  (28 shorter events, 3.1 us)
Async XLA Ops:
  0.0 56.0 %copy-start = (bf16[512,2048]{1,0:T(8,128)(2,1)S(1)}, bf16[512,2048]{1,0:T(8,128)(2,1)}, u32[]{:S(2)}) copy-start(bf16[512,2048]{1,0:T(8,128)(2,1)} %param.19) | copy-start | bytes 6291460
  0.0 11.7 %copy-start.2 = (bf16[1,12,128,128]{3,2,1,0:T(8,128)(2,1)S(1)}, bf16[1,12,128,128]{3,2,1,0:T(8,128)(2,1)}, u32[]{:S(2)}) copy-start(bf16[1,12,128,128]{3,2,1,0:T(8,128)(2,1)} %param.13) | copy-start | bytes 1179652
  0.0 8.6 %collective-permute-start = (bf16[1,768,128]{2,1,0:T(8,128)(2,1)}, bf16[1,768,128]{2,1,0:T(8,128)(2,1)S(1)}, u32[]{:S(2)}, u32[]{:S(2)}) collective-permute-start(bf16[1,768,128]{2,1,0:T(8,128)(2,1)} %param.12), channel_id=1, source_target_pairs={{0,1},{1,2},{2,3},{3,4},{4,5},{5,6},{6,7},{8,9},{9,10},{10,11},{11... | collective-permute-start | bytes 589832 | tf_op jit(solution)/shard_map/ppermute | solution.py:17
  2.1 8.0 %collective-permute-start.1 = (bf16[1,768,128]{2,1,0:T(8,128)(2,1)}, bf16[1,768,128]{2,1,0:T(8,128)(2,1)S(1)}, u32[]{:S(2)}, u32[]{:S(2)}) collective-permute-start(bf16[1,768,128]{2,1,0:T(8,128)(2,1)} %param.12), channel_id=1, source_target_pairs={{1,0},{2,1},{3,2},{4,3},{5,4},{6,5},{7,6},{9,8},{10,9},{11,10},{12... | collective-permute-start | bytes 589832 | tf_op jit(solution)/shard_map/ppermute | solution.py:19
  11.7 3.1 %copy-start.6 = (s32[1,12]{1,0:T(1,128)S(1)}, s32[1,12]{1,0:T(1,128)}, u32[]{:S(2)}) copy-start(s32[1,12]{1,0:T(1,128)} %param.15) | copy-start | bytes 148
  13.1 2.2 %copy-start.4 = (bf16[128,512]{1,0:T(8,128)(2,1)S(1)}, bf16[128,512]{1,0:T(8,128)(2,1)}, u32[]{:S(2)}) copy-start(bf16[128,512]{1,0:T(8,128)(2,1)} %param.17) | copy-start | bytes 393220
  13.1 2.2 %copy-start.5 = (f32[512]{0:T(512)S(1)}, f32[512]{0:T(512)}, u32[]{:S(2)}) copy-start(f32[512]{0:T(512)} %param.18) | copy-start | bytes 6148
  26.4 25.9 %all-to-all-start = ((bf16[4,2,49152]{2,1,0:T(2,128)(2,1)}), bf16[4,2,49152]{2,1,0:T(2,128)(2,1)S(1)}, u32[]{:S(2)}, u32[]{:S(2)}) async-start(bf16[4,2,49152]{2,1,0:T(2,128)(2,1)} %reshape.53), calls=%async_computation | async-start | bytes 1572864 | tf_op jit(solution)/shard_map/all_to_all | solution.py:73
  56.0 4.5 %copy-start.1 = (bf16[4,192,512]{2,1,0:T(8,128)(2,1)S(1)}, bf16[4,192,512]{2,1,0:T(8,128)(2,1)}, u32[]{:S(2)}) copy-start(bf16[4,192,512]{2,1,0:T(8,128)(2,1)} %custom-call.4) | copy-start | bytes 2359300
  56.0 4.5 %copy-start.3 = (f32[2048]{0:T(1024)S(1)}, f32[2048]{0:T(1024)}, u32[]{:S(2)}) copy-start(f32[2048]{0:T(1024)} %param.21) | copy-start | bytes 24580
where the time goes:
time: 96.7 us; the launch traced here: 96.3 us
  blocking collectives  22.6 us (23%)
  waiting for transfers between devices  22.5 us (23%)
  matrix products  17.2 us (18%)
  starting transfers between devices  11.5 us (12%)
  local copies, waits for them, and re-layouts  11.1 us (11%)
  other arithmetic  10.4 us (11%)
    all_to_all x1, blocking collectives, shards(): lax.all_to_all(sequence, 'snap', split_axis=0, concat_axis=1, tiled=True)  22.6 us
    all_to_all x1, waiting for transfers between devices, shards(): lax.all_to_all(conv[None], 'snap', split_axis=1, concat_axis=0, tiled=True)  21 us
    dot_general x4, matrix products, gate_step(): jnp.dot(hidden, w_state, preferred_element_type=jnp.float32)  10.5 us
    unnamed x19, local copies, waits for them, and re-layouts  6.46 us
    unnamed x3, other arithmetic  6.4 us
    all_to_all x1, starting transfers between devices, shards(): lax.all_to_all(conv[None], 'snap', split_axis=1, concat_axis=0, tiled=True)  4.88 us
    ppermute x1, starting transfers between devices, padded(): lax.ppermute(head, axis, [((i + 1) % count, i) for i in range(ends)])  4.54 us
    dot_general x1, matrix products, shards(): jnp.einsum('tvp,pg->tvg', regrouped, w_input, preferred_element_type=jnp....  4.46 us
  transfers between devices with their start and end apart: 3, of which 2 were waited for; matrix products, arithmetic and copies ran while one was open for 1% of the time, Pallas kernels for 0%

commit v1 on v0

v1 whole, which is shorter than its diff:
```python
import functools

import jax
import jax.numpy as jnp
from jax import lax
from jax.experimental import pallas as pl
from jax.experimental.pallas import tpu as pltpu
from jax.sharding import PartitionSpec as P

forget_bias = 2.0
BF16 = jnp.bfloat16
F32 = jnp.float32
VMEM = pl.BlockSpec(memory_space=pltpu.VMEM)
SMEM = pl.BlockSpec(memory_space=pltpu.SMEM)
ANY = pl.BlockSpec(memory_space=pl.ANY)


def aggregate_kernel(own, left, right, tiles, src, dst, count, whole, straight, cross, window, total):
    rows = own.shape[0]
    block = tiles.shape[1]
    slots = tiles.shape[0]
    row_blocks = rows // block
    half = rows // 2
    base = (lax.axis_index("vert") - 1) * row_blocks
    parity = lax.axis_index("snap") % 2
    window[0:rows] = left[...]
    window[rows : 2 * rows] = own[...]
    window[2 * rows : 3 * rows] = right[...]
    total[...] = jnp.zeros_like(total)
    products = []
    for slot in range(slots):
        column = jnp.clip(src[0, slot] - base, 0, 3 * row_blocks - 1)
        start = pl.multiple_of(column * block, block)
        products.append(
            jnp.dot(tiles[slot], window[pl.ds(start, block)], preferred_element_type=F32)
        )
    for slot in range(slots):
        start = pl.multiple_of(jnp.clip(dst[0, slot], 0, row_blocks - 1) * block, block)
        alive = slot < count[0, 0]
        total[pl.ds(start, block)] += jnp.where(alive, products[slot], 0.0)
    whole[...] = total[...].astype(BF16)
    near = pl.multiple_of(parity * half, half)
    far = pl.multiple_of((1 - parity) * half, half)
    straight[...] = total[pl.ds(near, half)].astype(BF16)
    cross[...] = total[pl.ds(far, half)].astype(BF16)


def aggregate(own, left, right, tiles, src, dst, count):
    rows, width = own.shape
    shape = jax.ShapeDtypeStruct
    return pl.pallas_call(
        aggregate_kernel,
        out_shape=(
            shape((rows, width), BF16),
            shape((rows // 2, width), BF16),
            shape((rows // 2, width), BF16),
        ),
        in_specs=[VMEM, VMEM, VMEM, VMEM, SMEM, SMEM, SMEM],
        out_specs=(VMEM, VMEM, VMEM),
        scratch_shapes=[pltpu.VMEM((3 * rows, width), BF16), pltpu.VMEM((rows, width), F32)],
        compiler_params=pltpu.CompilerParams(vmem_limit_bytes=8 << 20),
        name="aggregate",
    )(own, left, right, tiles, src, dst, count)


def recur_kernel(snaps, first, chunk, *refs):
    passed = 2 * (snaps // 2 - 1)
    own, pair = refs[:2]
    taken = refs[2 : 2 + passed]
    w_conv, b_conv, w_input, w_state, b_gates = refs[2 + passed : 7 + passed]
    out, rows_in, conv, hidden, cell, sem = refs[-6:]
    rows = rows_in.shape[0]
    width = w_state.shape[0]
    me = lax.axis_index("snap")
    parity = me % 2
    mine = parity if first else 1 - parity
    offset = pl.multiple_of(mine * rows, rows)
    for step in range(snaps):

        @pl.when(step <= me)
        def _(step=step):
            @pl.when(step == me)
            def _():
                rows_in[...] = own[pl.ds(offset, rows)]

            @pl.when((step == me - 1) & (parity == 1))
            def _():
                rows_in[...] = pair[pl.ds(offset, rows)]

            for ahead in range(1, snaps // 2 - step // 2):
                for turned in range(2):

                    @pl.when((me // 2 == step // 2 + ahead) & ((mine != step % 2) == (turned == 1)))
                    def _(ahead=ahead, turned=turned):
                        rows_in[...] = taken[2 * (ahead - 1) + turned][...]

            reached = jnp.dot(rows_in[...], w_conv[...], preferred_element_type=F32) + b_conv[...]
            conv[...] = jnp.maximum(reached, 0.0).astype(BF16)
            for low in range(0, width, chunk):
                gates = []
                for gate in range(4):
                    part = slice(gate * width + low, gate * width + low + chunk)
                    value = jnp.dot(conv[...], w_input[:, part], preferred_element_type=F32)
                    if step:
                        value += jnp.dot(
                            hidden[step % 2], w_state[:, part], preferred_element_type=F32
                        )
                    gates.append(value + b_gates[:, part])
                part = slice(low, low + chunk)
                fresh = (0.5 * jnp.tanh(0.5 * gates[0]) + 0.5) * jnp.tanh(gates[2])
                if step:
                    keep = 0.5 * jnp.tanh(0.5 * (gates[1] + forget_bias)) + 0.5
                    fresh += keep * cell[:, part]
                cell[:, part] = fresh
                shown = (0.5 * jnp.tanh(0.5 * gates[3]) + 0.5) * jnp.tanh(fresh)
                hidden[(step + 1) % 2, :, part] = shown.astype(BF16)

    copy = pltpu.make_async_copy(
        hidden.at[(me + 1) % 2], out.at[0, pl.ds(offset, rows)], sem
    )
    copy.start()
    copy.wait()


def recur(first, own, pair, taken, weights, before):
    rows = own.shape[0] // 2
    width = weights[3].shape[0]
    snaps = lax.axis_size("snap")
    operands = [own, pair, *taken, *weights]
    specs = [VMEM] * len(operands)
    aliases = {}
    if before is not None:
        aliases = {len(operands): 0}
        operands.append(before)
        specs.append(ANY)
    return pl.pallas_call(
        functools.partial(recur_kernel, snaps, first, width // 2),
        out_shape=jax.ShapeDtypeStruct((1, 2 * rows, width), BF16),
        in_specs=specs,
        out_specs=ANY,
        scratch_shapes=[
            pltpu.VMEM((rows, own.shape[1]), BF16),
            pltpu.VMEM((rows, weights[2].shape[0]), BF16),
            pltpu.VMEM((2, rows, width), BF16),
            pltpu.VMEM((rows, width), F32),
            pltpu.SemaphoreType.DMA,
        ],
        input_output_aliases=aliases,
        compiler_params=pltpu.CompilerParams(vmem_limit_bytes=40 << 20),
        cost_estimate=pl.CostEstimate(
            flops=14 * rows * width * width * snaps,
            transcendentals=5 * rows * width * snaps,
            bytes_accessed=8 * width * width * 2,
        ),
        name="recur_first" if first else "recur_second",
    )(*operands)


def shards(
    features,
    adjacency_tiles,
    src_block,
    dst_block,
    block_count,
    w_conv,
    b_conv,
    w_input,
    w_state,
    b_gates,
):
    own = features[0]
    owners = lax.axis_size("vert")
    snaps = lax.axis_size("snap")
    left = lax.ppermute(own, "vert", [(i, i + 1) for i in range(owners - 1)])
    right = lax.ppermute(own, "vert", [(i + 1, i) for i in range(owners - 1)])
    whole, straight, cross = aggregate(
        own, left, right, adjacency_tiles[0], src_block, dst_block, block_count
    )
    taken = []
    for ahead in range(1, snaps // 2):
        starts = [(i, b) for i in range(snaps // 2 - ahead) for b in range(2)]
        taken.append(
            lax.ppermute(straight, "snap", [(2 * i + b, 2 * (i + ahead) + b) for i, b in starts])
        )
        taken.append(
            lax.ppermute(cross, "snap", [(2 * i + b, 2 * (i + ahead) + 1 - b) for i, b in starts])
        )
    pair = lax.ppermute(whole, "snap", [(2 * i, 2 * i + 1) for i in range(snaps // 2)])
    swap = [(i, i ^ 1) for i in range(snaps)]
    swapped = [lax.ppermute(part, "snap", swap) for part in taken]
    weights = (w_conv, b_conv[None], w_input, w_state, b_gates[None])
    out = recur(True, whole, pair, taken, weights, None)
    return recur(False, whole, pair, swapped, weights, out)


def solution(mesh):
    placed = (
        P("snap", "vert", None),
        P("snap", "vert", None, None),
        P("snap", "vert"),
        P("snap", "vert"),
        P("snap", "vert"),
        P(),
        P(),
        P(),
        P(),
        P(),
    )
    return jax.shard_map(
        shards, mesh=mesh, in_specs=placed, out_specs=P("snap", "vert", None), check_vma=False
    )
```

time: 96.7 us -> 51.9 us (0.54)
  the two profiles are of different devices: /device:TPU:4 before, /device:TPU:28 now
where the time goes in v1:
time: 51.9 us; the launch traced here: 51.5 us
  Pallas kernels  17.6 us (34%)
  waiting for transfers between devices  14.6 us (28%)
  starting transfers between devices  9.81 us (19%)
  local copies, waits for them, and re-layouts  8.7 us (17%)
  between operations  0.75 us (1%)
    pallas_call x2, Pallas kernels, recur(): pl.pallas_call(functools.partial(recur_kernel, snaps, first, width // 2),...  16.7 us
    unnamed x22, local copies, waits for them, and re-layouts  8.7 us
    ppermute x1, waiting for transfers between devices, shards(): lax.ppermute(straight, 'snap', [(2 * i + b, 2 * (i + ahead) + b) for i, b...  7.61 us
    ppermute x1, waiting for transfers between devices, shards(): left = lax.ppermute(own, 'vert', [(i, i + 1) for i in range(owners - 1)])  4.48 us
    ppermute x1, starting transfers between devices, shards(): right = lax.ppermute(own, 'vert', [(i + 1, i) for i in range(owners - 1)])  2.77 us
    ppermute x1, starting transfers between devices, shards(): left = lax.ppermute(own, 'vert', [(i, i + 1) for i in range(owners - 1)])  1.92 us
    ppermute x1, waiting for transfers between devices, shards(): lax.ppermute(cross, 'snap', [(2 * i + b, 2 * (i + ahead) + 1 - b) for i,...  1.48 us
    ppermute x1, starting transfers between devices, shards(): lax.ppermute(whole, 'snap', [(2 * i, 2 * i + 1) for i in range(snaps // 2)])  1.29 us
  transfers between devices with their start and end apart: 7, of which 4 were waited for; matrix products, arithmetic and copies ran while one was open for 0% of the time, Pallas kernels for 16%

profile of v1, /device:TPU:28, one launch (start us, length us, event | category | flops | bytes accessed | tf_op | source)
XLA Modules:
  0.0 51.5 jit_solution(76683135414444874)
XLA Ops:
  0.0 2.8 %collective-permute-start.1 = (bf16[768,128]{1,0:T(8,128)(2,1)}, bf16[768,128]{1,0:T(8,128)(2,1)S(1)}, u32[]{:S(2)}, u32[]{:S(2)}) collective-permute-start(bf16[768,128]{1,0:T(8,128)(2,1)} %bitcast.5), channel_id=1, source_target_pairs={{1,0},{2,1},{3,2},{4,3},{5,4},{6,5},{7,6},{9,8},{10,9},{11,10},{12... | collective-permute-start | bytes 589832 | tf_op jit(solution)/shard_map/ppermute | solution.py:175
  2.8 1.9 %collective-permute-start = (bf16[768,128]{1,0:T(8,128)(2,1)}, bf16[768,128]{1,0:T(8,128)(2,1)S(1)}, u32[]{:S(2)}, u32[]{:S(2)}) collective-permute-start(bf16[768,128]{1,0:T(8,128)(2,1)} %bitcast.6), channel_id=1, source_target_pairs={{0,1},{1,2},{2,3},{3,4},{4,5},{5,6},{6,7},{8,9},{9,10},{10,11},{11... | collective-permute-start | bytes 589832 | tf_op jit(solution)/shard_map/ppermute | solution.py:174
  5.3 1.0 %collective-permute-done.1.right = bf16[768,128]{1,0:T(8,128)(2,1)S(1)} collective-permute-done((bf16[768,128]{1,0:T(8,128)(2,1)}, bf16[768,128]{1,0:T(8,128)(2,1)S(1)}, u32[]{:S(2)}, u32[]{:S(2)}) %collective-permute-start.1) | collective-permute-done | bytes 196640 | tf_op jit(solution)/shard_map/ppermute | solution.py:175
  6.4 4.5 %collective-permute-done.left = bf16[768,128]{1,0:T(8,128)(2,1)S(1)} collective-permute-done((bf16[768,128]{1,0:T(8,128)(2,1)}, bf16[768,128]{1,0:T(8,128)(2,1)S(1)}, u32[]{:S(2)}, u32[]{:S(2)}) %collective-permute-start) | collective-permute-done | bytes 196640 | tf_op jit(solution)/shard_map/ppermute | solution.py:174
  10.9 1.0 %copy-done = bf16[1,12,128,128]{3,2,1,0:T(8,128)(2,1)S(1)} copy-done((bf16[1,12,128,128]{3,2,1,0:T(8,128)(2,1)S(1)}, bf16[1,12,128,128]{3,2,1,0:T(8,128)(2,1)}, u32[]{:S(2)}) %copy-start) | copy-done | bytes 393240
  11.9 0.9 %copy-done.1 = bf16[1,768,128]{2,1,0:T(8,128)(2,1)S(1)} copy-done((bf16[1,768,128]{2,1,0:T(8,128)(2,1)S(1)}, bf16[1,768,128]{2,1,0:T(8,128)(2,1)}, u32[]{:S(2)}) %copy-start.1) | copy-done | bytes 196632
  12.8 0.7 %copy-done.2 = s32[1,12]{1,0:T(1,128)S(1)} copy-done((s32[1,12]{1,0:T(1,128)S(1)}, s32[1,12]{1,0:T(1,128)}, u32[]{:S(2)}) %copy-start.2) | copy-done | bytes 72
  13.5 0.7 %copy-done.3 = s32[1,12]{1,0:T(1,128)S(1)} copy-done((s32[1,12]{1,0:T(1,128)S(1)}, s32[1,12]{1,0:T(1,128)}, u32[]{:S(2)}) %copy-start.3) | copy-done | bytes 72
  14.1 0.9 %aggregate.1 = (bf16[768,128]{1,0:T(8,128)(2,1)S(1)}, bf16[384,128]{1,0:T(8,128)(2,1)S(1)}, bf16[384,128]{1,0:T(8,128)(2,1)S(1)}) custom-call(bf16[768,128]{1,0:T(8,128)(2,1)S(1)} %bitcast.7, bf16[768,128]{1,0:T(8,128)(2,1)S(1)} %collective-permute-done.left, bf16[768,128]{1,0:T(8,128)(2,1)S(1)} %collective-permute-done.1.right, ...), custom_call_target="tpu_custom_call" | custom-call | tf_op jit(solution)/shard_map/aggregate/pallas_call | solution.py:51
  15.0 1.3 %collective-permute-start.2 = (bf16[768,128]{1,0:T(8,128)(2,1)S(1)}, bf16[768,128]{1,0:T(8,128)(2,1)S(1)}, u32[]{:S(2)}, u32[]{:S(2)}) collective-permute-start(bf16[768,128]{1,0:T(8,128)(2,1)S(1)} %get-tuple-element.8.refs_0_), channel_id=1, source_target_pairs={{0,8},{16,24},{1,9},{17,25},{2,10},{18,26},{3,11},{19,27},{4,12},{... | collective-permute-start | bytes 589832 | tf_op jit(solution)/shard_map/ppermute | solution.py:188
  16.3 1.3 %collective-permute-start.3 = (bf16[384,128]{1,0:T(8,128)(2,1)S(1)}, bf16[384,128]{1,0:T(8,128)(2,1)S(1)}, u32[]{:S(2)}, u32[]{:S(2)}) collective-permute-start(bf16[384,128]{1,0:T(8,128)(2,1)S(1)} %get-tuple-element.9), channel_id=1, source_target_pairs={{0,16},{8,24},{1,17},{9,25},{2,18},{10,26},{3,19},{11,27},{4,20},{... | collective-permute-start | bytes 294920 | tf_op jit(solution)/shard_map/ppermute | solution.py:183
  17.6 1.3 %collective-permute-start.5 = (bf16[384,128]{1,0:T(8,128)(2,1)S(1)}, bf16[384,128]{1,0:T(8,128)(2,1)S(1)}, u32[]{:S(2)}, u32[]{:S(2)}) collective-permute-start(bf16[384,128]{1,0:T(8,128)(2,1)S(1)} %get-tuple-element.10), channel_id=1, source_target_pairs={{0,24},{8,16},{1,25},{9,17},{2,26},{10,18},{3,27},{11,19},{4,28},{... | collective-permute-start | bytes 294920 | tf_op jit(solution)/shard_map/ppermute | solution.py:186
  18.9 7.6 %collective-permute-done.3.refs_2_ = bf16[384,128]{1,0:T(8,128)(2,1)S(1)} collective-permute-done((bf16[384,128]{1,0:T(8,128)(2,1)S(1)}, bf16[384,128]{1,0:T(8,128)(2,1)S(1)}, u32[]{:S(2)}, u32[]{:S(2)}) %collective-permute-start.3) | collective-permute-done | bytes 98336 | tf_op jit(solution)/shard_map/ppermute | solution.py:183
  26.5 0.7 %collective-permute-start.4 = (bf16[384,128]{1,0:T(8,128)(2,1)S(1)}, bf16[384,128]{1,0:T(8,128)(2,1)S(1)}, u32[]{:S(2)}, u32[]{:S(2)}) collective-permute-start(bf16[384,128]{1,0:T(8,128)(2,1)S(1)} %collective-permute-done.3.refs_2_), channel_id=1, source_target_pairs={{0,8},{8,0},{16,24},{24,16},{1,9},{9,1},{17,25},{25,17},{2,10},{10... | collective-permute-start | bytes 294920 | tf_op jit(solution)/shard_map/ppermute | solution.py:190
  27.2 1.5 %collective-permute-done.5.refs_3_ = bf16[384,128]{1,0:T(8,128)(2,1)S(1)} collective-permute-done((bf16[384,128]{1,0:T(8,128)(2,1)S(1)}, bf16[384,128]{1,0:T(8,128)(2,1)S(1)}, u32[]{:S(2)}, u32[]{:S(2)}) %collective-permute-start.5) | collective-permute-done | bytes 98336 | tf_op jit(solution)/shard_map/ppermute | solution.py:186
  28.7 0.6 %collective-permute-start.6 = (bf16[384,128]{1,0:T(8,128)(2,1)S(1)}, bf16[384,128]{1,0:T(8,128)(2,1)S(1)}, u32[]{:S(2)}, u32[]{:S(2)}) collective-permute-start(bf16[384,128]{1,0:T(8,128)(2,1)S(1)} %collective-permute-done.5.refs_3_), channel_id=1, source_target_pairs={{0,8},{8,0},{16,24},{24,16},{1,9},{9,1},{17,25},{25,17},{2,10},{10... | collective-permute-start | bytes 294920 | tf_op jit(solution)/shard_map/ppermute | solution.py:190
  29.2 0.0 collective-permute-done.2.refs_1_
  29.2 1.6 %copy-done.4 = bf16[512,2048]{1,0:T(8,128)(2,1)S(1)} copy-done((bf16[512,2048]{1,0:T(8,128)(2,1)S(1)}, bf16[512,2048]{1,0:T(8,128)(2,1)}, u32[]{:S(2)}) %copy-start.4) | copy-done | bytes 2097176
  30.8 1.6 %copy-done.6 = bf16[512,2048]{1,0:T(8,128)(2,1)S(1)} copy-done((bf16[512,2048]{1,0:T(8,128)(2,1)S(1)}, bf16[512,2048]{1,0:T(8,128)(2,1)}, u32[]{:S(2)}) %copy-start.6) | copy-done | bytes 2097176
  32.4 0.9 %copy-done.8 = bf16[128,512]{1,0:T(8,128)(2,1)S(1)} copy-done((bf16[128,512]{1,0:T(8,128)(2,1)S(1)}, bf16[128,512]{1,0:T(8,128)(2,1)}, u32[]{:S(2)}) %copy-start.8) | copy-done | bytes 131096
  33.3 0.7 %copy-done.9 = f32[2048]{0:T(1024)S(1)} copy-done((f32[2048]{0:T(1024)S(1)}, f32[2048]{0:T(1024)}, u32[]{:S(2)}) %copy-start.9) | copy-done | bytes 8216
  34.0 0.7 %copy-done.10 = f32[512]{0:T(512)S(1)} copy-done((f32[512]{0:T(512)S(1)}, f32[512]{0:T(512)}, u32[]{:S(2)}) %copy-start.10) | copy-done | bytes 2072
  34.7 8.3 %recur_first.1.refs_9_ = bf16[1,768,512]{2,1,0:T(8,128)(2,1)} custom-call(bf16[768,128]{1,0:T(8,128)(2,1)S(1)} %get-tuple-element.8.refs_0_, bf16[768,128]{1,0:T(8,128)(2,1)S(1)} %collective-permute-done.2.refs_1_, bf16[384,128]{1,0:T(8,128)(2,1)S(1)} %collective-permute-done.3.refs_2_, bf16[384,128]{1,0:T(8,128)(2,1)S(1)} %collective-permute-done.5.refs_3_, ...), custom_call_target="tpu_custom_call" | custom-call | flops 5637144576 | bytes 4194304 | tf_op jit(solution)/shard_map/recur_first/pallas_call | solution.py:136
  43.1 8.4 %recur_second.1 = bf16[1,768,512]{2,1,0:T(8,128)(2,1)} custom-call(bf16[768,128]{1,0:T(8,128)(2,1)S(1)} %get-tuple-element.8.refs_0_, bf16[768,128]{1,0:T(8,128)(2,1)S(1)} %collective-permute-done.2.refs_1_, bf16[384,128]{1,0:T(8,128)(2,1)S(1)} %collective-permute-done.4.refs_2_, ...), custom_call_target="tpu_custom_call", output_to_operand_aliasing={{}: (9, {})} | custom-call | flops 5637144576 | bytes 4194304 | tf_op jit(solution)/shard_map/recur_second/pallas_call | solution.py:136
  (15 shorter events, 0.0 us)
Async XLA Ops:
  0.0 6.4 %collective-permute-start.1 = (bf16[768,128]{1,0:T(8,128)(2,1)}, bf16[768,128]{1,0:T(8,128)(2,1)S(1)}, u32[]{:S(2)}, u32[]{:S(2)}) collective-permute-start(bf16[768,128]{1,0:T(8,128)(2,1)} %bitcast.5), channel_id=1, source_target_pairs={{1,0},{2,1},{3,2},{4,3},{5,4},{6,5},{7,6},{9,8},{10,9},{11,10},{12... | collective-permute-start | bytes 589832 | tf_op jit(solution)/shard_map/ppermute | solution.py:175
  2.8 8.1 %collective-permute-start = (bf16[768,128]{1,0:T(8,128)(2,1)}, bf16[768,128]{1,0:T(8,128)(2,1)S(1)}, u32[]{:S(2)}, u32[]{:S(2)}) collective-permute-start(bf16[768,128]{1,0:T(8,128)(2,1)} %bitcast.6), channel_id=1, source_target_pairs={{0,1},{1,2},{2,3},{3,4},{4,5},{5,6},{6,7},{8,9},{9,10},{10,11},{11... | collective-permute-start | bytes 589832 | tf_op jit(solution)/shard_map/ppermute | solution.py:174
  10.9 1.0 %copy-start = (bf16[1,12,128,128]{3,2,1,0:T(8,128)(2,1)S(1)}, bf16[1,12,128,128]{3,2,1,0:T(8,128)(2,1)}, u32[]{:S(2)}) copy-start(bf16[1,12,128,128]{3,2,1,0:T(8,128)(2,1)} %param.11) | copy-start | bytes 1179652
  11.9 0.9 %copy-start.1 = (bf16[1,768,128]{2,1,0:T(8,128)(2,1)S(1)}, bf16[1,768,128]{2,1,0:T(8,128)(2,1)}, u32[]{:S(2)}) copy-start(bf16[1,768,128]{2,1,0:T(8,128)(2,1)} %param.10) | copy-start | bytes 589828
  12.8 0.7 %copy-start.2 = (s32[1,12]{1,0:T(1,128)S(1)}, s32[1,12]{1,0:T(1,128)}, u32[]{:S(2)}) copy-start(s32[1,12]{1,0:T(1,128)} %src.1) | copy-start | bytes 148
  13.5 0.7 %copy-start.3 = (s32[1,12]{1,0:T(1,128)S(1)}, s32[1,12]{1,0:T(1,128)}, u32[]{:S(2)}) copy-start(s32[1,12]{1,0:T(1,128)} %dst.1) | copy-start | bytes 148
  15.0 14.2 %collective-permute-start.2 = (bf16[768,128]{1,0:T(8,128)(2,1)S(1)}, bf16[768,128]{1,0:T(8,128)(2,1)S(1)}, u32[]{:S(2)}, u32[]{:S(2)}) collective-permute-start(bf16[768,128]{1,0:T(8,128)(2,1)S(1)} %get-tuple-element.8.refs_0_), channel_id=1, source_target_pairs={{0,8},{16,24},{1,9},{17,25},{2,10},{18,26},{3,11},{19,27},{4,12},{... | collective-permute-start | bytes 589832 | tf_op jit(solution)/shard_map/ppermute | solution.py:188
  16.3 10.2 %collective-permute-start.3 = (bf16[384,128]{1,0:T(8,128)(2,1)S(1)}, bf16[384,128]{1,0:T(8,128)(2,1)S(1)}, u32[]{:S(2)}, u32[]{:S(2)}) collective-permute-start(bf16[384,128]{1,0:T(8,128)(2,1)S(1)} %get-tuple-element.9), channel_id=1, source_target_pairs={{0,16},{8,24},{1,17},{9,25},{2,18},{10,26},{3,19},{11,27},{4,20},{... | collective-permute-start | bytes 294920 | tf_op jit(solution)/shard_map/ppermute | solution.py:183
  17.6 11.1 %collective-permute-start.5 = (bf16[384,128]{1,0:T(8,128)(2,1)S(1)}, bf16[384,128]{1,0:T(8,128)(2,1)S(1)}, u32[]{:S(2)}, u32[]{:S(2)}) collective-permute-start(bf16[384,128]{1,0:T(8,128)(2,1)S(1)} %get-tuple-element.10), channel_id=1, source_target_pairs={{0,24},{8,16},{1,25},{9,17},{2,26},{10,18},{3,27},{11,19},{4,28},{... | collective-permute-start | bytes 294920 | tf_op jit(solution)/shard_map/ppermute | solution.py:186
  26.5 16.5 %collective-permute-start.4 = (bf16[384,128]{1,0:T(8,128)(2,1)S(1)}, bf16[384,128]{1,0:T(8,128)(2,1)S(1)}, u32[]{:S(2)}, u32[]{:S(2)}) collective-permute-start(bf16[384,128]{1,0:T(8,128)(2,1)S(1)} %collective-permute-done.3.refs_2_), channel_id=1, source_target_pairs={{0,8},{8,0},{16,24},{24,16},{1,9},{9,1},{17,25},{25,17},{2,10},{10... | collective-permute-start | bytes 294920 | tf_op jit(solution)/shard_map/ppermute | solution.py:190
  28.7 14.4 %collective-permute-start.6 = (bf16[384,128]{1,0:T(8,128)(2,1)S(1)}, bf16[384,128]{1,0:T(8,128)(2,1)S(1)}, u32[]{:S(2)}, u32[]{:S(2)}) collective-permute-start(bf16[384,128]{1,0:T(8,128)(2,1)S(1)} %collective-permute-done.5.refs_3_), channel_id=1, source_target_pairs={{0,8},{8,0},{16,24},{24,16},{1,9},{9,1},{17,25},{25,17},{2,10},{10... | collective-permute-start | bytes 294920 | tf_op jit(solution)/shard_map/ppermute | solution.py:190
  29.2 1.6 %copy-start.4 = (bf16[512,2048]{1,0:T(8,128)(2,1)S(1)}, bf16[512,2048]{1,0:T(8,128)(2,1)}, u32[]{:S(2)}) copy-start(bf16[512,2048]{1,0:T(8,128)(2,1)} %refs_6_.3) | copy-start | bytes 6291460
  30.8 1.6 %copy-start.6 = (bf16[512,2048]{1,0:T(8,128)(2,1)S(1)}, bf16[512,2048]{1,0:T(8,128)(2,1)}, u32[]{:S(2)}) copy-start(bf16[512,2048]{1,0:T(8,128)(2,1)} %refs_7_.3) | copy-start | bytes 6291460
  32.4 0.9 %copy-start.8 = (bf16[128,512]{1,0:T(8,128)(2,1)S(1)}, bf16[128,512]{1,0:T(8,128)(2,1)}, u32[]{:S(2)}) copy-start(bf16[128,512]{1,0:T(8,128)(2,1)} %refs_4_.3) | copy-start | bytes 393220
  33.3 0.7 %copy-start.9 = (f32[2048]{0:T(1024)S(1)}, f32[2048]{0:T(1024)}, u32[]{:S(2)}) copy-start(f32[2048]{0:T(1024)} %param.19) | copy-start | bytes 24580
  34.0 0.7 %copy-start.10 = (f32[512]{0:T(512)S(1)}, f32[512]{0:T(512)}, u32[]{:S(2)}) copy-start(f32[512]{0:T(512)} %param.16) | copy-start | bytes 6148
  34.7 8.3 %copy-start.5 = (bf16[512,2048]{1,0:T(8,128)(2,1)S(1)}, bf16[512,2048]{1,0:T(8,128)(2,1)}, u32[]{:S(2)}) copy-start(bf16[512,2048]{1,0:T(8,128)(2,1)} %refs_6_.3) | copy-start | bytes 6291460
  34.7 8.4 %copy-start.7 = (bf16[512,2048]{1,0:T(8,128)(2,1)S(1)}, bf16[512,2048]{1,0:T(8,128)(2,1)}, u32[]{:S(2)}) copy-start(bf16[512,2048]{1,0:T(8,128)(2,1)} %refs_7_.3) | copy-start | bytes 6291460

commit v2 on v0

v2 whole, which is shorter than its diff:
```python
import functools

import jax
import jax.numpy as jnp
from jax import lax
from jax.experimental import pallas as pl
from jax.experimental.pallas import tpu as pltpu
from jax.sharding import PartitionSpec as P

forget_bias = 2.0
BF16 = jnp.bfloat16
F32 = jnp.float32
VMEM = pl.BlockSpec(memory_space=pltpu.VMEM)
SMEM = pl.BlockSpec(memory_space=pltpu.SMEM)
HBM = pl.BlockSpec(memory_space=pltpu.HBM)
GRANT = 24 << 20


def load_kernel(total, *refs):
    sems = refs[-1]
    copies = []
    for place in range(total):
        copies.append(
            pltpu.make_async_copy(refs[place], refs[total + place], sems.at[place])
        )
    for copy in copies:
        copy.start()
    for copy in copies:
        copy.wait()


def load(arrays):
    bytes_moved = sum(array.size * array.dtype.itemsize for array in arrays)
    return pl.pallas_call(
        functools.partial(load_kernel, len(arrays)),
        out_shape=[jax.ShapeDtypeStruct(array.shape, array.dtype) for array in arrays],
        in_specs=[HBM] * len(arrays),
        out_specs=[VMEM] * len(arrays),
        scratch_shapes=[pltpu.SemaphoreType.DMA((len(arrays),))],
        compiler_params=pltpu.CompilerParams(vmem_limit_bytes=GRANT),
        cost_estimate=pl.CostEstimate(
            flops=0, transcendentals=0, bytes_accessed=2 * bytes_moved
        ),
        name="load",
    )(*(pltpu.with_memory_space_constraint(array, pltpu.HBM) for array in arrays))


def aggregate_kernel(
    own, left, right, tiles, src_in, dst_in, count, whole, window, total, src, dst, sems
):
    lists = ((src_in, src), (dst_in, dst))
    copies = [pltpu.make_async_copy(a, b, sems.at[i]) for i, (a, b) in enumerate(lists)]
    for copy in copies:
        copy.start()
    rows = own.shape[0]
    block = tiles.shape[1]
    slots = tiles.shape[0]
    row_blocks = rows // block
    base = (lax.axis_index("vert") - 1) * row_blocks
    window[0:rows] = left[...]
    window[rows : 2 * rows] = own[...]
    window[2 * rows : 3 * rows] = right[...]
    total[...] = jnp.zeros_like(total)
    for copy in copies:
        copy.wait()
    products = []
    for slot in range(slots):
        column = jnp.clip(src[0, slot] - base, 0, 3 * row_blocks - 1)
        start = pl.multiple_of(column * block, block)
        products.append(
            jnp.dot(tiles[slot], window[pl.ds(start, block)], preferred_element_type=F32)
        )
    for slot in range(slots):
        start = pl.multiple_of(jnp.clip(dst[0, slot], 0, row_blocks - 1) * block, block)
        alive = slot < count[0, 0]
        total[pl.ds(start, block)] += jnp.where(alive, products[slot], 0.0)
    whole[...] = total[...].astype(BF16)


def aggregate(own, left, right, tiles, src, dst, count):
    rows, width = own.shape
    return pl.pallas_call(
        aggregate_kernel,
        out_shape=jax.ShapeDtypeStruct((rows, width), BF16),
        in_specs=[VMEM] * 4 + [HBM] * 2 + [SMEM],
        out_specs=VMEM,
        scratch_shapes=[
            pltpu.VMEM((3 * rows, width), BF16),
            pltpu.VMEM((rows, width), F32),
            *(pltpu.SMEM(array.shape, jnp.int32) for array in (src, dst)),
            pltpu.SemaphoreType.DMA((2,)),
        ],
        compiler_params=pltpu.CompilerParams(vmem_limit_bytes=GRANT),
        name="aggregate",
    )(own, left, right, tiles, src, dst, count)


def convolve(rows_in, w_conv, b_conv, conv):
    reached = jnp.dot(rows_in[...], w_conv[...], preferred_element_type=F32) + b_conv[...]
    conv[...] = jnp.maximum(reached, 0.0).astype(BF16)


def pregate_kernel(rows_in, w_conv, b_conv, w_input, pre, conv):
    convolve(rows_in, w_conv, b_conv, conv)
    width = w_input.shape[1] // 4
    for gate in range(4):
        part = slice(gate * width, (gate + 1) * width)
        pre[:, part] = jnp.dot(conv[...], w_input[:, part], preferred_element_type=F32)


def pregate(rows_in, w_conv, b_conv, w_input):
    rows = rows_in.shape[0]
    depth, gates = w_input.shape
    return pl.pallas_call(
        pregate_kernel,
        out_shape=jax.ShapeDtypeStruct((rows, gates), F32),
        in_specs=[VMEM] * 4,
        out_specs=VMEM,
        scratch_shapes=[pltpu.VMEM((rows, depth), BF16)],
        compiler_params=pltpu.CompilerParams(vmem_limit_bytes=GRANT),
        cost_estimate=pl.CostEstimate(
            flops=2 * rows * depth * gates, transcendentals=0, bytes_accessed=rows * gates * 4
        ),
        name="pregate",
    )(rows_in, w_conv, b_conv, w_input)


def gate_step(conv, pre, w_input, w_state, b_gates, hidden, cell, fresh_hidden, done, first):
    width = w_state.shape[0]
    chunk = width // 2
    for low in range(0, width, chunk):
        gates = []
        for gate in range(4):
            part = slice(gate * width + low, gate * width + low + chunk)
            if pre is None:
                value = jnp.dot(conv[...], w_input[:, part], preferred_element_type=F32)
            else:
                value = pre[:, part]
            if not first:
                value += jnp.dot(hidden[...], w_state[:, part], preferred_element_type=F32)
            bias = b_gates[:, part]
            if gate == 1:
                bias = bias + forget_bias
            gates.append(value + bias)
        part = slice(low, low + chunk)
        fresh = (0.5 * jnp.tanh(0.5 * gates[0]) + 0.5) * jnp.tanh(gates[2])
        if not first:
            fresh += (0.5 * jnp.tanh(0.5 * gates[1]) + 0.5) * cell[:, part]
        cell[:, part] = fresh
        shown = (0.5 * jnp.tanh(0.5 * gates[3]) + 0.5) * jnp.tanh(fresh)
        fresh_hidden[:, part] = shown.astype(BF16)
        if done is not None:
            done(part)


def step_kernel(on_first, on_later, on_own, carried, *refs):
    own_refs = 2 if on_own is not None else 1
    rows_in, w_conv, b_conv, w_input, w_state, b_gates = refs[:6]
    conv, spare = refs[-3:-1] if on_own is not None else refs[-2:]
    me = lax.axis_index("snap")
    start = 6 + (1 if on_own is not None else 0) + (2 if carried else 0)
    if on_own is not None:
        pre = refs[6]
        out = refs[start]
        hidden, cell = refs[start + 1 : start + 3]
        sems = refs[-1]
    else:
        hidden, cell = refs[start : start + 2]

    def taken(first):
        convolve(rows_in, w_conv, b_conv, conv)
        target = hidden if first else spare
        gate_step(conv, None, w_input, w_state, b_gates, hidden, cell, target, None, first)
        if not first:
            hidden[...] = spare[...]

    for device in on_first:

        @pl.when(me == device)
        def _():
            taken(True)

    if on_later is not None:

        @pl.when(me >= on_later)
        def _():
            taken(False)

    if on_own is None:
        return
    width = w_state.shape[0]

    def sent(part):
        return pltpu.make_async_copy(
            spare.at[:, part], out.at[0, :, part], sems.at[part.start * 2 // width]
        )

    def last(first):
        gate_step(
            conv,
            pre,
            w_input,
            w_state,
            b_gates,
            hidden,
            cell,
            spare,
            lambda part: sent(part).start(),
            first,
        )

    @pl.when(me == 0)
    def _():
        last(True)

    @pl.when(me > 0)
    def _():
        last(False)

    for low in range(0, width, width // 2):
        sent(slice(low, low + width // 2)).wait()


def step(on_first, on_later, on_own, rows_in, weights, pre, state, name):
    rows = rows_in.shape[0]
    depth, gates = weights[2].shape
    width = gates // 4
    shape = jax.ShapeDtypeStruct
    operands = [rows_in, *weights]
    if on_own is not None:
        operands.append(pre)
    outs = [shape((rows, width), BF16), shape((rows, width), F32)]
    out_specs = [VMEM, VMEM]
    scratch = [pltpu.VMEM((rows, depth), BF16), pltpu.VMEM((rows, width), BF16)]
    aliases = {}
    if on_own is not None:
        outs = [shape((1, rows, width), BF16)] + outs
        out_specs = [HBM] + out_specs
        scratch.append(pltpu.SemaphoreType.DMA((2,)))
    if state is not None:
        skip = len(outs) - 2
        aliases = {len(operands): skip, len(operands) + 1: skip + 1}
        operands += state
    return pl.pallas_call(
        functools.partial(step_kernel, on_first, on_later, on_own, state is not None),
        out_shape=outs,
        in_specs=[VMEM] * len(operands),
        out_specs=out_specs,
        scratch_shapes=scratch,
        input_output_aliases=aliases,
        compiler_params=pltpu.CompilerParams(vmem_limit_bytes=GRANT),
        cost_estimate=pl.CostEstimate(
            flops=2 * rows * (depth + width) * gates,
            transcendentals=5 * rows * width,
            bytes_accessed=rows * width * 8,
        ),
        name=name,
    )(*operands)


def shards(
    features,
    adjacency_tiles,
    src_block,
    dst_block,
    block_count,
    w_conv,
    b_conv,
    w_input,
    w_state,
    b_gates,
):
    owners = lax.axis_size("vert")
    snaps = lax.axis_size("snap")
    last = snaps - 1
    left = lax.ppermute(features[0], "vert", [(i, i + 1) for i in range(owners - 1)])
    right = lax.ppermute(features[0], "vert", [(i + 1, i) for i in range(owners - 1)])
    own, tiles, w_conv, b_conv, w_input, w_state, b_gates = load(
        [features[0], adjacency_tiles[0], w_conv, b_conv[None], w_input, w_state, b_gates[None]]
    )
    lists = [
        pltpu.with_memory_space_constraint(array, pltpu.HBM)
        for array in (src_block, dst_block)
    ]
    whole = aggregate(own, left, right, tiles, *lists, block_count)
    weights = [w_conv, b_conv, w_input, w_state, b_gates]

    handed = snaps >= 3
    arrived = {}
    for hop in range(last, 0, -1):
        routes = [(i, i + hop) for i in range(snaps - hop)]
        if handed and hop == last - 1:
            routes = routes[1:]
        arrived[hop] = lax.ppermute(whole, "snap", routes)
    if handed:
        passed_back = lax.ppermute(arrived[last], "snap", [(last, last - 1)])
    pre = pregate(whole, w_conv, b_conv, w_input)

    state = None
    for stage in range(1, last):
        hop = snaps - stage
        on_first = [] if stage == 2 else [hop]
        on_later = None if stage == 1 else hop + 1
        state = step(on_first, on_later, None, arrived[hop], weights, None, state, "step")
        if stage == min(2, last - 1):
            state = step([last - 1], None, None, passed_back, weights, None, state, "step_back")
    on_first = [1] if snaps == 2 or snaps > 3 else []
    on_later = 2 if handed else None
    rows_in = arrived[1] if snaps > 1 else whole
    return step(on_first, on_later, True, rows_in, weights, pre, state, "step_last")[0]


def solution(mesh):
    placed = (
        P("snap", "vert", None),
        P("snap", "vert", None, None),
        P("snap", "vert"),
        P("snap", "vert"),
        P("snap", "vert"),
        P(),
        P(),
        P(),
        P(),
        P(),
    )
    return jax.shard_map(
        shards, mesh=mesh, in_specs=placed, out_specs=P("snap", "vert", None), check_vma=False
    )
```

time: 96.7 us -> 39.2 us (0.41)
  the two profiles are of different devices: /device:TPU:4 before, /device:TPU:20 now
where the time goes in v2:
time: 39.2 us; the launch traced here: 38.9 us
  Pallas kernels  14.8 us (38%)
  starting transfers between devices  12 us (31%)
  waiting for transfers between devices  11.1 us (28%)
  between operations  0.93 us (2%)
    pallas_call x4, Pallas kernels, step(): pl.pallas_call(functools.partial(step_kernel, on_first, on_later, on_own,...  9.27 us
    ppermute x1, waiting for transfers between devices, shards(): passed_back = lax.ppermute(arrived[last], 'snap', [(last, last - 1)])  8.2 us
    ppermute x3, starting transfers between devices, shards(): arrived[hop] = lax.ppermute(whole, 'snap', routes)  6.06 us
    ppermute x1, waiting for transfers between devices, shards(): lax.ppermute(features[0], 'vert', [(i, i + 1) for i in range(owners - 1)])  2.93 us
    ppermute x1, starting transfers between devices, shards(): lax.ppermute(features[0], 'vert', [(i + 1, i) for i in range(owners - 1)])  2.77 us
    pallas_call x1, Pallas kernels, load(): pl.pallas_call(functools.partial(load_kernel, len(arrays)), out_shape=[ja...  2.58 us
    pallas_call x1, Pallas kernels, pregate(): pl.pallas_call(pregate_kernel, out_shape=jax.ShapeDtypeStruct((rows, gate...  1.98 us
    ppermute x1, starting transfers between devices, shards(): lax.ppermute(features[0], 'vert', [(i, i + 1) for i in range(owners - 1)])  1.92 us
  transfers between devices with their start and end apart: 6, of which 2 were waited for; matrix products, arithmetic and copies ran while one was open for 0% of the time, Pallas kernels for 16%

profile of v2, /device:TPU:20, one launch (start us, length us, event | category | flops | bytes accessed | tf_op | source)
XLA Modules:
  0.0 38.9 jit_solution(7950177275862261934)
XLA Ops:
  0.0 2.8 %collective-permute-start.1 = (bf16[768,128]{1,0:T(8,128)(2,1)}, bf16[768,128]{1,0:T(8,128)(2,1)S(1)}, u32[]{:S(2)}, u32[]{:S(2)}) collective-permute-start(bf16[768,128]{1,0:T(8,128)(2,1)} %bitcast.5), channel_id=1, source_target_pairs={{1,0},{2,1},{3,2},{4,3},{5,4},{6,5},{7,6},{9,8},{10,9},{11,10},{12... | collective-permute-start | bytes 589832 | tf_op jit(solution)/shard_map/ppermute | solution.py:277
  2.8 1.9 %collective-permute-start = (bf16[768,128]{1,0:T(8,128)(2,1)}, bf16[768,128]{1,0:T(8,128)(2,1)S(1)}, u32[]{:S(2)}, u32[]{:S(2)}) collective-permute-start(bf16[768,128]{1,0:T(8,128)(2,1)} %bitcast.6), channel_id=1, source_target_pairs={{0,1},{1,2},{2,3},{3,4},{4,5},{5,6},{6,7},{8,9},{9,10},{10,11},{11... | collective-permute-start | bytes 589832 | tf_op jit(solution)/shard_map/ppermute | solution.py:276
  5.4 2.6 %load.1 = (bf16[768,128]{1,0:T(8,128)(2,1)S(1)}, bf16[12,128,128]{2,1,0:T(8,128)(2,1)S(1)}, bf16[128,512]{1,0:T(8,128)(2,1)S(1)}, f32[1,512]{1,0:T(1,128)S(1)}, ...) custom-call(bf16[768,128]{1,0:T(8,128)(2,1)} %bitcast.7, ...), custom_call_target="tpu_custom_call" | custom-call | bytes 9850880 | tf_op jit(solution)/shard_map/load/pallas_call | solution.py:34
  7.9 0.0 collective-permute-done.1.right
  7.9 2.9 %collective-permute-done.left = bf16[768,128]{1,0:T(8,128)(2,1)S(1)} collective-permute-done((bf16[768,128]{1,0:T(8,128)(2,1)}, bf16[768,128]{1,0:T(8,128)(2,1)S(1)}, u32[]{:S(2)}, u32[]{:S(2)}) %collective-permute-start) | collective-permute-done | bytes 196640 | tf_op jit(solution)/shard_map/ppermute | solution.py:276
  10.9 1.0 %aggregate.1.rows_in = bf16[768,128]{1,0:T(8,128)(2,1)S(1)} custom-call(bf16[768,128]{1,0:T(8,128)(2,1)S(1)} %get-tuple-element.19.own, bf16[768,128]{1,0:T(8,128)(2,1)S(1)} %collective-permute-done.left, bf16[768,128]{1,0:T(8,128)(2,1)S(1)} %collective-permute-done.1.right, bf16[12,128,128]{2,1,0:T(8,128)(2,1)S(1)} %get-tuple-element.20.tiles, ...), custom_call_target="tpu_custom_call" | custom-call | tf_op jit(solution)/shard_map/aggregate/pallas_call | solution.py:82
  11.9 0.7 %collective-permute-start.3 = (bf16[768,128]{1,0:T(8,128)(2,1)S(1)}, bf16[768,128]{1,0:T(8,128)(2,1)S(1)}, u32[]{:S(2)}, u32[]{:S(2)}) collective-permute-start(bf16[768,128]{1,0:T(8,128)(2,1)S(1)} %aggregate.1.rows_in), channel_id=1, source_target_pairs={{0,24},{1,25},{2,26},{3,27},{4,28},{5,29},{6,30},{7,31}} | collective-permute-start | bytes 589832 | tf_op jit(solution)/shard_map/ppermute | solution.py:294
  12.6 0.7 %collective-permute-start.5 = (bf16[768,128]{1,0:T(8,128)(2,1)S(1)}, bf16[768,128]{1,0:T(8,128)(2,1)S(1)}, u32[]{:S(2)}, u32[]{:S(2)}) collective-permute-start(bf16[768,128]{1,0:T(8,128)(2,1)S(1)} %aggregate.1.rows_in), channel_id=1, source_target_pairs={{8,24},{9,25},{10,26},{11,27},{12,28},{13,29},{14,30},{15,31}} | collective-permute-start | bytes 589832 | tf_op jit(solution)/shard_map/ppermute | solution.py:294
  13.2 4.7 %collective-permute-start.2 = (bf16[768,128]{1,0:T(8,128)(2,1)S(1)}, bf16[768,128]{1,0:T(8,128)(2,1)S(1)}, u32[]{:S(2)}, u32[]{:S(2)}) collective-permute-start(bf16[768,128]{1,0:T(8,128)(2,1)S(1)} %aggregate.1.rows_in), channel_id=1, source_target_pairs={{0,8},{8,16},{16,24},{1,9},{9,17},{17,25},{2,10},{10,18},{18,26},{... | collective-permute-start | bytes 589832 | tf_op jit(solution)/shard_map/ppermute | solution.py:294
  18.0 2.0 %pregate.1.refs_6_ = f32[768,2048]{1,0:T(8,128)S(1)} custom-call(bf16[768,128]{1,0:T(8,128)(2,1)S(1)} %aggregate.1.rows_in, bf16[128,512]{1,0:T(8,128)(2,1)S(1)} %get-tuple-element.21.w_conv.refs_1_, f32[1,512]{1,0:T(1,128)S(1)} %get-tuple-element.22.b_conv.refs_2_, bf16[512,2048]{1,0:T(8,128)(2,1)S(1)} %get-tuple-element.23.w_input.refs_3_), custom_call_target="tpu_custom_call" | custom-call | flops 1610612736 | bytes 6291456 | tf_op jit(solution)/shard_map/pregate/pallas_call | solution.py:114
  19.9 0.0 collective-permute-done.3.refs_0_
  20.0 1.3 %collective-permute-start.4 = (bf16[768,128]{1,0:T(8,128)(2,1)S(1)}, bf16[768,128]{1,0:T(8,128)(2,1)S(1)}, u32[]{:S(2)}, u32[]{:S(2)}) collective-permute-start(bf16[768,128]{1,0:T(8,128)(2,1)S(1)} %collective-permute-done.3.refs_0_), channel_id=1, source_target_pairs={{24,16},{25,17},{26,18},{27,19},{28,20},{29,21},{30,22},{31,23}} | collective-permute-start | bytes 589832 | tf_op jit(solution)/shard_map/ppermute | solution.py:296
  21.3 0.0 collective-permute-done.5.refs_0_
  21.3 8.2 %collective-permute-done.4.refs_0_ = bf16[768,128]{1,0:T(8,128)(2,1)S(1)} collective-permute-done((bf16[768,128]{1,0:T(8,128)(2,1)S(1)}, bf16[768,128]{1,0:T(8,128)(2,1)S(1)}, u32[]{:S(2)}, u32[]{:S(2)}) %collective-permute-start.4) | collective-permute-done | bytes 196640 | tf_op jit(solution)/shard_map/ppermute | solution.py:296
  29.5 1.8 %step_back.1 = (bf16[768,512]{1,0:T(8,128)(2,1)S(1)}, f32[768,512]{1,0:T(8,128)S(1)}) custom-call(bf16[768,128]{1,0:T(8,128)(2,1)S(1)} %collective-permute-done.4.refs_0_, bf16[128,512]{1,0:T(8,128)(2,1)S(1)} %get-tuple-element.21.w_conv.refs_1_, f32[1,512]{1,0:T(1,128)S(1)} %get-tuple-element.22.b_conv.refs_2_, ...), custom_call_target="tpu_custom_call", output_to_operand_aliasing={{0}: (6, {}), {1}: (7, {})} | custom-call | flops 3221225472 | bytes 3145728 | tf_op jit(solution)/shard_map/step_back/pallas_call | solution.py:244
  31.3 0.0 collective-permute-done.2.refs_0_
  31.3 7.5 %step_last.1 = (bf16[1,768,512]{2,1,0:T(8,128)(2,1)}, bf16[768,512]{1,0:T(8,128)(2,1)S(1)}, f32[768,512]{1,0:T(8,128)S(1)}) custom-call(bf16[768,128]{1,0:T(8,128)(2,1)S(1)} %collective-permute-done.2.refs_0_, bf16[128,512]{1,0:T(8,128)(2,1)S(1)} %get-tuple-element.21.w_conv.refs_1_, ...), custom_call_target="tpu_custom_call", output_to_operand_aliasing={{1}: (7, {}), {2}: (8, {})} | custom-call | flops 3221225472 | bytes 3145728 | tf_op jit(solution)/shard_map/step_last/pallas_call | solution.py:244
  (2 shorter events, 0.0 us)
Async XLA Ops:
  0.0 7.9 %collective-permute-start.1 = (bf16[768,128]{1,0:T(8,128)(2,1)}, bf16[768,128]{1,0:T(8,128)(2,1)S(1)}, u32[]{:S(2)}, u32[]{:S(2)}) collective-permute-start(bf16[768,128]{1,0:T(8,128)(2,1)} %bitcast.5), channel_id=1, source_target_pairs={{1,0},{2,1},{3,2},{4,3},{5,4},{6,5},{7,6},{9,8},{10,9},{11,10},{12... | collective-permute-start | bytes 589832 | tf_op jit(solution)/shard_map/ppermute | solution.py:277
  2.8 8.1 %collective-permute-start = (bf16[768,128]{1,0:T(8,128)(2,1)}, bf16[768,128]{1,0:T(8,128)(2,1)S(1)}, u32[]{:S(2)}, u32[]{:S(2)}) collective-permute-start(bf16[768,128]{1,0:T(8,128)(2,1)} %bitcast.6), channel_id=1, source_target_pairs={{0,1},{1,2},{2,3},{3,4},{4,5},{5,6},{6,7},{8,9},{9,10},{10,11},{11... | collective-permute-start | bytes 589832 | tf_op jit(solution)/shard_map/ppermute | solution.py:276
  11.9 8.1 %collective-permute-start.3 = (bf16[768,128]{1,0:T(8,128)(2,1)S(1)}, bf16[768,128]{1,0:T(8,128)(2,1)S(1)}, u32[]{:S(2)}, u32[]{:S(2)}) collective-permute-start(bf16[768,128]{1,0:T(8,128)(2,1)S(1)} %aggregate.1.rows_in), channel_id=1, source_target_pairs={{0,24},{1,25},{2,26},{3,27},{4,28},{5,29},{6,30},{7,31}} | collective-permute-start | bytes 589832 | tf_op jit(solution)/shard_map/ppermute | solution.py:294
  12.6 8.7 %collective-permute-start.5 = (bf16[768,128]{1,0:T(8,128)(2,1)S(1)}, bf16[768,128]{1,0:T(8,128)(2,1)S(1)}, u32[]{:S(2)}, u32[]{:S(2)}) collective-permute-start(bf16[768,128]{1,0:T(8,128)(2,1)S(1)} %aggregate.1.rows_in), channel_id=1, source_target_pairs={{8,24},{9,25},{10,26},{11,27},{12,28},{13,29},{14,30},{15,31}} | collective-permute-start | bytes 589832 | tf_op jit(solution)/shard_map/ppermute | solution.py:294
  13.2 18.0 %collective-permute-start.2 = (bf16[768,128]{1,0:T(8,128)(2,1)S(1)}, bf16[768,128]{1,0:T(8,128)(2,1)S(1)}, u32[]{:S(2)}, u32[]{:S(2)}) collective-permute-start(bf16[768,128]{1,0:T(8,128)(2,1)S(1)} %aggregate.1.rows_in), channel_id=1, source_target_pairs={{0,8},{8,16},{16,24},{1,9},{9,17},{17,25},{2,10},{10,18},{18,26},{... | collective-permute-start | bytes 589832 | tf_op jit(solution)/shard_map/ppermute | solution.py:294
  20.0 9.6 %collective-permute-start.4 = (bf16[768,128]{1,0:T(8,128)(2,1)S(1)}, bf16[768,128]{1,0:T(8,128)(2,1)S(1)}, u32[]{:S(2)}, u32[]{:S(2)}) collective-permute-start(bf16[768,128]{1,0:T(8,128)(2,1)S(1)} %collective-permute-done.3.refs_0_), channel_id=1, source_target_pairs={{24,16},{25,17},{26,18},{27,19},{28,20},{29,21},{30,22},{31,23}} | collective-permute-start | bytes 589832 | tf_op jit(solution)/shard_map/ppermute | solution.py:296

commit v3 on v2

--- a/solution.py
+++ b/solution.py
@@ -6,6 +6,7 @@
 from jax.experimental import pallas as pl
 from jax.experimental.pallas import tpu as pltpu
 from jax.sharding import PartitionSpec as P
+
 
 forget_bias = 2.0
 BF16 = jnp.bfloat16
@@ -14,6 +15,7 @@
 SMEM = pl.BlockSpec(memory_space=pltpu.SMEM)
 HBM = pl.BlockSpec(memory_space=pltpu.HBM)
 GRANT = 24 << 20
+PARTS = 2
 
 
 def load_kernel(total, *refs):
@@ -46,8 +48,10 @@
 
 
 def aggregate_kernel(
-    own, left, right, tiles, src_in, dst_in, count, whole, window, total, src, dst, sems
+    parts, own, left, right, tiles, src_in, dst_in, count, *refs
 ):
+    pieces = refs[:parts]
+    window, total, src, dst, sems = refs[parts:]
     lists = ((src_in, src), (dst_in, dst))
     copies = [pltpu.make_async_copy(a, b, sems.at[i]) for i, (a, b) in enumerate(lists)]
     for copy in copies:
@@ -74,16 +78,18 @@
         start = pl.multiple_of(jnp.clip(dst[0, slot], 0, row_blocks - 1) * block, block)
         alive = slot < count[0, 0]
         total[pl.ds(start, block)] += jnp.where(alive, products[slot], 0.0)
-    whole[...] = total[...].astype(BF16)
-
-
-def aggregate(own, left, right, tiles, src, dst, count):
+    share = rows // parts
+    for part, piece in enumerate(pieces):
+        piece[...] = total[part * share : (part + 1) * share].astype(BF16)
+
+
+def aggregate(parts, own, left, right, tiles, src, dst, count):
     rows, width = own.shape
     return pl.pallas_call(
-        aggregate_kernel,
-        out_shape=jax.ShapeDtypeStruct((rows, width), BF16),
+        functools.partial(aggregate_kernel, parts),
+        out_shape=[jax.ShapeDtypeStruct((rows // parts, width), BF16)] * parts,
         in_specs=[VMEM] * 4 + [HBM] * 2 + [SMEM],
-        out_specs=VMEM,
+        out_specs=[VMEM] * parts,
         scratch_shapes=[
             pltpu.VMEM((3 * rows, width), BF16),
             pltpu.VMEM((rows, width), F32),
@@ -100,7 +106,8 @@
     conv[...] = jnp.maximum(reached, 0.0).astype(BF16)
 
 
-def pregate_kernel(rows_in, w_conv, b_conv, w_input, pre, conv):
+def pregate_kernel(rows_in, w_conv, b_conv, w_input, *refs):
+    pre, _, conv = refs[-3:]
     convolve(rows_in, w_conv, b_conv, conv)
     width = w_input.shape[1] // 4
     for gate in range(4):
@@ -108,21 +115,27 @@
         pre[:, part] = jnp.dot(conv[...], w_input[:, part], preferred_element_type=F32)
 
 
-def pregate(rows_in, w_conv, b_conv, w_input):
+def pregate(rows_in, w_conv, b_conv, w_input, out):
     rows = rows_in.shape[0]
     depth, gates = w_input.shape
+    operands = [rows_in, w_conv, b_conv, w_input]
+    fresh = isinstance(out, tuple)
     return pl.pallas_call(
         pregate_kernel,
-        out_shape=jax.ShapeDtypeStruct((rows, gates), F32),
-        in_specs=[VMEM] * 4,
-        out_specs=VMEM,
+        out_shape=[
+            jax.ShapeDtypeStruct((rows, gates), F32),
+            jax.ShapeDtypeStruct(out if fresh else out.shape, BF16),
+        ],
+        in_specs=[VMEM] * 4 + ([] if fresh else [HBM]),
+        out_specs=[VMEM, HBM],
         scratch_shapes=[pltpu.VMEM((rows, depth), BF16)],
+        input_output_aliases={} if fresh else {4: 1},
         compiler_params=pltpu.CompilerParams(vmem_limit_bytes=GRANT),
         cost_estimate=pl.CostEstimate(
             flops=2 * rows * depth * gates, transcendentals=0, bytes_accessed=rows * gates * 4
         ),
         name="pregate",
-    )(rows_in, w_conv, b_conv, w_input)
+    )(*operands, *([] if fresh else [out]))
 
 
 def gate_step(conv, pre, w_input, w_state, b_gates, hidden, cell, fresh_hidden, done, first):
@@ -153,19 +166,13 @@
             done(part)
 
 
-def step_kernel(on_first, on_later, on_own, carried, *refs):
-    own_refs = 2 if on_own is not None else 1
+def step_kernel(on_first, on_later, offset, inputs, *refs):
     rows_in, w_conv, b_conv, w_input, w_state, b_gates = refs[:6]
-    conv, spare = refs[-3:-1] if on_own is not None else refs[-2:]
+    ending = offset is not None
     me = lax.axis_index("snap")
-    start = 6 + (1 if on_own is not None else 0) + (2 if carried else 0)
-    if on_own is not None:
-        pre = refs[6]
-        out = refs[start]
-        hidden, cell = refs[start + 1 : start + 3]
-        sems = refs[-1]
-    else:
-        hidden, cell = refs[start : start + 2]
+    out, hidden, cell, conv, spare = refs[inputs : inputs + 5]
+    if ending:
+        pre, sems = refs[7], refs[-1]
 
     def taken(first):
         convolve(rows_in, w_conv, b_conv, conv)
@@ -186,13 +193,15 @@
         def _():
             taken(False)
 
-    if on_own is None:
+    if not ending:
         return
-    width = w_state.shape[0]
+    rows, width = spare.shape
 
     def sent(part):
         return pltpu.make_async_copy(
-            spare.at[:, part], out.at[0, :, part], sems.at[part.start * 2 // width]
+            spare.at[:, part],
+            out.at[0, offset : offset + rows, part],
+            sems.at[part.start * 2 // width],
         )
 
     def last(first):
@@ -221,31 +230,30 @@
         sent(slice(low, low + width // 2)).wait()
 
 
-def step(on_first, on_later, on_own, rows_in, weights, pre, state, name):
+def step(on_first, on_later, rows_in, weights, out, state, pre=None, offset=None):
     rows = rows_in.shape[0]
     depth, gates = weights[2].shape
     width = gates // 4
     shape = jax.ShapeDtypeStruct
-    operands = [rows_in, *weights]
-    if on_own is not None:
+    operands = [rows_in, *weights, out]
+    specs = [VMEM] * 6 + [HBM]
+    outs = [shape(out.shape, BF16), shape((rows, width), BF16), shape((rows, width), F32)]
+    scratch = [pltpu.VMEM((rows, depth), BF16), pltpu.VMEM((rows, width), BF16)]
+    aliases = {6: 0}
+    if offset is not None:
         operands.append(pre)
-    outs = [shape((rows, width), BF16), shape((rows, width), F32)]
-    out_specs = [VMEM, VMEM]
-    scratch = [pltpu.VMEM((rows, depth), BF16), pltpu.VMEM((rows, width), BF16)]
-    aliases = {}
-    if on_own is not None:
-        outs = [shape((1, rows, width), BF16)] + outs
-        out_specs = [HBM] + out_specs
+        specs.append(VMEM)
         scratch.append(pltpu.SemaphoreType.DMA((2,)))
     if state is not None:
-        skip = len(outs) - 2
-        aliases = {len(operands): skip, len(operands) + 1: skip + 1}
-        operands += state
+        for place, array in enumerate(state):
+            aliases[len(operands)] = 1 + place
+            operands.append(array)
+            specs.append(VMEM)
     return pl.pallas_call(
-        functools.partial(step_kernel, on_first, on_later, on_own, state is not None),
+        functools.partial(step_kernel, on_first, on_later, offset, len(operands)),
         out_shape=outs,
-        in_specs=[VMEM] * len(operands),
-        out_specs=out_specs,
+        in_specs=specs,
+        out_specs=[HBM, VMEM, VMEM],
         scratch_shapes=scratch,
         input_output_aliases=aliases,
         compiler_params=pltpu.CompilerParams(vmem_limit_bytes=GRANT),
@@ -254,7 +262,6 @@
             transcendentals=5 * rows * width,
             bytes_accessed=rows * width * 8,
         ),
-        name=name,
     )(*operands)
 
 
@@ -282,32 +289,65 @@
         pltpu.with_memory_space_constraint(array, pltpu.HBM)
         for array in (src_block, dst_block)
     ]
-    whole = aggregate(own, left, right, tiles, *lists, block_count)
+    halves = aggregate(PARTS, own, left, right, tiles, *lists, block_count)
     weights = [w_conv, b_conv, w_input, w_state, b_gates]
-
     handed = snaps >= 3
-    arrived = {}
-    for hop in range(last, 0, -1):
+
+    def shifted(part, hop):
         routes = [(i, i + hop) for i in range(snaps - hop)]
         if handed and hop == last - 1:
             routes = routes[1:]
-        arrived[hop] = lax.ppermute(whole, "snap", routes)
-    if handed:
-        passed_back = lax.ppermute(arrived[last], "snap", [(last, last - 1)])
-    pre = pregate(whole, w_conv, b_conv, w_input)
-
-    state = None
-    for stage in range(1, last):
+        return lax.ppermute(halves[part], "snap", routes)
+
+    arrived = {(hop, part): shifted(part, hop) for hop, part in sends(snaps)}
+    out = (1, own.shape[0], w_state.shape[0])
+    share = own.shape[0] // PARTS
+    pre = {}
+    for part in range(PARTS):
+        pre[part], out = pregate(halves[part], w_conv, b_conv, w_input, out)
+    passed_back = {}
+    states = {part: None for part in range(PARTS)}
+
+    def advance(part, stage):
         hop = snaps - stage
         on_first = [] if stage == 2 else [hop]
         on_later = None if stage == 1 else hop + 1
-        state = step(on_first, on_later, None, arrived[hop], weights, None, state, "step")
-        if stage == min(2, last - 1):
-            state = step([last - 1], None, None, passed_back, weights, None, state, "step_back")
-    on_first = [1] if snaps == 2 or snaps > 3 else []
-    on_later = 2 if handed else None
-    rows_in = arrived[1] if snaps > 1 else whole
-    return step(on_first, on_later, True, rows_in, weights, pre, state, "step_last")[0]
+        out_now, *state = step(on_first, on_later, arrived[hop, part], weights, out, states[part])
+        states[part] = state
+        return out_now
+
+    def receive_back(part):
+        out_now, *state = step([last - 1], None, passed_back[part], weights, out, states[part])
+        states[part] = state
+        return out_now
+
+    if handed:
+        for part in range(PARTS):
+            passed_back[part] = lax.ppermute(
+                arrived[last, part], "snap", [(last, last - 1)]
+            )
+            out = advance(part, 1) if snaps > 3 else out
+    for part in range(PARTS):
+        if snaps == 3:
+            out = advance(part, 1)
+        for stage in range(2, last):
+            out = advance(part, stage)
+            if stage == 2:
+                out = receive_back(part)
+        if snaps == 3:
+            out = receive_back(part)
+        on_first = [1] if snaps == 2 or snaps > 3 else []
+        on_later = 2 if handed else None
+        rows_in = arrived[1, part] if snaps > 1 else halves[part]
+        out = step(
+            on_first, on_later, rows_in, weights, out, states[part], pre[part], part * share
+        )[0]
+    return out
+
+
+def sends(snaps):
+    order = [(snaps - 1, part) for part in range(PARTS)] if snaps > 1 else []
+    return order + [(hop, part) for part in range(PARTS) for hop in range(snaps - 2, 0, -1)]
 
 
 def solution(mesh):
@@ -323,6 +363,7 @@
         P(),
         P(),
     )
+
     return jax.shard_map(
         shards, mesh=mesh, in_specs=placed, out_specs=P("snap", "vert", None), check_vma=False
     )

time: 39.2 us -> 43 us (1.097)
  the two profiles are of different devices: /device:TPU:20 before, /device:TPU:28 now
where the time goes in v3:
time: 43 us; the launch traced here: 42.7 us
  Pallas kernels  20.8 us (48%)
  starting transfers between devices  16.8 us (39%)
  waiting for transfers between devices  4.08 us (9%)
  between operations  1.02 us (2%)
    pallas_call x8, Pallas kernels, step(): pl.pallas_call(functools.partial(step_kernel, on_first, on_later, offset,...  15 us
    ppermute x6, starting transfers between devices, shifted(): return lax.ppermute(halves[part], 'snap', routes)  7.74 us
    ppermute x1, starting transfers between devices, shards(): lax.ppermute(features[0], 'vert', [(i + 1, i) for i in range(owners - 1)])  4.54 us
    ppermute x6, waiting for transfers between devices, shifted(): return lax.ppermute(halves[part], 'snap', routes)  3.83 us
    ppermute x2, starting transfers between devices, shards(): lax.ppermute(arrived[last, part], 'snap', [(last, last - 1)])  2.58 us
    pallas_call x1, Pallas kernels, load(): pl.pallas_call(functools.partial(load_kernel, len(arrays)), out_shape=[ja...  2.58 us
    pallas_call x2, Pallas kernels, pregate(): pl.pallas_call(pregate_kernel, out_shape=[jax.ShapeDtypeStruct((rows, gat...  2.2 us
    ppermute x1, starting transfers between devices, shards(): lax.ppermute(features[0], 'vert', [(i, i + 1) for i in range(owners - 1)])  1.91 us
  transfers between devices with their start and end apart: 10, of which 3 were waited for; matrix products, arithmetic and copies ran while one was open for 0% of the time, Pallas kernels for 36%

profile of v3, /device:TPU:28, one launch (start us, length us, event | category | flops | bytes accessed | tf_op | source)
XLA Modules:
  0.0 42.7 jit_solution(10875174869770626853)
XLA Ops:
  0.0 1.9 %collective-permute-start = (bf16[768,128]{1,0:T(8,128)(2,1)}, bf16[768,128]{1,0:T(8,128)(2,1)S(1)}, u32[]{:S(2)}, u32[]{:S(2)}) collective-permute-start(bf16[768,128]{1,0:T(8,128)(2,1)} %bitcast.5), channel_id=1, source_target_pairs={{0,1},{1,2},{2,3},{3,4},{4,5},{5,6},{6,7},{8,9},{9,10},{10,11},{11... | collective-permute-start | bytes 589832 | tf_op jit(solution)/shard_map/ppermute | solution.py:283
  1.9 4.5 %collective-permute-start.1 = (bf16[768,128]{1,0:T(8,128)(2,1)}, bf16[768,128]{1,0:T(8,128)(2,1)S(1)}, u32[]{:S(2)}, u32[]{:S(2)}) collective-permute-start(bf16[768,128]{1,0:T(8,128)(2,1)} %bitcast.6), channel_id=1, source_target_pairs={{1,0},{2,1},{3,2},{4,3},{5,4},{6,5},{7,6},{9,8},{10,9},{11,10},{12... | collective-permute-start | bytes 589832 | tf_op jit(solution)/shard_map/ppermute | solution.py:284
  7.1 2.6 %load.1 = (bf16[768,128]{1,0:T(8,128)(2,1)S(1)}, bf16[12,128,128]{2,1,0:T(8,128)(2,1)S(1)}, bf16[128,512]{1,0:T(8,128)(2,1)S(1)}, f32[1,512]{1,0:T(1,128)S(1)}, ...) custom-call(bf16[768,128]{1,0:T(8,128)(2,1)} %bitcast.7, ...), custom_call_target="tpu_custom_call" | custom-call | bytes 9850880 | tf_op jit(solution)/shard_map/load/pallas_call | solution.py:36
  9.7 0.0 collective-permute-done.left
  9.7 0.2 collective-permute-done.1.right
  9.9 1.0 %aggregate.1 = (bf16[384,128]{1,0:T(8,128)(2,1)S(1)}, bf16[384,128]{1,0:T(8,128)(2,1)S(1)}) custom-call(bf16[768,128]{1,0:T(8,128)(2,1)S(1)} %get-tuple-element.38.own, bf16[768,128]{1,0:T(8,128)(2,1)S(1)} %collective-permute-done.left, bf16[768,128]{1,0:T(8,128)(2,1)S(1)} %collective-permute-done.1.right, ...), custom_call_target="tpu_custom_call" | custom-call | tf_op jit(solution)/shard_map/aggregate/pallas_call | solution.py:88
  10.9 1.3 %collective-permute-start.7 = (bf16[384,128]{1,0:T(8,128)(2,1)S(1)}, bf16[384,128]{1,0:T(8,128)(2,1)S(1)}, u32[]{:S(2)}, u32[]{:S(2)}) collective-permute-start(bf16[384,128]{1,0:T(8,128)(2,1)S(1)} %get-tuple-element.46.rows_in), channel_id=1, source_target_pairs={{0,24},{1,25},{2,26},{3,27},{4,28},{5,29},{6,30},{7,31}} | collective-permute-start | bytes 294920 | tf_op jit(solution)/shard_map/ppermute | solution.py:300
  12.2 1.3 %collective-permute-start.9 = (bf16[384,128]{1,0:T(8,128)(2,1)S(1)}, bf16[384,128]{1,0:T(8,128)(2,1)S(1)}, u32[]{:S(2)}, u32[]{:S(2)}) collective-permute-start(bf16[384,128]{1,0:T(8,128)(2,1)S(1)} %get-tuple-element.46.rows_in), channel_id=1, source_target_pairs={{8,24},{9,25},{10,26},{11,27},{12,28},{13,29},{14,30},{15,31}} | collective-permute-start | bytes 294920 | tf_op jit(solution)/shard_map/ppermute | solution.py:300
  13.5 1.3 %collective-permute-start.6 = (bf16[384,128]{1,0:T(8,128)(2,1)S(1)}, bf16[384,128]{1,0:T(8,128)(2,1)S(1)}, u32[]{:S(2)}, u32[]{:S(2)}) collective-permute-start(bf16[384,128]{1,0:T(8,128)(2,1)S(1)} %get-tuple-element.46.rows_in), channel_id=1, source_target_pairs={{0,8},{8,16},{16,24},{1,9},{9,17},{17,25},{2,10},{10,18},{18,26},{... | collective-permute-start | bytes 294920 | tf_op jit(solution)/shard_map/ppermute | solution.py:300
  14.8 1.3 %collective-permute-start.3 = (bf16[384,128]{1,0:T(8,128)(2,1)S(1)}, bf16[384,128]{1,0:T(8,128)(2,1)S(1)}, u32[]{:S(2)}, u32[]{:S(2)}) collective-permute-start(bf16[384,128]{1,0:T(8,128)(2,1)S(1)} %get-tuple-element.40.rows_in), channel_id=1, source_target_pairs={{0,24},{1,25},{2,26},{3,27},{4,28},{5,29},{6,30},{7,31}} | collective-permute-start | bytes 294920 | tf_op jit(solution)/shard_map/ppermute | solution.py:300
  16.1 1.3 %collective-permute-start.5 = (bf16[384,128]{1,0:T(8,128)(2,1)S(1)}, bf16[384,128]{1,0:T(8,128)(2,1)S(1)}, u32[]{:S(2)}, u32[]{:S(2)}) collective-permute-start(bf16[384,128]{1,0:T(8,128)(2,1)S(1)} %get-tuple-element.40.rows_in), channel_id=1, source_target_pairs={{8,24},{9,25},{10,26},{11,27},{12,28},{13,29},{14,30},{15,31}} | collective-permute-start | bytes 294920 | tf_op jit(solution)/shard_map/ppermute | solution.py:300
  17.4 1.1 %pregate.2 = (f32[384,2048]{1,0:T(8,128)S(1)}, bf16[1,768,512]{2,1,0:T(8,128)(2,1)}) custom-call(bf16[384,128]{1,0:T(8,128)(2,1)S(1)} %get-tuple-element.46.rows_in, bf16[128,512]{1,0:T(8,128)(2,1)S(1)} %get-tuple-element.41.w_conv.refs_1_, f32[1,512]{1,0:T(1,128)S(1)} %get-tuple-element.42.b_conv.refs_2_, ...), custom_call_target="tpu_custom_call" | custom-call | flops 805306368 | bytes 3145728 | tf_op jit(solution)/shard_map/pregate/pallas_call | solution.py:123
  18.5 1.1 %pregate.3 = (f32[384,2048]{1,0:T(8,128)S(1)}, bf16[1,768,512]{2,1,0:T(8,128)(2,1)}) custom-call(bf16[384,128]{1,0:T(8,128)(2,1)S(1)} %get-tuple-element.40.rows_in, bf16[128,512]{1,0:T(8,128)(2,1)S(1)} %get-tuple-element.41.w_conv.refs_1_, f32[1,512]{1,0:T(1,128)S(1)} %get-tuple-element.42.b_conv.refs_2_, ...), custom_call_target="tpu_custom_call", output_to_operand_aliasing={{1}: (4, {})} | custom-call | flops 805306368 | bytes 3145728 | tf_op jit(solution)/shard_map/pregate/pallas_call | solution.py:123
  19.7 0.6 %collective-permute-done.7.refs_0_ = bf16[384,128]{1,0:T(8,128)(2,1)S(1)} collective-permute-done((bf16[384,128]{1,0:T(8,128)(2,1)S(1)}, bf16[384,128]{1,0:T(8,128)(2,1)S(1)}, u32[]{:S(2)}, u32[]{:S(2)}) %collective-permute-start.7) | collective-permute-done | bytes 98336 | tf_op jit(solution)/shard_map/ppermute | solution.py:300
  20.3 1.3 %collective-permute-start.2 = (bf16[384,128]{1,0:T(8,128)(2,1)S(1)}, bf16[384,128]{1,0:T(8,128)(2,1)S(1)}, u32[]{:S(2)}, u32[]{:S(2)}) collective-permute-start(bf16[384,128]{1,0:T(8,128)(2,1)S(1)} %get-tuple-element.40.rows_in), channel_id=1, source_target_pairs={{0,8},{8,16},{16,24},{1,9},{9,17},{17,25},{2,10},{10,18},{18,26},{... | collective-permute-start | bytes 294920 | tf_op jit(solution)/shard_map/ppermute | solution.py:300
  21.6 1.0 %shard_map.100 = (bf16[1,768,512]{2,1,0:T(8,128)(2,1)}, bf16[384,512]{1,0:T(8,128)(2,1)S(1)}, f32[384,512]{1,0:T(8,128)S(1)}) custom-call(bf16[384,128]{1,0:T(8,128)(2,1)S(1)} %collective-permute-done.7.refs_0_, bf16[128,512]{1,0:T(8,128)(2,1)S(1)} %get-tuple-element.41.w_conv.refs_1_, ...), custom_call_target="tpu_custom_call", output_to_operand_aliasing={{0}: (6, {})} | custom-call | flops 1610612736 | bytes 1572864 | tf_op jit(solution)/shard_map/pallas_call | solution.py:252
  22.6 3.2 %collective-permute-done.3.refs_0_ = bf16[384,128]{1,0:T(8,128)(2,1)S(1)} collective-permute-done((bf16[384,128]{1,0:T(8,128)(2,1)S(1)}, bf16[384,128]{1,0:T(8,128)(2,1)S(1)}, u32[]{:S(2)}, u32[]{:S(2)}) %collective-permute-start.3) | collective-permute-done | bytes 98336 | tf_op jit(solution)/shard_map/ppermute | solution.py:300
  25.8 1.3 %collective-permute-start.8 = (bf16[384,128]{1,0:T(8,128)(2,1)S(1)}, bf16[384,128]{1,0:T(8,128)(2,1)S(1)}, u32[]{:S(2)}, u32[]{:S(2)}) collective-permute-start(bf16[384,128]{1,0:T(8,128)(2,1)S(1)} %collective-permute-done.7.refs_0_), channel_id=1, source_target_pairs={{24,16},{25,17},{26,18},{27,19},{28,20},{29,21},{30,22},{31,23}} | collective-permute-start | bytes 294920 | tf_op jit(solution)/shard_map/ppermute | solution.py:326
  27.1 1.0 %shard_map.101 = (bf16[1,768,512]{2,1,0:T(8,128)(2,1)}, bf16[384,512]{1,0:T(8,128)(2,1)S(1)}, f32[384,512]{1,0:T(8,128)S(1)}) custom-call(bf16[384,128]{1,0:T(8,128)(2,1)S(1)} %collective-permute-done.3.refs_0_, bf16[128,512]{1,0:T(8,128)(2,1)S(1)} %get-tuple-element.41.w_conv.refs_1_, ...), custom_call_target="tpu_custom_call", output_to_operand_aliasing={{0}: (6, {})} | custom-call | flops 1610612736 | bytes 1572864 | tf_op jit(solution)/shard_map/pallas_call | solution.py:252
  28.1 1.3 %collective-permute-start.4 = (bf16[384,128]{1,0:T(8,128)(2,1)S(1)}, bf16[384,128]{1,0:T(8,128)(2,1)S(1)}, u32[]{:S(2)}, u32[]{:S(2)}) collective-permute-start(bf16[384,128]{1,0:T(8,128)(2,1)S(1)} %collective-permute-done.3.refs_0_), channel_id=1, source_target_pairs={{24,16},{25,17},{26,18},{27,19},{28,20},{29,21},{30,22},{31,23}} | collective-permute-start | bytes 294920 | tf_op jit(solution)/shard_map/ppermute | solution.py:326
  29.5 2.1 %shard_map.102 = (bf16[1,768,512]{2,1,0:T(8,128)(2,1)}, bf16[384,512]{1,0:T(8,128)(2,1)S(1)}, f32[384,512]{1,0:T(8,128)S(1)}) custom-call(bf16[384,128]{1,0:T(8,128)(2,1)S(1)} %collective-permute-done.9.refs_0_, bf16[128,512]{1,0:T(8,128)(2,1)S(1)} %get-tuple-element.41.w_conv.refs_1_, ...), custom_call_target="tpu_custom_call", output_to_operand_aliasing={{0}: (6, {}), {1}: (7, {}), {2}: (8, {})} | custom-call | flops 1610612736 | bytes 1572864 | tf_op jit(solution)/shard_map/pallas_call | solution.py:252
  31.6 4.2 %shard_map.104 = (bf16[1,768,512]{2,1,0:T(8,128)(2,1)}, bf16[384,512]{1,0:T(8,128)(2,1)S(1)}, f32[384,512]{1,0:T(8,128)S(1)}) custom-call(bf16[384,128]{1,0:T(8,128)(2,1)S(1)} %collective-permute-done.6.refs_0_, bf16[128,512]{1,0:T(8,128)(2,1)S(1)} %get-tuple-element.41.w_conv.refs_1_, ...), custom_call_target="tpu_custom_call", output_to_operand_aliasing={{0}: (6, {}), {1}: (8, {}), {2}: (9, {})} | custom-call | flops 1610612736 | bytes 1572864 | tf_op jit(solution)/shard_map/pallas_call | solution.py:252
  35.9 2.3 %shard_map.105 = (bf16[1,768,512]{2,1,0:T(8,128)(2,1)}, bf16[384,512]{1,0:T(8,128)(2,1)S(1)}, f32[384,512]{1,0:T(8,128)S(1)}) custom-call(bf16[384,128]{1,0:T(8,128)(2,1)S(1)} %collective-permute-done.5.refs_0_, bf16[128,512]{1,0:T(8,128)(2,1)S(1)} %get-tuple-element.41.w_conv.refs_1_, ...), custom_call_target="tpu_custom_call", output_to_operand_aliasing={{0}: (6, {}), {1}: (7, {}), {2}: (8, {})} | custom-call | flops 1610612736 | bytes 1572864 | tf_op jit(solution)/shard_map/pallas_call | solution.py:252
  38.3 4.2 %shard_map.107 = (bf16[1,768,512]{2,1,0:T(8,128)(2,1)}, bf16[384,512]{1,0:T(8,128)(2,1)S(1)}, f32[384,512]{1,0:T(8,128)S(1)}) custom-call(bf16[384,128]{1,0:T(8,128)(2,1)S(1)} %collective-permute-done.2.refs_0_, bf16[128,512]{1,0:T(8,128)(2,1)S(1)} %get-tuple-element.41.w_conv.refs_1_, ...), custom_call_target="tpu_custom_call", output_to_operand_aliasing={{0}: (6, {}), {1}: (8, {}), {2}: (9, {})} | custom-call | flops 1610612736 | bytes 1572864 | tf_op jit(solution)/shard_map/pallas_call | solution.py:252
  (8 shorter events, 0.1 us)
Async XLA Ops:
  0.0 9.7 %collective-permute-start = (bf16[768,128]{1,0:T(8,128)(2,1)}, bf16[768,128]{1,0:T(8,128)(2,1)S(1)}, u32[]{:S(2)}, u32[]{:S(2)}) collective-permute-start(bf16[768,128]{1,0:T(8,128)(2,1)} %bitcast.5), channel_id=1, source_target_pairs={{0,1},{1,2},{2,3},{3,4},{4,5},{5,6},{6,7},{8,9},{9,10},{10,11},{11... | collective-permute-start | bytes 589832 | tf_op jit(solution)/shard_map/ppermute | solution.py:283
  1.9 8.0 %collective-permute-start.1 = (bf16[768,128]{1,0:T(8,128)(2,1)}, bf16[768,128]{1,0:T(8,128)(2,1)S(1)}, u32[]{:S(2)}, u32[]{:S(2)}) collective-permute-start(bf16[768,128]{1,0:T(8,128)(2,1)} %bitcast.6), channel_id=1, source_target_pairs={{1,0},{2,1},{3,2},{4,3},{5,4},{6,5},{7,6},{9,8},{10,9},{11,10},{12... | collective-permute-start | bytes 589832 | tf_op jit(solution)/shard_map/ppermute | solution.py:284
  10.9 9.3 %collective-permute-start.7 = (bf16[384,128]{1,0:T(8,128)(2,1)S(1)}, bf16[384,128]{1,0:T(8,128)(2,1)S(1)}, u32[]{:S(2)}, u32[]{:S(2)}) collective-permute-start(bf16[384,128]{1,0:T(8,128)(2,1)S(1)} %get-tuple-element.46.rows_in), channel_id=1, source_target_pairs={{0,24},{1,25},{2,26},{3,27},{4,28},{5,29},{6,30},{7,31}} | collective-permute-start | bytes 294920 | tf_op jit(solution)/shard_map/ppermute | solution.py:300
  12.2 15.9 %collective-permute-start.9 = (bf16[384,128]{1,0:T(8,128)(2,1)S(1)}, bf16[384,128]{1,0:T(8,128)(2,1)S(1)}, u32[]{:S(2)}, u32[]{:S(2)}) collective-permute-start(bf16[384,128]{1,0:T(8,128)(2,1)S(1)} %get-tuple-element.46.rows_in), channel_id=1, source_target_pairs={{8,24},{9,25},{10,26},{11,27},{12,28},{13,29},{14,30},{15,31}} | collective-permute-start | bytes 294920 | tf_op jit(solution)/shard_map/ppermute | solution.py:300
  13.5 18.1 %collective-permute-start.6 = (bf16[384,128]{1,0:T(8,128)(2,1)S(1)}, bf16[384,128]{1,0:T(8,128)(2,1)S(1)}, u32[]{:S(2)}, u32[]{:S(2)}) collective-permute-start(bf16[384,128]{1,0:T(8,128)(2,1)S(1)} %get-tuple-element.46.rows_in), channel_id=1, source_target_pairs={{0,8},{8,16},{16,24},{1,9},{9,17},{17,25},{2,10},{10,18},{18,26},{... | collective-permute-start | bytes 294920 | tf_op jit(solution)/shard_map/ppermute | solution.py:300
  14.8 11.0 %collective-permute-start.3 = (bf16[384,128]{1,0:T(8,128)(2,1)S(1)}, bf16[384,128]{1,0:T(8,128)(2,1)S(1)}, u32[]{:S(2)}, u32[]{:S(2)}) collective-permute-start(bf16[384,128]{1,0:T(8,128)(2,1)S(1)} %get-tuple-element.40.rows_in), channel_id=1, source_target_pairs={{0,24},{1,25},{2,26},{3,27},{4,28},{5,29},{6,30},{7,31}} | collective-permute-start | bytes 294920 | tf_op jit(solution)/shard_map/ppermute | solution.py:300
  16.1 19.8 %collective-permute-start.5 = (bf16[384,128]{1,0:T(8,128)(2,1)S(1)}, bf16[384,128]{1,0:T(8,128)(2,1)S(1)}, u32[]{:S(2)}, u32[]{:S(2)}) collective-permute-start(bf16[384,128]{1,0:T(8,128)(2,1)S(1)} %get-tuple-element.40.rows_in), channel_id=1, source_target_pairs={{8,24},{9,25},{10,26},{11,27},{12,28},{13,29},{14,30},{15,31}} | collective-permute-start | bytes 294920 | tf_op jit(solution)/shard_map/ppermute | solution.py:300
  20.3 18.0 %collective-permute-start.2 = (bf16[384,128]{1,0:T(8,128)(2,1)S(1)}, bf16[384,128]{1,0:T(8,128)(2,1)S(1)}, u32[]{:S(2)}, u32[]{:S(2)}) collective-permute-start(bf16[384,128]{1,0:T(8,128)(2,1)S(1)} %get-tuple-element.40.rows_in), channel_id=1, source_target_pairs={{0,8},{8,16},{16,24},{1,9},{9,17},{17,25},{2,10},{10,18},{18,26},{... | collective-permute-start | bytes 294920 | tf_op jit(solution)/shard_map/ppermute | solution.py:300
  25.8 5.8 %collective-permute-start.8 = (bf16[384,128]{1,0:T(8,128)(2,1)S(1)}, bf16[384,128]{1,0:T(8,128)(2,1)S(1)}, u32[]{:S(2)}, u32[]{:S(2)}) collective-permute-start(bf16[384,128]{1,0:T(8,128)(2,1)S(1)} %collective-permute-done.7.refs_0_), channel_id=1, source_target_pairs={{24,16},{25,17},{26,18},{27,19},{28,20},{29,21},{30,22},{31,23}} | collective-permute-start | bytes 294920 | tf_op jit(solution)/shard_map/ppermute | solution.py:326
  28.1 10.1 %collective-permute-start.4 = (bf16[384,128]{1,0:T(8,128)(2,1)S(1)}, bf16[384,128]{1,0:T(8,128)(2,1)S(1)}, u32[]{:S(2)}, u32[]{:S(2)}) collective-permute-start(bf16[384,128]{1,0:T(8,128)(2,1)S(1)} %collective-permute-done.3.refs_0_), channel_id=1, source_target_pairs={{24,16},{25,17},{26,18},{27,19},{28,20},{29,21},{30,22},{31,23}} | collective-permute-start | bytes 294920 | tf_op jit(solution)/shard_map/ppermute | solution.py:326

commit v4 on v3

--- a/solution.py
+++ b/solution.py
@@ -15,7 +15,8 @@
 SMEM = pl.BlockSpec(memory_space=pltpu.SMEM)
 HBM = pl.BlockSpec(memory_space=pltpu.HBM)
 GRANT = 24 << 20
-PARTS = 2
+PARTS = 1
+LAST_BLOCKS = 4
 
 
 def load_kernel(total, *refs):
@@ -106,39 +107,51 @@
     conv[...] = jnp.maximum(reached, 0.0).astype(BF16)
 
 
-def pregate_kernel(rows_in, w_conv, b_conv, w_input, *refs):
+def bias_of(b_gates, gate, part):
+    return b_gates[:, part] + (forget_bias if gate == 1 else 0.0)
+
+
+def pregate_kernel(only, rows_in, w_conv, b_conv, w_input, b_gates, *refs):
     pre, _, conv = refs[-3:]
-    convolve(rows_in, w_conv, b_conv, conv)
     width = w_input.shape[1] // 4
-    for gate in range(4):
-        part = slice(gate * width, (gate + 1) * width)
-        pre[:, part] = jnp.dot(conv[...], w_input[:, part], preferred_element_type=F32)
-
-
-def pregate(rows_in, w_conv, b_conv, w_input, out):
+
+    def run():
+        convolve(rows_in, w_conv, b_conv, conv)
+        for gate in range(4):
+            part = slice(gate * width, (gate + 1) * width)
+            pre[:, part] = jnp.dot(
+                conv[...], w_input[:, part], preferred_element_type=F32
+            ) + bias_of(b_gates, gate, part)
+
+    if only is None:
+        run()
+    else:
+        pl.when(lax.axis_index("snap") == only)(run)
+
+
+def pregate(only, rows_in, w_conv, b_conv, w_input, b_gates, out):
     rows = rows_in.shape[0]
     depth, gates = w_input.shape
-    operands = [rows_in, w_conv, b_conv, w_input]
     fresh = isinstance(out, tuple)
     return pl.pallas_call(
-        pregate_kernel,
+        functools.partial(pregate_kernel, only),
         out_shape=[
             jax.ShapeDtypeStruct((rows, gates), F32),
             jax.ShapeDtypeStruct(out if fresh else out.shape, BF16),
         ],
-        in_specs=[VMEM] * 4 + ([] if fresh else [HBM]),
+        in_specs=[VMEM] * 5 + ([] if fresh else [HBM]),
         out_specs=[VMEM, HBM],
         scratch_shapes=[pltpu.VMEM((rows, depth), BF16)],
-        input_output_aliases={} if fresh else {4: 1},
+        input_output_aliases={} if fresh else {5: 1},
         compiler_params=pltpu.CompilerParams(vmem_limit_bytes=GRANT),
         cost_estimate=pl.CostEstimate(
             flops=2 * rows * depth * gates, transcendentals=0, bytes_accessed=rows * gates * 4
         ),
         name="pregate",
-    )(*operands, *([] if fresh else [out]))
-
-
-def gate_step(conv, pre, w_input, w_state, b_gates, hidden, cell, fresh_hidden, done, first):
+    )(rows_in, w_conv, b_conv, w_input, b_gates, *([] if fresh else [out]))
+
+
+def gate_step(inner, pre, w_input, w_state, b_gates, hidden, cell, target, rows, store_cell=True):
     width = w_state.shape[0]
     chunk = width // 2
     for low in range(0, width, chunk):
@@ -146,115 +159,60 @@
         for gate in range(4):
             part = slice(gate * width + low, gate * width + low + chunk)
             if pre is None:
-                value = jnp.dot(conv[...], w_input[:, part], preferred_element_type=F32)
+                value = jnp.dot(inner[rows], w_input[:, part], preferred_element_type=F32)
             else:
-                value = pre[:, part]
-            if not first:
-                value += jnp.dot(hidden[...], w_state[:, part], preferred_element_type=F32)
-            bias = b_gates[:, part]
-            if gate == 1:
-                bias = bias + forget_bias
-            gates.append(value + bias)
+                value = pre[rows, part]
+            if hidden is not None:
+                value += jnp.dot(hidden[rows], w_state[:, part], preferred_element_type=F32)
+            if pre is None:
+                value += bias_of(b_gates, gate, part)
+            gates.append(value)
         part = slice(low, low + chunk)
         fresh = (0.5 * jnp.tanh(0.5 * gates[0]) + 0.5) * jnp.tanh(gates[2])
-        if not first:
-            fresh += (0.5 * jnp.tanh(0.5 * gates[1]) + 0.5) * cell[:, part]
-        cell[:, part] = fresh
+        if hidden is not None:
+            fresh += (0.5 * jnp.tanh(0.5 * gates[1]) + 0.5) * cell[rows, part]
+        if store_cell:
+            cell[rows, part] = fresh
         shown = (0.5 * jnp.tanh(0.5 * gates[3]) + 0.5) * jnp.tanh(fresh)
-        fresh_hidden[:, part] = shown.astype(BF16)
-        if done is not None:
-            done(part)
-
-
-def step_kernel(on_first, on_later, offset, inputs, *refs):
+        target[rows, part] = shown.astype(BF16)
+
+
+def step_kernel(on_first, on_later, inputs, *refs):
     rows_in, w_conv, b_conv, w_input, w_state, b_gates = refs[:6]
-    ending = offset is not None
+    before = refs[7] if inputs > 7 else None
+    _, hidden, cell, conv = refs[inputs:]
     me = lax.axis_index("snap")
-    out, hidden, cell, conv, spare = refs[inputs : inputs + 5]
-    if ending:
-        pre, sems = refs[7], refs[-1]
+    every = slice(None)
 
     def taken(first):
         convolve(rows_in, w_conv, b_conv, conv)
-        target = hidden if first else spare
-        gate_step(conv, None, w_input, w_state, b_gates, hidden, cell, target, None, first)
-        if not first:
-            hidden[...] = spare[...]
+        source = None if first else before
+        gate_step(conv, None, w_input, w_state, b_gates, source, cell, hidden, every)
 
     for device in on_first:
-
-        @pl.when(me == device)
-        def _():
-            taken(True)
-
+        pl.when(me == device)(functools.partial(taken, True))
     if on_later is not None:
-
-        @pl.when(me >= on_later)
-        def _():
-            taken(False)
-
-    if not ending:
-        return
-    rows, width = spare.shape
-
-    def sent(part):
-        return pltpu.make_async_copy(
-            spare.at[:, part],
-            out.at[0, offset : offset + rows, part],
-            sems.at[part.start * 2 // width],
-        )
-
-    def last(first):
-        gate_step(
-            conv,
-            pre,
-            w_input,
-            w_state,
-            b_gates,
-            hidden,
-            cell,
-            spare,
-            lambda part: sent(part).start(),
-            first,
-        )
-
-    @pl.when(me == 0)
-    def _():
-        last(True)
-
-    @pl.when(me > 0)
-    def _():
-        last(False)
-
-    for low in range(0, width, width // 2):
-        sent(slice(low, low + width // 2)).wait()
-
-
-def step(on_first, on_later, rows_in, weights, out, state, pre=None, offset=None):
+        pl.when(me >= on_later)(functools.partial(taken, False))
+
+
+def step(on_first, on_later, rows_in, weights, out, state):
     rows = rows_in.shape[0]
     depth, gates = weights[2].shape
     width = gates // 4
     shape = jax.ShapeDtypeStruct
     operands = [rows_in, *weights, out]
-    specs = [VMEM] * 6 + [HBM]
-    outs = [shape(out.shape, BF16), shape((rows, width), BF16), shape((rows, width), F32)]
-    scratch = [pltpu.VMEM((rows, depth), BF16), pltpu.VMEM((rows, width), BF16)]
     aliases = {6: 0}
-    if offset is not None:
-        operands.append(pre)
-        specs.append(VMEM)
-        scratch.append(pltpu.SemaphoreType.DMA((2,)))
     if state is not None:
-        for place, array in enumerate(state):
-            aliases[len(operands)] = 1 + place
-            operands.append(array)
-            specs.append(VMEM)
+        aliases[8] = 2
+        if on_later is None:
+            aliases[7] = 1
+        operands += state
     return pl.pallas_call(
-        functools.partial(step_kernel, on_first, on_later, offset, len(operands)),
-        out_shape=outs,
-        in_specs=specs,
+        functools.partial(step_kernel, on_first, on_later, len(operands)),
+        out_shape=[shape(out.shape, BF16), shape((rows, width), BF16), shape((rows, width), F32)],
+        in_specs=[VMEM] * 6 + [HBM] + [VMEM] * (len(operands) - 7),
         out_specs=[HBM, VMEM, VMEM],
-        scratch_shapes=scratch,
+        scratch_shapes=[pltpu.VMEM((rows, depth), BF16)],
         input_output_aliases=aliases,
         compiler_params=pltpu.CompilerParams(vmem_limit_bytes=GRANT),
         cost_estimate=pl.CostEstimate(
@@ -263,6 +221,93 @@
             bytes_accessed=rows * width * 8,
         ),
     )(*operands)
+
+
+def finish_kernel(snaps, offset, *refs):
+    rows_in, w_conv, b_conv, w_input, w_state, b_gates, _, pre = refs[:8]
+    out, cell, conv, middle, shown, sems = refs[-6:]
+    before = refs[8] if snaps >= 3 else None
+    prepared = refs[10] if snaps > 3 else None
+    me = lax.axis_index("snap")
+    rows = shown.shape[0]
+    every = slice(None)
+
+    def taken(first, ready):
+        if ready is None:
+            convolve(rows_in, w_conv, b_conv, conv)
+        source = None if first else before
+        gate_step(conv, ready, w_input, w_state, b_gates, source, cell, middle, every)
+
+    if snaps == 3:
+
+        @pl.when(me == 1)
+        def _():
+            middle[...] = before[...]
+
+    if snaps == 2 or snaps > 3:
+        pl.when(me == 1)(functools.partial(taken, True, None))
+    if snaps > 3:
+        pl.when(me == snaps - 2)(functools.partial(taken, False, prepared))
+        pl.when((me > 1) & (me != snaps - 2))(functools.partial(taken, False, None))
+    elif snaps == 3:
+        pl.when(me == 2)(functools.partial(taken, False, None))
+
+    blocks = LAST_BLOCKS if rows % (16 * LAST_BLOCKS) == 0 else 1
+    share = rows // blocks
+
+    def sent(block):
+        start = block * share
+        return pltpu.make_async_copy(
+            shown.at[start : start + share],
+            out.at[0, offset + start : offset + start + share],
+            sems.at[block],
+        )
+
+    def last(first):
+        source = None if first else middle
+        for block in range(blocks):
+            part = slice(block * share, (block + 1) * share)
+            gate_step(None, pre, w_input, w_state, b_gates, source, cell, shown, part, False)
+            sent(block).start()
+
+    pl.when(me == 0)(functools.partial(last, True))
+    pl.when(me > 0)(functools.partial(last, False))
+    for block in range(blocks):
+        sent(block).wait()
+
+
+def finish(snaps, offset, rows_in, weights, out, pre, state, prepared):
+    rows = rows_in.shape[0]
+    depth, gates = weights[2].shape
+    width = gates // 4
+    shape = jax.ShapeDtypeStruct
+    operands = [rows_in, *weights, out, pre]
+    aliases = {6: 0}
+    if state is not None:
+        aliases[9] = 1
+        operands += state
+    if prepared is not None:
+        operands.append(prepared)
+    return pl.pallas_call(
+        functools.partial(finish_kernel, snaps, offset),
+        out_shape=[shape(out.shape, BF16), shape((rows, width), F32)],
+        in_specs=[VMEM] * 6 + [HBM] + [VMEM] * (len(operands) - 7),
+        out_specs=[HBM, VMEM],
+        scratch_shapes=[
+            pltpu.VMEM((rows, depth), BF16),
+            pltpu.VMEM((rows, width), BF16),
+            pltpu.VMEM((rows, width), BF16),
+            pltpu.SemaphoreType.DMA((LAST_BLOCKS,)),
+        ],
+        input_output_aliases=aliases,
+        compiler_params=pltpu.CompilerParams(vmem_limit_bytes=GRANT),
+        cost_estimate=pl.CostEstimate(
+            flops=2 * rows * (depth + 2 * width) * gates,
+            transcendentals=10 * rows * width,
+            bytes_accessed=rows * width * 8,
+        ),
+        name="finish",
+    )(*operands)[0]
 
 
 def shards(
@@ -304,7 +349,7 @@
     share = own.shape[0] // PARTS
     pre = {}
     for part in range(PARTS):
-        pre[part], out = pregate(halves[part], w_conv, b_conv, w_input, out)
+        pre[part], out = pregate(None, halves[part], w_conv, b_conv, w_input, b_gates, out)
     passed_back = {}
     states = {part: None for part in range(PARTS)}
 
@@ -314,6 +359,14 @@
         on_later = None if stage == 1 else hop + 1
         out_now, *state = step(on_first, on_later, arrived[hop, part], weights, out, states[part])
         states[part] = state
+        return out_now
+
+    prepared = {part: None for part in range(PARTS)}
+
+    def prepare(part):
+        prepared[part], out_now = pregate(
+            last - 1, arrived[1, part], w_conv, b_conv, w_input, b_gates, out
+        )
         return out_now
 
     def receive_back(part):
@@ -333,15 +386,14 @@
         for stage in range(2, last):
             out = advance(part, stage)
             if stage == 2:
+                out = prepare(part)
                 out = receive_back(part)
         if snaps == 3:
             out = receive_back(part)
-        on_first = [1] if snaps == 2 or snaps > 3 else []
-        on_later = 2 if handed else None
         rows_in = arrived[1, part] if snaps > 1 else halves[part]
-        out = step(
-            on_first, on_later, rows_in, weights, out, states[part], pre[part], part * share
-        )[0]
+        out = finish(
+            snaps, part * share, rows_in, weights, out, pre[part], states[part], prepared[part]
+        )
     return out
 
 

time: 43 us -> 39.6 us (0.921)
  the two profiles are of different devices: /device:TPU:28 before, /device:TPU:19 now
where the time goes in v4:
time: 39.6 us; the launch traced here: 39.4 us
  Pallas kernels  14.9 us (38%)
  starting transfers between devices  13.5 us (34%)
  waiting for transfers between devices  9.96 us (25%)
  between operations  0.95 us (2%)
    ppermute x3, waiting for transfers between devices, shifted(): return lax.ppermute(halves[part], 'snap', routes)  9.95 us
    ppermute x3, starting transfers between devices, shifted(): return lax.ppermute(halves[part], 'snap', routes)  5.79 us
    pallas_call x1, Pallas kernels, finish(): pl.pallas_call(functools.partial(finish_kernel, snaps, offset), out_shape...  5.55 us
    pallas_call x2, Pallas kernels, pregate(): pl.pallas_call(functools.partial(pregate_kernel, only), out_shape=[jax.Sh...  4 us
    ppermute x1, starting transfers between devices, shards(): lax.ppermute(features[0], 'vert', [(i, i + 1) for i in range(owners - 1)])  3.88 us
    pallas_call x1, Pallas kernels, load(): pl.pallas_call(functools.partial(load_kernel, len(arrays)), out_shape=[ja...  2.58 us
    ppermute x1, starting transfers between devices, shards(): lax.ppermute(features[0], 'vert', [(i + 1, i) for i in range(owners - 1)])  2.57 us
    pallas_call x3, Pallas kernels, step(): pl.pallas_call(functools.partial(step_kernel, on_first, on_later, len(ope...  1.82 us
  transfers between devices with their start and end apart: 6, of which 1 were waited for; matrix products, arithmetic and copies ran while one was open for 0% of the time, Pallas kernels for 17%

profile of v4, /device:TPU:19, one launch (start us, length us, event | category | flops | bytes accessed | tf_op | source)
XLA Modules:
  0.0 39.4 jit_solution(4981184307283300204)
XLA Ops:
  0.0 2.6 %collective-permute-start.1 = (bf16[768,128]{1,0:T(8,128)(2,1)}, bf16[768,128]{1,0:T(8,128)(2,1)S(1)}, u32[]{:S(2)}, u32[]{:S(2)}) collective-permute-start(bf16[768,128]{1,0:T(8,128)(2,1)} %bitcast.5), channel_id=1, source_target_pairs={{1,0},{2,1},{3,2},{4,3},{5,4},{6,5},{7,6},{9,8},{10,9},{11,10},{12... | collective-permute-start | bytes 589832 | tf_op jit(solution)/shard_map/ppermute | solution.py:329
  2.6 3.9 %collective-permute-start = (bf16[768,128]{1,0:T(8,128)(2,1)}, bf16[768,128]{1,0:T(8,128)(2,1)S(1)}, u32[]{:S(2)}, u32[]{:S(2)}) collective-permute-start(bf16[768,128]{1,0:T(8,128)(2,1)} %bitcast.6), channel_id=1, source_target_pairs={{0,1},{1,2},{2,3},{3,4},{4,5},{5,6},{6,7},{8,9},{9,10},{10,11},{11... | collective-permute-start | bytes 589832 | tf_op jit(solution)/shard_map/ppermute | solution.py:328
  7.1 2.6 %load.1 = (bf16[768,128]{1,0:T(8,128)(2,1)S(1)}, bf16[12,128,128]{2,1,0:T(8,128)(2,1)S(1)}, bf16[128,512]{1,0:T(8,128)(2,1)S(1)}, f32[1,512]{1,0:T(1,128)S(1)}, ...) custom-call(bf16[768,128]{1,0:T(8,128)(2,1)} %bitcast.7, ...), custom_call_target="tpu_custom_call" | custom-call | bytes 9850880 | tf_op jit(solution)/shard_map/load/pallas_call | solution.py:37
  9.7 0.0 collective-permute-done.1.right
  9.7 0.0 collective-permute-done.left
  9.7 1.0 %aggregate.1.rows_in = bf16[768,128]{1,0:T(8,128)(2,1)S(1)} custom-call(bf16[768,128]{1,0:T(8,128)(2,1)S(1)} %get-tuple-element.26.own, bf16[768,128]{1,0:T(8,128)(2,1)S(1)} %collective-permute-done.left, bf16[768,128]{1,0:T(8,128)(2,1)S(1)} %collective-permute-done.1.right, bf16[12,128,128]{2,1,0:T(8,128)(2,1)S(1)} %get-tuple-element.27.tiles, ...), custom_call_target="tpu_custom_call" | custom-call | tf_op jit(solution)/shard_map/aggregate/pallas_call | solution.py:89
  10.7 0.7 %collective-permute-start.3 = (bf16[768,128]{1,0:T(8,128)(2,1)S(1)}, bf16[768,128]{1,0:T(8,128)(2,1)S(1)}, u32[]{:S(2)}, u32[]{:S(2)}) collective-permute-start(bf16[768,128]{1,0:T(8,128)(2,1)S(1)} %aggregate.1.rows_in), channel_id=1, source_target_pairs={{0,24},{1,25},{2,26},{3,27},{4,28},{5,29},{6,30},{7,31}} | collective-permute-start | bytes 589832 | tf_op jit(solution)/shard_map/ppermute | solution.py:345
  11.4 0.7 %collective-permute-start.5 = (bf16[768,128]{1,0:T(8,128)(2,1)S(1)}, bf16[768,128]{1,0:T(8,128)(2,1)S(1)}, u32[]{:S(2)}, u32[]{:S(2)}) collective-permute-start(bf16[768,128]{1,0:T(8,128)(2,1)S(1)} %aggregate.1.rows_in), channel_id=1, source_target_pairs={{8,24},{9,25},{10,26},{11,27},{12,28},{13,29},{14,30},{15,31}} | collective-permute-start | bytes 589832 | tf_op jit(solution)/shard_map/ppermute | solution.py:345
  12.1 4.4 %collective-permute-start.2 = (bf16[768,128]{1,0:T(8,128)(2,1)S(1)}, bf16[768,128]{1,0:T(8,128)(2,1)S(1)}, u32[]{:S(2)}, u32[]{:S(2)}) collective-permute-start(bf16[768,128]{1,0:T(8,128)(2,1)S(1)} %aggregate.1.rows_in), channel_id=1, source_target_pairs={{0,8},{8,16},{16,24},{1,9},{9,17},{17,25},{2,10},{10,18},{18,26},{... | collective-permute-start | bytes 589832 | tf_op jit(solution)/shard_map/ppermute | solution.py:345
  16.5 2.0 %pregate.2 = (f32[768,2048]{1,0:T(8,128)S(1)}, bf16[1,768,512]{2,1,0:T(8,128)(2,1)}) custom-call(bf16[768,128]{1,0:T(8,128)(2,1)S(1)} %aggregate.1.rows_in, bf16[128,512]{1,0:T(8,128)(2,1)S(1)} %get-tuple-element.28.w_conv.refs_1_, f32[1,512]{1,0:T(1,128)S(1)} %get-tuple-element.29.b_conv.refs_2_, bf16[512,2048]{1,0:T(8,128)(2,1)S(1)} %get-tuple-element.30.w_input.refs_3_, ...), custom_call_target="tpu_custom_call" | custom-call | flops 1610612736 | bytes 6291456 | tf_op jit(solution)/shard_map/pregate/pallas_call | solution.py:136
  18.5 0.0 collective-permute-done.3.refs_0_
  18.5 1.3 %collective-permute-start.4 = (bf16[768,128]{1,0:T(8,128)(2,1)S(1)}, bf16[768,128]{1,0:T(8,128)(2,1)S(1)}, u32[]{:S(2)}, u32[]{:S(2)}) collective-permute-start(bf16[768,128]{1,0:T(8,128)(2,1)S(1)} %collective-permute-done.3.refs_0_), channel_id=1, source_target_pairs={{24,16},{25,17},{26,18},{27,19},{28,20},{29,21},{30,22},{31,23}} | collective-permute-start | bytes 589832 | tf_op jit(solution)/shard_map/ppermute | solution.py:379
  19.9 0.0 collective-permute-done.5.refs_0_
  19.9 9.9 %collective-permute-done.2.rows_in.refs_0_ = bf16[768,128]{1,0:T(8,128)(2,1)S(1)} collective-permute-done((bf16[768,128]{1,0:T(8,128)(2,1)S(1)}, bf16[768,128]{1,0:T(8,128)(2,1)S(1)}, u32[]{:S(2)}, u32[]{:S(2)}) %collective-permute-start.2) | collective-permute-done | bytes 196640 | tf_op jit(solution)/shard_map/ppermute | solution.py:345
  29.9 2.0 %pregate.3 = (f32[768,2048]{1,0:T(8,128)S(1)}, bf16[1,768,512]{2,1,0:T(8,128)(2,1)}) custom-call(bf16[768,128]{1,0:T(8,128)(2,1)S(1)} %collective-permute-done.2.rows_in.refs_0_, bf16[128,512]{1,0:T(8,128)(2,1)S(1)} %get-tuple-element.28.w_conv.refs_1_, f32[1,512]{1,0:T(1,128)S(1)} %get-tuple-element.29.b_conv.refs_2_, ...), custom_call_target="tpu_custom_call", output_to_operand_aliasing={{1}: (5, {})} | custom-call | flops 1610612736 | bytes 6291456 | tf_op jit(solution)/shard_map/pregate/pallas_call | solution.py:136
  31.9 0.0 collective-permute-done.4.refs_0_
  31.9 1.8 %shard_map.102 = (bf16[1,768,512]{2,1,0:T(8,128)(2,1)}, bf16[768,512]{1,0:T(8,128)(2,1)S(1)}, f32[768,512]{1,0:T(8,128)S(1)}) custom-call(bf16[768,128]{1,0:T(8,128)(2,1)S(1)} %collective-permute-done.4.refs_0_, bf16[128,512]{1,0:T(8,128)(2,1)S(1)} %get-tuple-element.28.w_conv.refs_1_, ...), custom_call_target="tpu_custom_call", output_to_operand_aliasing={{0}: (6, {}), {2}: (8, {}), {1}: (7, {})} | custom-call | flops 3221225472 | bytes 3145728 | tf_op jit(solution)/shard_map/pallas_call | solution.py:210
  33.7 5.5 %finish.1 = (bf16[1,768,512]{2,1,0:T(8,128)(2,1)}, f32[768,512]{1,0:T(8,128)S(1)}) custom-call(bf16[768,128]{1,0:T(8,128)(2,1)S(1)} %collective-permute-done.2.rows_in.refs_0_, bf16[128,512]{1,0:T(8,128)(2,1)S(1)} %get-tuple-element.28.w_conv.refs_1_, f32[1,512]{1,0:T(1,128)S(1)} %get-tuple-element.29.b_conv.refs_2_, ...), custom_call_target="tpu_custom_call", output_to_operand_aliasing={{0}: (6, {}), {1}: (9, {})} | custom-call | flops 4831838208 | bytes 3145728 | tf_op jit(solution)/shard_map/finish/pallas_call | solution.py:291
  (2 shorter events, 0.0 us)
Async XLA Ops:
  0.0 9.7 %collective-permute-start.1 = (bf16[768,128]{1,0:T(8,128)(2,1)}, bf16[768,128]{1,0:T(8,128)(2,1)S(1)}, u32[]{:S(2)}, u32[]{:S(2)}) collective-permute-start(bf16[768,128]{1,0:T(8,128)(2,1)} %bitcast.5), channel_id=1, source_target_pairs={{1,0},{2,1},{3,2},{4,3},{5,4},{6,5},{7,6},{9,8},{10,9},{11,10},{12... | collective-permute-start | bytes 589832 | tf_op jit(solution)/shard_map/ppermute | solution.py:329
  2.6 7.1 %collective-permute-start = (bf16[768,128]{1,0:T(8,128)(2,1)}, bf16[768,128]{1,0:T(8,128)(2,1)S(1)}, u32[]{:S(2)}, u32[]{:S(2)}) collective-permute-start(bf16[768,128]{1,0:T(8,128)(2,1)} %bitcast.6), channel_id=1, source_target_pairs={{0,1},{1,2},{2,3},{3,4},{4,5},{5,6},{6,7},{8,9},{9,10},{10,11},{11... | collective-permute-start | bytes 589832 | tf_op jit(solution)/shard_map/ppermute | solution.py:328
  10.7 7.8 %collective-permute-start.3 = (bf16[768,128]{1,0:T(8,128)(2,1)S(1)}, bf16[768,128]{1,0:T(8,128)(2,1)S(1)}, u32[]{:S(2)}, u32[]{:S(2)}) collective-permute-start(bf16[768,128]{1,0:T(8,128)(2,1)S(1)} %aggregate.1.rows_in), channel_id=1, source_target_pairs={{0,24},{1,25},{2,26},{3,27},{4,28},{5,29},{6,30},{7,31}} | collective-permute-start | bytes 589832 | tf_op jit(solution)/shard_map/ppermute | solution.py:345
  11.4 8.5 %collective-permute-start.5 = (bf16[768,128]{1,0:T(8,128)(2,1)S(1)}, bf16[768,128]{1,0:T(8,128)(2,1)S(1)}, u32[]{:S(2)}, u32[]{:S(2)}) collective-permute-start(bf16[768,128]{1,0:T(8,128)(2,1)S(1)} %aggregate.1.rows_in), channel_id=1, source_target_pairs={{8,24},{9,25},{10,26},{11,27},{12,28},{13,29},{14,30},{15,31}} | collective-permute-start | bytes 589832 | tf_op jit(solution)/shard_map/ppermute | solution.py:345
  12.1 17.8 %collective-permute-start.2 = (bf16[768,128]{1,0:T(8,128)(2,1)S(1)}, bf16[768,128]{1,0:T(8,128)(2,1)S(1)}, u32[]{:S(2)}, u32[]{:S(2)}) collective-permute-start(bf16[768,128]{1,0:T(8,128)(2,1)S(1)} %aggregate.1.rows_in), channel_id=1, source_target_pairs={{0,8},{8,16},{16,24},{1,9},{9,17},{17,25},{2,10},{10,18},{18,26},{... | collective-permute-start | bytes 589832 | tf_op jit(solution)/shard_map/ppermute | solution.py:345
  18.5 13.3 %collective-permute-start.4 = (bf16[768,128]{1,0:T(8,128)(2,1)S(1)}, bf16[768,128]{1,0:T(8,128)(2,1)S(1)}, u32[]{:S(2)}, u32[]{:S(2)}) collective-permute-start(bf16[768,128]{1,0:T(8,128)(2,1)S(1)} %collective-permute-done.3.refs_0_), channel_id=1, source_target_pairs={{24,16},{25,17},{26,18},{27,19},{28,20},{29,21},{30,22},{31,23}} | collective-permute-start | bytes 589832 | tf_op jit(solution)/shard_map/ppermute | solution.py:379

commit v5 on v4

--- a/solution.py
+++ b/solution.py
@@ -49,7 +49,7 @@
 
 
 def aggregate_kernel(
-    parts, own, left, right, tiles, src_in, dst_in, count, *refs
+    parts, own, outer, inner, tiles, src_in, dst_in, count, *refs
 ):
     pieces = refs[:parts]
     window, total, src, dst, sems = refs[parts:]
@@ -62,9 +62,19 @@
     slots = tiles.shape[0]
     row_blocks = rows // block
     base = (lax.axis_index("vert") - 1) * row_blocks
-    window[0:rows] = left[...]
     window[rows : 2 * rows] = own[...]
-    window[2 * rows : 3 * rows] = right[...]
+    side = lax.axis_index("vert") % 2
+
+    @pl.when(side == 0)
+    def _():
+        window[0:rows] = outer[...]
+        window[2 * rows : 3 * rows] = inner[...]
+
+    @pl.when(side == 1)
+    def _():
+        window[0:rows] = inner[...]
+        window[2 * rows : 3 * rows] = outer[...]
+
     total[...] = jnp.zeros_like(total)
     for copy in copies:
         copy.wait()
@@ -84,7 +94,7 @@
         piece[...] = total[part * share : (part + 1) * share].astype(BF16)
 
 
-def aggregate(parts, own, left, right, tiles, src, dst, count):
+def aggregate(parts, own, outer, inner, tiles, src, dst, count):
     rows, width = own.shape
     return pl.pallas_call(
         functools.partial(aggregate_kernel, parts),
@@ -99,42 +109,35 @@
         ],
         compiler_params=pltpu.CompilerParams(vmem_limit_bytes=GRANT),
         name="aggregate",
-    )(own, left, right, tiles, src, dst, count)
-
-
-def convolve(rows_in, w_conv, b_conv, conv):
-    reached = jnp.dot(rows_in[...], w_conv[...], preferred_element_type=F32) + b_conv[...]
-    conv[...] = jnp.maximum(reached, 0.0).astype(BF16)
+    )(own, outer, inner, tiles, src, dst, count)
+
+
+def convolve(rows_in, w_conv, b_conv, conv, part=slice(None)):
+    reached = jnp.dot(rows_in[part], w_conv[...], preferred_element_type=F32) + b_conv[...]
+    conv[part] = jnp.maximum(reached, 0.0).astype(BF16)
 
 
 def bias_of(b_gates, gate, part):
     return b_gates[:, part] + (forget_bias if gate == 1 else 0.0)
 
 
-def pregate_kernel(only, rows_in, w_conv, b_conv, w_input, b_gates, *refs):
+def pregate_kernel(rows_in, w_conv, b_conv, w_input, b_gates, *refs):
     pre, _, conv = refs[-3:]
     width = w_input.shape[1] // 4
-
-    def run():
-        convolve(rows_in, w_conv, b_conv, conv)
-        for gate in range(4):
-            part = slice(gate * width, (gate + 1) * width)
-            pre[:, part] = jnp.dot(
-                conv[...], w_input[:, part], preferred_element_type=F32
-            ) + bias_of(b_gates, gate, part)
-
-    if only is None:
-        run()
-    else:
-        pl.when(lax.axis_index("snap") == only)(run)
-
-
-def pregate(only, rows_in, w_conv, b_conv, w_input, b_gates, out):
+    convolve(rows_in, w_conv, b_conv, conv)
+    for gate in range(4):
+        part = slice(gate * width, (gate + 1) * width)
+        pre[:, part] = jnp.dot(
+            conv[...], w_input[:, part], preferred_element_type=F32
+        ) + bias_of(b_gates, gate, part)
+
+
+def pregate(rows_in, w_conv, b_conv, w_input, b_gates, out):
     rows = rows_in.shape[0]
     depth, gates = w_input.shape
     fresh = isinstance(out, tuple)
     return pl.pallas_call(
-        functools.partial(pregate_kernel, only),
+        pregate_kernel,
         out_shape=[
             jax.ShapeDtypeStruct((rows, gates), F32),
             jax.ShapeDtypeStruct(out if fresh else out.shape, BF16),
@@ -227,31 +230,8 @@
     rows_in, w_conv, b_conv, w_input, w_state, b_gates, _, pre = refs[:8]
     out, cell, conv, middle, shown, sems = refs[-6:]
     before = refs[8] if snaps >= 3 else None
-    prepared = refs[10] if snaps > 3 else None
     me = lax.axis_index("snap")
     rows = shown.shape[0]
-    every = slice(None)
-
-    def taken(first, ready):
-        if ready is None:
-            convolve(rows_in, w_conv, b_conv, conv)
-        source = None if first else before
-        gate_step(conv, ready, w_input, w_state, b_gates, source, cell, middle, every)
-
-    if snaps == 3:
-
-        @pl.when(me == 1)
-        def _():
-            middle[...] = before[...]
-
-    if snaps == 2 or snaps > 3:
-        pl.when(me == 1)(functools.partial(taken, True, None))
-    if snaps > 3:
-        pl.when(me == snaps - 2)(functools.partial(taken, False, prepared))
-        pl.when((me > 1) & (me != snaps - 2))(functools.partial(taken, False, None))
-    elif snaps == 3:
-        pl.when(me == 2)(functools.partial(taken, False, None))
-
     blocks = LAST_BLOCKS if rows % (16 * LAST_BLOCKS) == 0 else 1
     share = rows // blocks
 
@@ -263,20 +243,34 @@
             sems.at[block],
         )
 
-    def last(first):
-        source = None if first else middle
-        for block in range(blocks):
-            part = slice(block * share, (block + 1) * share)
-            gate_step(None, pre, w_input, w_state, b_gates, source, cell, shown, part, False)
+    def run(source, begins, carried):
+        def taken(part):
+            convolve(rows_in, w_conv, b_conv, conv, part)
+            gate_step(conv, None, w_input, w_state, b_gates, source, cell, middle, part)
+
+        def last(block, part):
+            gate_step(None, pre, w_input, w_state, b_gates, carried, cell, shown, part, False)
             sent(block).start()
 
-    pl.when(me == 0)(functools.partial(last, True))
-    pl.when(me > 0)(functools.partial(last, False))
+        parts = [slice(block * share, (block + 1) * share) for block in range(blocks)]
+        if begins:
+            taken(parts[0])
+        for block, part in enumerate(parts):
+            if begins and block + 1 < blocks:
+                taken(parts[block + 1])
+            last(block, part)
+
+    pl.when(me == 0)(functools.partial(run, None, False, None))
+    if snaps > 1:
+        middle_now = before if snaps == 3 else middle
+        pl.when(me == 1)(functools.partial(run, None, snaps != 3, middle_now))
+    if snaps > 2:
+        pl.when(me > 1)(functools.partial(run, before, True, middle))
     for block in range(blocks):
         sent(block).wait()
 
 
-def finish(snaps, offset, rows_in, weights, out, pre, state, prepared):
+def finish(snaps, offset, rows_in, weights, out, pre, state):
     rows = rows_in.shape[0]
     depth, gates = weights[2].shape
     width = gates // 4
@@ -286,8 +280,6 @@
     if state is not None:
         aliases[9] = 1
         operands += state
-    if prepared is not None:
-        operands.append(prepared)
     return pl.pallas_call(
         functools.partial(finish_kernel, snaps, offset),
         out_shape=[shape(out.shape, BF16), shape((rows, width), F32)],
@@ -325,17 +317,18 @@
     owners = lax.axis_size("vert")
     snaps = lax.axis_size("snap")
     last = snaps - 1
-    left = lax.ppermute(features[0], "vert", [(i, i + 1) for i in range(owners - 1)])
-    right = lax.ppermute(features[0], "vert", [(i + 1, i) for i in range(owners - 1)])
-    own, tiles, w_conv, b_conv, w_input, w_state, b_gates = load(
-        [features[0], adjacency_tiles[0], w_conv, b_conv[None], w_input, w_state, b_gates[None]]
-    )
+    odd = [(i, i + 1) for i in range(1, owners - 1, 2)]
+    even = [(i, i + 1) for i in range(0, owners - 1, 2)]
+    outer = lax.ppermute(features[0], "vert", odd + [(b, a) for a, b in odd])
+    inner = lax.ppermute(features[0], "vert", even + [(b, a) for a, b in even])
+    own, tiles = load([features[0], adjacency_tiles[0]])
     lists = [
         pltpu.with_memory_space_constraint(array, pltpu.HBM)
         for array in (src_block, dst_block)
     ]
-    halves = aggregate(PARTS, own, left, right, tiles, *lists, block_count)
-    weights = [w_conv, b_conv, w_input, w_state, b_gates]
+    halves = aggregate(PARTS, own, outer, inner, tiles, *lists, block_count)
+    weights = load([w_conv, b_conv[None], w_input, w_state, b_gates[None]])
+    w_conv, b_conv, w_input, w_state, b_gates = weights
     handed = snaps >= 3
 
     def shifted(part, hop):
@@ -349,7 +342,7 @@
     share = own.shape[0] // PARTS
     pre = {}
     for part in range(PARTS):
-        pre[part], out = pregate(None, halves[part], w_conv, b_conv, w_input, b_gates, out)
+        pre[part], out = pregate(halves[part], w_conv, b_conv, w_input, b_gates, out)
     passed_back = {}
     states = {part: None for part in range(PARTS)}
 
@@ -359,14 +352,6 @@
         on_later = None if stage == 1 else hop + 1
         out_now, *state = step(on_first, on_later, arrived[hop, part], weights, out, states[part])
         states[part] = state
-        return out_now
-
-    prepared = {part: None for part in range(PARTS)}
-
-    def prepare(part):
-        prepared[part], out_now = pregate(
-            last - 1, arrived[1, part], w_conv, b_conv, w_input, b_gates, out
-        )
         return out_now
 
     def receive_back(part):
@@ -386,13 +371,12 @@
         for stage in range(2, last):
             out = advance(part, stage)
             if stage == 2:
-                out = prepare(part)
                 out = receive_back(part)
         if snaps == 3:
             out = receive_back(part)
         rows_in = arrived[1, part] if snaps > 1 else halves[part]
         out = finish(
-            snaps, part * share, rows_in, weights, out, pre[part], states[part], prepared[part]
+            snaps, part * share, rows_in, weights, out, pre[part], states[part]
         )
     return out
 

time: 39.6 us -> 38.3 us (0.967)
  starting transfers between devices: 13.5 us -> 10.8 us
  waiting for transfers between devices: 9.96 us -> 11.1 us
  Pallas kernels: 14.9 us -> 15.3 us
    ppermute x3, waiting for transfers between devices: 9.95 us -> 0.01 us  [shifted(): return lax.ppermute(halves[part], 'snap', routes)]
    ppermute x1, waiting for transfers between devices: 0.01 us -> 6.29 us  [shards(): lax.ppermute(arrived[last, part], 'snap', [(last, last - 1)])]
    ppermute x2, waiting for transfers between devices: 0.01 us -> 4.78 us  [the longest x1 4.78 us: shards(): outer = lax.ppermute(features[0], 'vert', odd + [(b, a) for a, b in odd])]
    ppermute x2, starting transfers between devices: 6.45 us -> 3.67 us  [the longest x1 3 us: shards(): outer = lax.ppermute(features[0], 'vert', odd + [(b, a) for a, b in odd])]
    pallas_call x2 -> x1, Pallas kernels: 4 us -> 1.99 us  [pregate(): pl.pallas_call(pregate_kernel, out_shape=[jax.ShapeDtypeStruct((rows, gat...]
    pallas_call x1, Pallas kernels: 5.55 us -> 7.01 us  [finish(): pl.pallas_call(functools.partial(finish_kernel, snaps, offset), out_shape...]
    pallas_call x1 -> x2, Pallas kernels: 2.58 us -> 3.49 us  [load(): pl.pallas_call(functools.partial(load_kernel, len(arrays)), out_shape=[ja...]
  transfers between devices with their start and end apart: 6 -> 6, of which waited for: 1 -> 2; matrix products, arithmetic and copies ran while one was open for 0% -> 0% of each run, Pallas kernels for 17% -> 19%
where the time goes in v5:
time: 38.3 us; the launch traced here: 38 us
  Pallas kernels  15.3 us (40%)
  waiting for transfers between devices  11.1 us (29%)
  starting transfers between devices  10.8 us (28%)
  between operations  0.93 us (2%)
    pallas_call x1, Pallas kernels, finish(): pl.pallas_call(functools.partial(finish_kernel, snaps, offset), out_shape...  7.01 us
    ppermute x1, waiting for transfers between devices, shards(): lax.ppermute(arrived[last, part], 'snap', [(last, last - 1)])  6.29 us
    ppermute x3, starting transfers between devices, shifted(): return lax.ppermute(halves[part], 'snap', routes)  5.79 us
    ppermute x1, waiting for transfers between devices, shards(): outer = lax.ppermute(features[0], 'vert', odd + [(b, a) for a, b in odd])  4.78 us
    pallas_call x2, Pallas kernels, load(): pl.pallas_call(functools.partial(load_kernel, len(arrays)), out_shape=[ja...  3.49 us
    ppermute x1, starting transfers between devices, shards(): outer = lax.ppermute(features[0], 'vert', odd + [(b, a) for a, b in odd])  3 us
    pallas_call x1, Pallas kernels, pregate(): pl.pallas_call(pregate_kernel, out_shape=[jax.ShapeDtypeStruct((rows, gat...  1.99 us
    pallas_call x3, Pallas kernels, step(): pl.pallas_call(functools.partial(step_kernel, on_first, on_later, len(ope...  1.81 us
  transfers between devices with their start and end apart: 6, of which 2 were waited for; matrix products, arithmetic and copies ran while one was open for 0% of the time, Pallas kernels for 19%

profile of v5, /device:TPU:19, one launch (start us, length us, event | category | flops | bytes accessed | tf_op | source)
XLA Modules:
  0.0 38.0 jit_solution(517340251854404706)
XLA Ops:
  0.0 0.7 %collective-permute-start.1 = (bf16[768,128]{1,0:T(8,128)(2,1)}, bf16[768,128]{1,0:T(8,128)(2,1)S(1)}, u32[]{:S(2)}, u32[]{:S(2)}) collective-permute-start(bf16[768,128]{1,0:T(8,128)(2,1)} %bitcast.5), channel_id=1, source_target_pairs={{0,1},{2,3},{4,5},{6,7},{1,0},{3,2},{5,4},{7,6},{8,9},{10,11},{12,... | collective-permute-start | bytes 589832 | tf_op jit(solution)/shard_map/ppermute | solution.py:323
  0.7 3.0 %collective-permute-start = (bf16[768,128]{1,0:T(8,128)(2,1)}, bf16[768,128]{1,0:T(8,128)(2,1)S(1)}, u32[]{:S(2)}, u32[]{:S(2)}) collective-permute-start(bf16[768,128]{1,0:T(8,128)(2,1)} %bitcast.6), channel_id=1, source_target_pairs={{1,2},{3,4},{5,6},{2,1},{4,3},{6,5},{9,10},{11,12},{13,14},{10,9},... | collective-permute-start | bytes 589832 | tf_op jit(solution)/shard_map/ppermute | solution.py:322
  4.3 1.1 %load.2 = (bf16[768,128]{1,0:T(8,128)(2,1)S(1)}, bf16[12,128,128]{2,1,0:T(8,128)(2,1)S(1)}) custom-call(bf16[768,128]{1,0:T(8,128)(2,1)} %bitcast.7, bf16[12,128,128]{2,1,0:T(8,128)(2,1)} %bitcast.4), custom_call_target="tpu_custom_call" | custom-call | bytes 1179648 | tf_op jit(solution)/shard_map/load/pallas_call | solution.py:37
  5.5 0.0 collective-permute-done.1.inner
  5.5 4.8 %collective-permute-done.outer = bf16[768,128]{1,0:T(8,128)(2,1)S(1)} collective-permute-done((bf16[768,128]{1,0:T(8,128)(2,1)}, bf16[768,128]{1,0:T(8,128)(2,1)S(1)}, u32[]{:S(2)}, u32[]{:S(2)}) %collective-permute-start) | collective-permute-done | bytes 196640 | tf_op jit(solution)/shard_map/ppermute | solution.py:322
  10.2 1.0 %aggregate.1.rows_in = bf16[768,128]{1,0:T(8,128)(2,1)S(1)} custom-call(bf16[768,128]{1,0:T(8,128)(2,1)S(1)} %get-tuple-element.24.own, bf16[768,128]{1,0:T(8,128)(2,1)S(1)} %collective-permute-done.outer, bf16[768,128]{1,0:T(8,128)(2,1)S(1)} %collective-permute-done.1.inner, bf16[12,128,128]{2,1,0:T(8,128)(2,1)S(1)} %get-tuple-element.25.tiles, ...), custom_call_target="tpu_custom_call" | custom-call | tf_op jit(solution)/shard_map/aggregate/pallas_call | solution.py:99
  11.2 0.7 %collective-permute-start.3 = (bf16[768,128]{1,0:T(8,128)(2,1)S(1)}, bf16[768,128]{1,0:T(8,128)(2,1)S(1)}, u32[]{:S(2)}, u32[]{:S(2)}) collective-permute-start(bf16[768,128]{1,0:T(8,128)(2,1)S(1)} %aggregate.1.rows_in), channel_id=1, source_target_pairs={{0,24},{1,25},{2,26},{3,27},{4,28},{5,29},{6,30},{7,31}} | collective-permute-start | bytes 589832 | tf_op jit(solution)/shard_map/ppermute | solution.py:338
  11.9 2.4 %load.3 = (bf16[128,512]{1,0:T(8,128)(2,1)S(1)}, f32[1,512]{1,0:T(1,128)S(1)}, bf16[512,2048]{1,0:T(8,128)(2,1)S(1)}, bf16[512,2048]{1,0:T(8,128)(2,1)S(1)}, f32[1,2048]{1,0:T(1,128)S(1)}) custom-call(bf16[128,512]{1,0:T(8,128)(2,1)} %refs_0_.1, f32[1,512]{1,0:T(1,128)} %bitcast.9, bf16[512,2048]{1,0:T(8,128)(2,1)} %refs_2_.1, bf16[512,2048]{1,0:T(8,128)(2,1)} %refs_3_.1, ...), custom_call_target="tpu_custom_call" | custom-call | bytes 8671232 | tf_op jit(solution)/shard_map/load/pallas_call | solution.py:37
  14.3 0.7 %collective-permute-start.5 = (bf16[768,128]{1,0:T(8,128)(2,1)S(1)}, bf16[768,128]{1,0:T(8,128)(2,1)S(1)}, u32[]{:S(2)}, u32[]{:S(2)}) collective-permute-start(bf16[768,128]{1,0:T(8,128)(2,1)S(1)} %aggregate.1.rows_in), channel_id=1, source_target_pairs={{8,24},{9,25},{10,26},{11,27},{12,28},{13,29},{14,30},{15,31}} | collective-permute-start | bytes 589832 | tf_op jit(solution)/shard_map/ppermute | solution.py:338
  15.0 4.4 %collective-permute-start.2 = (bf16[768,128]{1,0:T(8,128)(2,1)S(1)}, bf16[768,128]{1,0:T(8,128)(2,1)S(1)}, u32[]{:S(2)}, u32[]{:S(2)}) collective-permute-start(bf16[768,128]{1,0:T(8,128)(2,1)S(1)} %aggregate.1.rows_in), channel_id=1, source_target_pairs={{0,8},{8,16},{16,24},{1,9},{9,17},{17,25},{2,10},{10,18},{18,26},{... | collective-permute-start | bytes 589832 | tf_op jit(solution)/shard_map/ppermute | solution.py:338
  19.4 2.0 %pregate.1 = (f32[768,2048]{1,0:T(8,128)S(1)}, bf16[1,768,512]{2,1,0:T(8,128)(2,1)}) custom-call(bf16[768,128]{1,0:T(8,128)(2,1)S(1)} %aggregate.1.rows_in, bf16[128,512]{1,0:T(8,128)(2,1)S(1)} %get-tuple-element.26.w_conv.refs_1_, f32[1,512]{1,0:T(1,128)S(1)} %get-tuple-element.27.b_conv.refs_2_, bf16[512,2048]{1,0:T(8,128)(2,1)S(1)} %get-tuple-element.28.w_input.refs_3_, ...), custom_call_target="tpu_custom_call" | custom-call | flops 1610612736 | bytes 6291456 | tf_op jit(solution)/shard_map/pregate/pallas_call | solution.py:139
  21.4 0.0 collective-permute-done.3.refs_0_
  21.4 1.3 %collective-permute-start.4 = (bf16[768,128]{1,0:T(8,128)(2,1)S(1)}, bf16[768,128]{1,0:T(8,128)(2,1)S(1)}, u32[]{:S(2)}, u32[]{:S(2)}) collective-permute-start(bf16[768,128]{1,0:T(8,128)(2,1)S(1)} %collective-permute-done.3.refs_0_), channel_id=1, source_target_pairs={{24,16},{25,17},{26,18},{27,19},{28,20},{29,21},{30,22},{31,23}} | collective-permute-start | bytes 589832 | tf_op jit(solution)/shard_map/ppermute | solution.py:364
  22.8 0.0 collective-permute-done.5.refs_0_
  22.8 6.3 %collective-permute-done.4.refs_0_ = bf16[768,128]{1,0:T(8,128)(2,1)S(1)} collective-permute-done((bf16[768,128]{1,0:T(8,128)(2,1)S(1)}, bf16[768,128]{1,0:T(8,128)(2,1)S(1)}, u32[]{:S(2)}, u32[]{:S(2)}) %collective-permute-start.4) | collective-permute-done | bytes 196640 | tf_op jit(solution)/shard_map/ppermute | solution.py:364
  29.1 1.8 %shard_map.102 = (bf16[1,768,512]{2,1,0:T(8,128)(2,1)}, bf16[768,512]{1,0:T(8,128)(2,1)S(1)}, f32[768,512]{1,0:T(8,128)S(1)}) custom-call(bf16[768,128]{1,0:T(8,128)(2,1)S(1)} %collective-permute-done.4.refs_0_, bf16[128,512]{1,0:T(8,128)(2,1)S(1)} %get-tuple-element.26.w_conv.refs_1_, ...), custom_call_target="tpu_custom_call", output_to_operand_aliasing={{0}: (6, {}), {2}: (8, {}), {1}: (7, {})} | custom-call | flops 3221225472 | bytes 3145728 | tf_op jit(solution)/shard_map/pallas_call | solution.py:213
  30.9 0.0 collective-permute-done.2.refs_0_
  30.9 7.0 %finish.1 = (bf16[1,768,512]{2,1,0:T(8,128)(2,1)}, f32[768,512]{1,0:T(8,128)S(1)}) custom-call(bf16[768,128]{1,0:T(8,128)(2,1)S(1)} %collective-permute-done.2.refs_0_, bf16[128,512]{1,0:T(8,128)(2,1)S(1)} %get-tuple-element.26.w_conv.refs_1_, f32[1,512]{1,0:T(1,128)S(1)} %get-tuple-element.27.b_conv.refs_2_, ...), custom_call_target="tpu_custom_call", output_to_operand_aliasing={{0}: (6, {}), {1}: (9, {})} | custom-call | flops 4831838208 | bytes 3145728 | tf_op jit(solution)/shard_map/finish/pallas_call | solution.py:283
  (2 shorter events, 0.0 us)
Async XLA Ops:
  0.0 5.5 %collective-permute-start.1 = (bf16[768,128]{1,0:T(8,128)(2,1)}, bf16[768,128]{1,0:T(8,128)(2,1)S(1)}, u32[]{:S(2)}, u32[]{:S(2)}) collective-permute-start(bf16[768,128]{1,0:T(8,128)(2,1)} %bitcast.5), channel_id=1, source_target_pairs={{0,1},{2,3},{4,5},{6,7},{1,0},{3,2},{5,4},{7,6},{8,9},{10,11},{12,... | collective-permute-start | bytes 589832 | tf_op jit(solution)/shard_map/ppermute | solution.py:323
  0.7 9.6 %collective-permute-start = (bf16[768,128]{1,0:T(8,128)(2,1)}, bf16[768,128]{1,0:T(8,128)(2,1)S(1)}, u32[]{:S(2)}, u32[]{:S(2)}) collective-permute-start(bf16[768,128]{1,0:T(8,128)(2,1)} %bitcast.6), channel_id=1, source_target_pairs={{1,2},{3,4},{5,6},{2,1},{4,3},{6,5},{9,10},{11,12},{13,14},{10,9},... | collective-permute-start | bytes 589832 | tf_op jit(solution)/shard_map/ppermute | solution.py:322
  11.2 10.2 %collective-permute-start.3 = (bf16[768,128]{1,0:T(8,128)(2,1)S(1)}, bf16[768,128]{1,0:T(8,128)(2,1)S(1)}, u32[]{:S(2)}, u32[]{:S(2)}) collective-permute-start(bf16[768,128]{1,0:T(8,128)(2,1)S(1)} %aggregate.1.rows_in), channel_id=1, source_target_pairs={{0,24},{1,25},{2,26},{3,27},{4,28},{5,29},{6,30},{7,31}} | collective-permute-start | bytes 589832 | tf_op jit(solution)/shard_map/ppermute | solution.py:338
  14.3 8.5 %collective-permute-start.5 = (bf16[768,128]{1,0:T(8,128)(2,1)S(1)}, bf16[768,128]{1,0:T(8,128)(2,1)S(1)}, u32[]{:S(2)}, u32[]{:S(2)}) collective-permute-start(bf16[768,128]{1,0:T(8,128)(2,1)S(1)} %aggregate.1.rows_in), channel_id=1, source_target_pairs={{8,24},{9,25},{10,26},{11,27},{12,28},{13,29},{14,30},{15,31}} | collective-permute-start | bytes 589832 | tf_op jit(solution)/shard_map/ppermute | solution.py:338
  15.0 15.9 %collective-permute-start.2 = (bf16[768,128]{1,0:T(8,128)(2,1)S(1)}, bf16[768,128]{1,0:T(8,128)(2,1)S(1)}, u32[]{:S(2)}, u32[]{:S(2)}) collective-permute-start(bf16[768,128]{1,0:T(8,128)(2,1)S(1)} %aggregate.1.rows_in), channel_id=1, source_target_pairs={{0,8},{8,16},{16,24},{1,9},{9,17},{17,25},{2,10},{10,18},{18,26},{... | collective-permute-start | bytes 589832 | tf_op jit(solution)/shard_map/ppermute | solution.py:338
  21.4 7.7 %collective-permute-start.4 = (bf16[768,128]{1,0:T(8,128)(2,1)S(1)}, bf16[768,128]{1,0:T(8,128)(2,1)S(1)}, u32[]{:S(2)}, u32[]{:S(2)}) collective-permute-start(bf16[768,128]{1,0:T(8,128)(2,1)S(1)} %collective-permute-done.3.refs_0_), channel_id=1, source_target_pairs={{24,16},{25,17},{26,18},{27,19},{28,20},{29,21},{30,22},{31,23}} | collective-permute-start | bytes 589832 | tf_op jit(solution)/shard_map/ppermute | solution.py:364

commit v6 on v5

--- a/solution.py
+++ b/solution.py
@@ -321,14 +321,15 @@
     even = [(i, i + 1) for i in range(0, owners - 1, 2)]
     outer = lax.ppermute(features[0], "vert", odd + [(b, a) for a, b in odd])
     inner = lax.ppermute(features[0], "vert", even + [(b, a) for a, b in even])
-    own, tiles = load([features[0], adjacency_tiles[0]])
+    own, tiles, *weights = load(
+        [features[0], adjacency_tiles[0], w_conv, b_conv[None], w_input, w_state, b_gates[None]]
+    )
+    w_conv, b_conv, w_input, w_state, b_gates = weights
     lists = [
         pltpu.with_memory_space_constraint(array, pltpu.HBM)
         for array in (src_block, dst_block)
     ]
     halves = aggregate(PARTS, own, outer, inner, tiles, *lists, block_count)
-    weights = load([w_conv, b_conv[None], w_input, w_state, b_gates[None]])
-    w_conv, b_conv, w_input, w_state, b_gates = weights
     handed = snaps >= 3
 
     def shifted(part, hop):

time: 38.3 us -> 37.5 us (0.979)
  the two profiles are of different devices: /device:TPU:19 before, /device:TPU:20 now
where the time goes in v6:
time: 37.5 us; the launch traced here: 37.3 us
  Pallas kernels  14.4 us (38%)
  waiting for transfers between devices  11.2 us (30%)
  starting transfers between devices  10.8 us (29%)
  between operations  0.92 us (2%)
    ppermute x1, waiting for transfers between devices, shards(): lax.ppermute(arrived[last, part], 'snap', [(last, last - 1)])  7.94 us
    pallas_call x1, Pallas kernels, finish(): pl.pallas_call(functools.partial(finish_kernel, snaps, offset), out_shape...  7.02 us
    ppermute x3, starting transfers between devices, shifted(): return lax.ppermute(halves[part], 'snap', routes)  6.07 us
    ppermute x1, starting transfers between devices, shards(): outer = lax.ppermute(features[0], 'vert', odd + [(b, a) for a, b in odd])  3.44 us
    ppermute x1, waiting for transfers between devices, shards(): outer = lax.ppermute(features[0], 'vert', odd + [(b, a) for a, b in odd])  3.23 us
    pallas_call x1, Pallas kernels, load(): pl.pallas_call(functools.partial(load_kernel, len(arrays)), out_shape=[ja...  2.58 us
    pallas_call x1, Pallas kernels, pregate(): pl.pallas_call(pregate_kernel, out_shape=[jax.ShapeDtypeStruct((rows, gat...  1.99 us
    pallas_call x3, Pallas kernels, step(): pl.pallas_call(functools.partial(step_kernel, on_first, on_later, len(ope...  1.82 us
  transfers between devices with their start and end apart: 6, of which 2 were waited for; matrix products, arithmetic and copies ran while one was open for 0% of the time, Pallas kernels for 17%

profile of v6, /device:TPU:20, one launch (start us, length us, event | category | flops | bytes accessed | tf_op | source)
XLA Modules:
  0.0 37.3 jit_solution(7766544106146726546)
XLA Ops:
  0.0 0.0 collective-permute-start.1
  0.0 3.4 %collective-permute-start = (bf16[768,128]{1,0:T(8,128)(2,1)}, bf16[768,128]{1,0:T(8,128)(2,1)S(1)}, u32[]{:S(2)}, u32[]{:S(2)}) collective-permute-start(bf16[768,128]{1,0:T(8,128)(2,1)} %bitcast.6), channel_id=1, source_target_pairs={{1,2},{3,4},{5,6},{2,1},{4,3},{6,5},{9,10},{11,12},{13,14},{10,9},... | collective-permute-start | bytes 589832 | tf_op jit(solution)/shard_map/ppermute | solution.py:322
  4.1 2.6 %load.1 = (bf16[768,128]{1,0:T(8,128)(2,1)S(1)}, bf16[12,128,128]{2,1,0:T(8,128)(2,1)S(1)}, bf16[128,512]{1,0:T(8,128)(2,1)S(1)}, f32[1,512]{1,0:T(1,128)S(1)}, ...) custom-call(bf16[768,128]{1,0:T(8,128)(2,1)} %bitcast.7, ...), custom_call_target="tpu_custom_call" | custom-call | bytes 9850880 | tf_op jit(solution)/shard_map/load/pallas_call | solution.py:37
  6.7 0.0 collective-permute-done.1.inner
  6.7 3.2 %collective-permute-done.outer = bf16[768,128]{1,0:T(8,128)(2,1)S(1)} collective-permute-done((bf16[768,128]{1,0:T(8,128)(2,1)}, bf16[768,128]{1,0:T(8,128)(2,1)S(1)}, u32[]{:S(2)}, u32[]{:S(2)}) %collective-permute-start) | collective-permute-done | bytes 196640 | tf_op jit(solution)/shard_map/ppermute | solution.py:322
  9.9 1.0 %aggregate.1.rows_in = bf16[768,128]{1,0:T(8,128)(2,1)S(1)} custom-call(bf16[768,128]{1,0:T(8,128)(2,1)S(1)} %get-tuple-element.24.own, bf16[768,128]{1,0:T(8,128)(2,1)S(1)} %collective-permute-done.outer, bf16[768,128]{1,0:T(8,128)(2,1)S(1)} %collective-permute-done.1.inner, bf16[12,128,128]{2,1,0:T(8,128)(2,1)S(1)} %get-tuple-element.25.tiles, ...), custom_call_target="tpu_custom_call" | custom-call | tf_op jit(solution)/shard_map/aggregate/pallas_call | solution.py:99
  10.9 0.7 %collective-permute-start.3 = (bf16[768,128]{1,0:T(8,128)(2,1)S(1)}, bf16[768,128]{1,0:T(8,128)(2,1)S(1)}, u32[]{:S(2)}, u32[]{:S(2)}) collective-permute-start(bf16[768,128]{1,0:T(8,128)(2,1)S(1)} %aggregate.1.rows_in), channel_id=1, source_target_pairs={{0,24},{1,25},{2,26},{3,27},{4,28},{5,29},{6,30},{7,31}} | collective-permute-start | bytes 589832 | tf_op jit(solution)/shard_map/ppermute | solution.py:339
  11.6 0.7 %collective-permute-start.5 = (bf16[768,128]{1,0:T(8,128)(2,1)S(1)}, bf16[768,128]{1,0:T(8,128)(2,1)S(1)}, u32[]{:S(2)}, u32[]{:S(2)}) collective-permute-start(bf16[768,128]{1,0:T(8,128)(2,1)S(1)} %aggregate.1.rows_in), channel_id=1, source_target_pairs={{8,24},{9,25},{10,26},{11,27},{12,28},{13,29},{14,30},{15,31}} | collective-permute-start | bytes 589832 | tf_op jit(solution)/shard_map/ppermute | solution.py:339
  12.3 4.7 %collective-permute-start.2 = (bf16[768,128]{1,0:T(8,128)(2,1)S(1)}, bf16[768,128]{1,0:T(8,128)(2,1)S(1)}, u32[]{:S(2)}, u32[]{:S(2)}) collective-permute-start(bf16[768,128]{1,0:T(8,128)(2,1)S(1)} %aggregate.1.rows_in), channel_id=1, source_target_pairs={{0,8},{8,16},{16,24},{1,9},{9,17},{17,25},{2,10},{10,18},{18,26},{... | collective-permute-start | bytes 589832 | tf_op jit(solution)/shard_map/ppermute | solution.py:339
  17.0 2.0 %pregate.1 = (f32[768,2048]{1,0:T(8,128)S(1)}, bf16[1,768,512]{2,1,0:T(8,128)(2,1)}) custom-call(bf16[768,128]{1,0:T(8,128)(2,1)S(1)} %aggregate.1.rows_in, bf16[128,512]{1,0:T(8,128)(2,1)S(1)} %get-tuple-element.26.w_conv.refs_1_, f32[1,512]{1,0:T(1,128)S(1)} %get-tuple-element.27.b_conv.refs_2_, bf16[512,2048]{1,0:T(8,128)(2,1)S(1)} %get-tuple-element.28.w_input.refs_3_, ...), custom_call_target="tpu_custom_call" | custom-call | flops 1610612736 | bytes 6291456 | tf_op jit(solution)/shard_map/pregate/pallas_call | solution.py:139
  19.0 0.0 collective-permute-done.3.refs_0_
  19.0 1.3 %collective-permute-start.4 = (bf16[768,128]{1,0:T(8,128)(2,1)S(1)}, bf16[768,128]{1,0:T(8,128)(2,1)S(1)}, u32[]{:S(2)}, u32[]{:S(2)}) collective-permute-start(bf16[768,128]{1,0:T(8,128)(2,1)S(1)} %collective-permute-done.3.refs_0_), channel_id=1, source_target_pairs={{24,16},{25,17},{26,18},{27,19},{28,20},{29,21},{30,22},{31,23}} | collective-permute-start | bytes 589832 | tf_op jit(solution)/shard_map/ppermute | solution.py:365
  20.4 0.0 collective-permute-done.5.refs_0_
  20.4 7.9 %collective-permute-done.4.refs_0_ = bf16[768,128]{1,0:T(8,128)(2,1)S(1)} collective-permute-done((bf16[768,128]{1,0:T(8,128)(2,1)S(1)}, bf16[768,128]{1,0:T(8,128)(2,1)S(1)}, u32[]{:S(2)}, u32[]{:S(2)}) %collective-permute-start.4) | collective-permute-done | bytes 196640 | tf_op jit(solution)/shard_map/ppermute | solution.py:365
  28.3 1.8 %shard_map.102 = (bf16[1,768,512]{2,1,0:T(8,128)(2,1)}, bf16[768,512]{1,0:T(8,128)(2,1)S(1)}, f32[768,512]{1,0:T(8,128)S(1)}) custom-call(bf16[768,128]{1,0:T(8,128)(2,1)S(1)} %collective-permute-done.4.refs_0_, bf16[128,512]{1,0:T(8,128)(2,1)S(1)} %get-tuple-element.26.w_conv.refs_1_, ...), custom_call_target="tpu_custom_call", output_to_operand_aliasing={{0}: (6, {}), {2}: (8, {}), {1}: (7, {})} | custom-call | flops 3221225472 | bytes 3145728 | tf_op jit(solution)/shard_map/pallas_call | solution.py:213
  30.1 0.0 collective-permute-done.2.refs_0_
  30.1 7.0 %finish.1 = (bf16[1,768,512]{2,1,0:T(8,128)(2,1)}, f32[768,512]{1,0:T(8,128)S(1)}) custom-call(bf16[768,128]{1,0:T(8,128)(2,1)S(1)} %collective-permute-done.2.refs_0_, bf16[128,512]{1,0:T(8,128)(2,1)S(1)} %get-tuple-element.26.w_conv.refs_1_, f32[1,512]{1,0:T(1,128)S(1)} %get-tuple-element.27.b_conv.refs_2_, ...), custom_call_target="tpu_custom_call", output_to_operand_aliasing={{0}: (6, {}), {1}: (9, {})} | custom-call | flops 4831838208 | bytes 3145728 | tf_op jit(solution)/shard_map/finish/pallas_call | solution.py:283
  (2 shorter events, 0.0 us)
Async XLA Ops:
  0.0 6.7 %collective-permute-start.1 = (bf16[768,128]{1,0:T(8,128)(2,1)}, bf16[768,128]{1,0:T(8,128)(2,1)S(1)}, u32[]{:S(2)}, u32[]{:S(2)}) collective-permute-start(bf16[768,128]{1,0:T(8,128)(2,1)} %bitcast.5), channel_id=1, source_target_pairs={{0,1},{2,3},{4,5},{6,7},{1,0},{3,2},{5,4},{7,6},{8,9},{10,11},{12,... | collective-permute-start | bytes 589832 | tf_op jit(solution)/shard_map/ppermute | solution.py:323
  0.0 9.9 %collective-permute-start = (bf16[768,128]{1,0:T(8,128)(2,1)}, bf16[768,128]{1,0:T(8,128)(2,1)S(1)}, u32[]{:S(2)}, u32[]{:S(2)}) collective-permute-start(bf16[768,128]{1,0:T(8,128)(2,1)} %bitcast.6), channel_id=1, source_target_pairs={{1,2},{3,4},{5,6},{2,1},{4,3},{6,5},{9,10},{11,12},{13,14},{10,9},... | collective-permute-start | bytes 589832 | tf_op jit(solution)/shard_map/ppermute | solution.py:322
  10.9 8.1 %collective-permute-start.3 = (bf16[768,128]{1,0:T(8,128)(2,1)S(1)}, bf16[768,128]{1,0:T(8,128)(2,1)S(1)}, u32[]{:S(2)}, u32[]{:S(2)}) collective-permute-start(bf16[768,128]{1,0:T(8,128)(2,1)S(1)} %aggregate.1.rows_in), channel_id=1, source_target_pairs={{0,24},{1,25},{2,26},{3,27},{4,28},{5,29},{6,30},{7,31}} | collective-permute-start | bytes 589832 | tf_op jit(solution)/shard_map/ppermute | solution.py:339
  11.6 8.8 %collective-permute-start.5 = (bf16[768,128]{1,0:T(8,128)(2,1)S(1)}, bf16[768,128]{1,0:T(8,128)(2,1)S(1)}, u32[]{:S(2)}, u32[]{:S(2)}) collective-permute-start(bf16[768,128]{1,0:T(8,128)(2,1)S(1)} %aggregate.1.rows_in), channel_id=1, source_target_pairs={{8,24},{9,25},{10,26},{11,27},{12,28},{13,29},{14,30},{15,31}} | collective-permute-start | bytes 589832 | tf_op jit(solution)/shard_map/ppermute | solution.py:339
  12.3 17.8 %collective-permute-start.2 = (bf16[768,128]{1,0:T(8,128)(2,1)S(1)}, bf16[768,128]{1,0:T(8,128)(2,1)S(1)}, u32[]{:S(2)}, u32[]{:S(2)}) collective-permute-start(bf16[768,128]{1,0:T(8,128)(2,1)S(1)} %aggregate.1.rows_in), channel_id=1, source_target_pairs={{0,8},{8,16},{16,24},{1,9},{9,17},{17,25},{2,10},{10,18},{18,26},{... | collective-permute-start | bytes 589832 | tf_op jit(solution)/shard_map/ppermute | solution.py:339
  19.0 9.3 %collective-permute-start.4 = (bf16[768,128]{1,0:T(8,128)(2,1)S(1)}, bf16[768,128]{1,0:T(8,128)(2,1)S(1)}, u32[]{:S(2)}, u32[]{:S(2)}) collective-permute-start(bf16[768,128]{1,0:T(8,128)(2,1)S(1)} %collective-permute-done.3.refs_0_), channel_id=1, source_target_pairs={{24,16},{25,17},{26,18},{27,19},{28,20},{29,21},{30,22},{31,23}} | collective-permute-start | bytes 589832 | tf_op jit(solution)/shard_map/ppermute | solution.py:365

commit v7 on v6

--- a/solution.py
+++ b/solution.py
@@ -14,6 +14,7 @@
 VMEM = pl.BlockSpec(memory_space=pltpu.VMEM)
 SMEM = pl.BlockSpec(memory_space=pltpu.SMEM)
 HBM = pl.BlockSpec(memory_space=pltpu.HBM)
+LIST = HBM
 GRANT = 24 << 20
 PARTS = 1
 LAST_BLOCKS = 4
@@ -48,59 +49,69 @@
     )(*(pltpu.with_memory_space_constraint(array, pltpu.HBM) for array in arrays))
 
 
-def aggregate_kernel(
-    parts, own, outer, inner, tiles, src_in, dst_in, count, *refs
-):
-    pieces = refs[:parts]
-    window, total, src, dst, sems = refs[parts:]
-    lists = ((src_in, src), (dst_in, dst))
-    copies = [pltpu.make_async_copy(a, b, sems.at[i]) for i, (a, b) in enumerate(lists)]
-    for copy in copies:
-        copy.start()
+def aggregate_kernel(early, own, outer, inner, tiles, src_in, dst_in, count, *refs):
+    whole, window, total, src, dst, sems = refs[-6:]
     rows = own.shape[0]
     block = tiles.shape[1]
     slots = tiles.shape[0]
     row_blocks = rows // block
-    base = (lax.axis_index("vert") - 1) * row_blocks
-    window[rows : 2 * rows] = own[...]
-    side = lax.axis_index("vert") % 2
-
-    @pl.when(side == 0)
-    def _():
-        window[0:rows] = outer[...]
-        window[2 * rows : 3 * rows] = inner[...]
-
-    @pl.when(side == 1)
-    def _():
-        window[0:rows] = inner[...]
-        window[2 * rows : 3 * rows] = outer[...]
-
-    total[...] = jnp.zeros_like(total)
-    for copy in copies:
-        copy.wait()
-    products = []
-    for slot in range(slots):
-        column = jnp.clip(src[0, slot] - base, 0, 3 * row_blocks - 1)
-        start = pl.multiple_of(column * block, block)
-        products.append(
-            jnp.dot(tiles[slot], window[pl.ds(start, block)], preferred_element_type=F32)
-        )
-    for slot in range(slots):
-        start = pl.multiple_of(jnp.clip(dst[0, slot], 0, row_blocks - 1) * block, block)
-        alive = slot < count[0, 0]
-        total[pl.ds(start, block)] += jnp.where(alive, products[slot], 0.0)
-    share = rows // parts
-    for part, piece in enumerate(pieces):
-        piece[...] = total[part * share : (part + 1) * share].astype(BF16)
-
-
-def aggregate(parts, own, outer, inner, tiles, src, dst, count):
+    owner = lax.axis_index("vert")
+    base = (owner - 1) * row_blocks
+    sender = lax.axis_index("snap") < max(1, lax.axis_size("snap") - 2)
+
+    def run():
+        lists = ((src_in, src), (dst_in, dst))
+        copies = [pltpu.make_async_copy(a, b, sems.at[i]) for i, (a, b) in enumerate(lists)]
+        for copy in copies:
+            copy.start()
+        window[rows : 2 * rows] = own[...]
+
+        @pl.when(owner % 2 == 0)
+        def _():
+            window[0:rows] = outer[...]
+            window[2 * rows : 3 * rows] = inner[...]
+
+        @pl.when(owner % 2 == 1)
+        def _():
+            window[0:rows] = inner[...]
+            window[2 * rows : 3 * rows] = outer[...]
+
+        total[...] = jnp.zeros_like(total)
+        for copy in copies:
+            copy.wait()
+        products = []
+        for slot in range(slots):
+            column = jnp.clip(src[0, slot] - base, 0, 3 * row_blocks - 1)
+            start = pl.multiple_of(column * block, block)
+            products.append(
+                jnp.dot(tiles[slot], window[pl.ds(start, block)], preferred_element_type=F32)
+            )
+        for slot in range(slots):
+            start = pl.multiple_of(jnp.clip(dst[0, slot], 0, row_blocks - 1) * block, block)
+            alive = slot < count[0, 0]
+            total[pl.ds(start, block)] += jnp.where(alive, products[slot], 0.0)
+        whole[...] = total[...].astype(BF16)
+
+    if early:
+        pl.when(sender)(run)
+    else:
+        pl.when(jnp.logical_not(sender))(run)
+
+        @pl.when(sender)
+        def _():
+            whole[...] = refs[0][...]
+
+
+def aggregate(ready, own, outer, inner, tiles, src, dst, count):
     rows, width = own.shape
+    operands = [own, outer, inner, tiles, src, dst, count]
+    if ready is not None:
+        operands.append(ready)
     return pl.pallas_call(
-        functools.partial(aggregate_kernel, parts),
-        out_shape=[jax.ShapeDtypeStruct((rows // parts, width), BF16)] * parts,
-        in_specs=[VMEM] * 4 + [HBM] * 2 + [SMEM],
-        out_specs=[VMEM] * parts,
+        functools.partial(aggregate_kernel, ready is None),
+        out_shape=jax.ShapeDtypeStruct((rows, width), BF16),
+        in_specs=[VMEM] * 4 + [LIST] * 2 + [SMEM] + [VMEM] * (len(operands) - 7),
+        out_specs=VMEM,
         scratch_shapes=[
             pltpu.VMEM((3 * rows, width), BF16),
             pltpu.VMEM((rows, width), F32),
@@ -109,7 +120,7 @@
         ],
         compiler_params=pltpu.CompilerParams(vmem_limit_bytes=GRANT),
         name="aggregate",
-    )(own, outer, inner, tiles, src, dst, count)
+    )(*operands)
 
 
 def convolve(rows_in, w_conv, b_conv, conv, part=slice(None)):
@@ -329,16 +340,24 @@
         pltpu.with_memory_space_constraint(array, pltpu.HBM)
         for array in (src_block, dst_block)
     ]
-    halves = aggregate(PARTS, own, outer, inner, tiles, *lists, block_count)
+    ready = aggregate(None, own, outer, inner, tiles, *lists, block_count)
     handed = snaps >= 3
 
-    def shifted(part, hop):
+    def shifted(hop):
         routes = [(i, i + hop) for i in range(snaps - hop)]
         if handed and hop == last - 1:
             routes = routes[1:]
-        return lax.ppermute(halves[part], "snap", routes)
-
-    arrived = {(hop, part): shifted(part, hop) for hop, part in sends(snaps)}
+        return lax.ppermute(ready if hop > 1 else whole, "snap", routes)
+
+    arrived = {}
+    for hop, part in sends(snaps):
+        if hop > 1:
+            arrived[hop, part] = shifted(hop)
+    whole = aggregate(ready, own, outer, inner, tiles, *lists, block_count)
+    halves = [whole]
+    for hop, part in sends(snaps):
+        if (hop, part) not in arrived:
+            arrived[hop, part] = shifted(hop)
     out = (1, own.shape[0], w_state.shape[0])
     share = own.shape[0] // PARTS
     pre = {}

time: 37.5 us -> 36.5 us (0.973)
  waiting for transfers between devices: 11.2 us -> 10.1 us
    ppermute x1, waiting for transfers between devices: 7.94 us -> 6.87 us  [shards(): lax.ppermute(arrived[last, part], 'snap', [(last, last - 1)])]
    pallas_call x1 -> x2, Pallas kernels: 0.99 us -> 1.02 us  [aggregate(): pl.pallas_call(functools.partial(aggregate_kernel, ready is None), out_sh...]
  transfers between devices with their start and end apart: 6 -> 6, of which waited for: 2 -> 2; matrix products, arithmetic and copies ran while one was open for 0% -> 0% of each run, Pallas kernels for 17% -> 20%
where the time goes in v7:
time: 36.5 us; the launch traced here: 36.3 us
  Pallas kernels  14.5 us (40%)
  starting transfers between devices  10.8 us (30%)
  waiting for transfers between devices  10.1 us (28%)
  between operations  0.93 us (3%)
    pallas_call x1, Pallas kernels, finish(): pl.pallas_call(functools.partial(finish_kernel, snaps, offset), out_shape...  7.07 us
    ppermute x1, waiting for transfers between devices, shards(): lax.ppermute(arrived[last, part], 'snap', [(last, last - 1)])  6.87 us
    ppermute x3, starting transfers between devices, shifted(): return lax.ppermute(ready if hop > 1 else whole, 'snap', routes)  6.07 us
    ppermute x1, starting transfers between devices, shards(): outer = lax.ppermute(features[0], 'vert', odd + [(b, a) for a, b in odd])  3.44 us
    ppermute x1, waiting for transfers between devices, shards(): outer = lax.ppermute(features[0], 'vert', odd + [(b, a) for a, b in odd])  3.23 us
    pallas_call x1, Pallas kernels, load(): pl.pallas_call(functools.partial(load_kernel, len(arrays)), out_shape=[ja...  2.58 us
    pallas_call x1, Pallas kernels, pregate(): pl.pallas_call(pregate_kernel, out_shape=[jax.ShapeDtypeStruct((rows, gat...  1.99 us
    pallas_call x3, Pallas kernels, step(): pl.pallas_call(functools.partial(step_kernel, on_first, on_later, len(ope...  1.81 us
  transfers between devices with their start and end apart: 6, of which 2 were waited for; matrix products, arithmetic and copies ran while one was open for 0% of the time, Pallas kernels for 20%

profile of v7, /device:TPU:20, one launch (start us, length us, event | category | flops | bytes accessed | tf_op | source)
XLA Modules:
  0.0 36.3 jit_solution(7348751255433863650)
XLA Ops:
  0.0 0.0 collective-permute-start.1
  0.0 3.4 %collective-permute-start = (bf16[768,128]{1,0:T(8,128)(2,1)}, bf16[768,128]{1,0:T(8,128)(2,1)S(1)}, u32[]{:S(2)}, u32[]{:S(2)}) collective-permute-start(bf16[768,128]{1,0:T(8,128)(2,1)} %bitcast.6), channel_id=1, source_target_pairs={{1,2},{3,4},{5,6},{2,1},{4,3},{6,5},{9,10},{11,12},{13,14},{10,9},... | collective-permute-start | bytes 589832 | tf_op jit(solution)/shard_map/ppermute | solution.py:333
  4.1 2.6 %load.1 = (bf16[768,128]{1,0:T(8,128)(2,1)S(1)}, bf16[12,128,128]{2,1,0:T(8,128)(2,1)S(1)}, bf16[128,512]{1,0:T(8,128)(2,1)S(1)}, f32[1,512]{1,0:T(1,128)S(1)}, ...) custom-call(bf16[768,128]{1,0:T(8,128)(2,1)} %bitcast.7, ...), custom_call_target="tpu_custom_call" | custom-call | bytes 9850880 | tf_op jit(solution)/shard_map/load/pallas_call | solution.py:38
  6.7 0.0 collective-permute-done.1.inner
  6.7 3.2 %collective-permute-done.outer = bf16[768,128]{1,0:T(8,128)(2,1)S(1)} collective-permute-done((bf16[768,128]{1,0:T(8,128)(2,1)}, bf16[768,128]{1,0:T(8,128)(2,1)S(1)}, u32[]{:S(2)}, u32[]{:S(2)}) %collective-permute-start) | collective-permute-done | bytes 196640 | tf_op jit(solution)/shard_map/ppermute | solution.py:333
  10.0 0.7 %collective-permute-start.3 = (bf16[768,128]{1,0:T(8,128)(2,1)S(1)}, bf16[768,128]{1,0:T(8,128)(2,1)S(1)}, u32[]{:S(2)}, u32[]{:S(2)}) collective-permute-start(bf16[768,128]{1,0:T(8,128)(2,1)S(1)} %aggregate.2.refs_0_), channel_id=1, source_target_pairs={{0,24},{1,25},{2,26},{3,27},{4,28},{5,29},{6,30},{7,31}} | collective-permute-start | bytes 589832 | tf_op jit(solution)/shard_map/ppermute | solution.py:350
  10.6 0.7 %collective-permute-start.5 = (bf16[768,128]{1,0:T(8,128)(2,1)S(1)}, bf16[768,128]{1,0:T(8,128)(2,1)S(1)}, u32[]{:S(2)}, u32[]{:S(2)}) collective-permute-start(bf16[768,128]{1,0:T(8,128)(2,1)S(1)} %aggregate.2.refs_0_), channel_id=1, source_target_pairs={{8,24},{9,25},{10,26},{11,27},{12,28},{13,29},{14,30},{15,31}} | collective-permute-start | bytes 589832 | tf_op jit(solution)/shard_map/ppermute | solution.py:350
  11.3 1.0 %aggregate.3.rows_in = bf16[768,128]{1,0:T(8,128)(2,1)S(1)} custom-call(bf16[768,128]{1,0:T(8,128)(2,1)S(1)} %get-tuple-element.24.own, bf16[768,128]{1,0:T(8,128)(2,1)S(1)} %collective-permute-done.outer, bf16[768,128]{1,0:T(8,128)(2,1)S(1)} %collective-permute-done.1.inner, bf16[12,128,128]{2,1,0:T(8,128)(2,1)S(1)} %get-tuple-element.25.tiles, ...), custom_call_target="tpu_custom_call" | custom-call | tf_op jit(solution)/shard_map/aggregate/pallas_call | solution.py:110
  12.3 4.7 %collective-permute-start.2 = (bf16[768,128]{1,0:T(8,128)(2,1)S(1)}, bf16[768,128]{1,0:T(8,128)(2,1)S(1)}, u32[]{:S(2)}, u32[]{:S(2)}) collective-permute-start(bf16[768,128]{1,0:T(8,128)(2,1)S(1)} %aggregate.3.rows_in), channel_id=1, source_target_pairs={{0,8},{8,16},{16,24},{1,9},{9,17},{17,25},{2,10},{10,18},{18,26},{... | collective-permute-start | bytes 589832 | tf_op jit(solution)/shard_map/ppermute | solution.py:350
  17.1 2.0 %pregate.1 = (f32[768,2048]{1,0:T(8,128)S(1)}, bf16[1,768,512]{2,1,0:T(8,128)(2,1)}) custom-call(bf16[768,128]{1,0:T(8,128)(2,1)S(1)} %aggregate.3.rows_in, bf16[128,512]{1,0:T(8,128)(2,1)S(1)} %get-tuple-element.26.w_conv.refs_1_, f32[1,512]{1,0:T(1,128)S(1)} %get-tuple-element.27.b_conv.refs_2_, bf16[512,2048]{1,0:T(8,128)(2,1)S(1)} %get-tuple-element.28.w_input.refs_3_, ...), custom_call_target="tpu_custom_call" | custom-call | flops 1610612736 | bytes 6291456 | tf_op jit(solution)/shard_map/pregate/pallas_call | solution.py:150
  19.1 0.0 collective-permute-done.3.refs_0_
  19.1 1.3 %collective-permute-start.4 = (bf16[768,128]{1,0:T(8,128)(2,1)S(1)}, bf16[768,128]{1,0:T(8,128)(2,1)S(1)}, u32[]{:S(2)}, u32[]{:S(2)}) collective-permute-start(bf16[768,128]{1,0:T(8,128)(2,1)S(1)} %collective-permute-done.3.refs_0_), channel_id=1, source_target_pairs={{24,16},{25,17},{26,18},{27,19},{28,20},{29,21},{30,22},{31,23}} | collective-permute-start | bytes 589832 | tf_op jit(solution)/shard_map/ppermute | solution.py:384
  20.4 0.0 collective-permute-done.5.refs_0_
  20.4 6.9 %collective-permute-done.4.refs_0_ = bf16[768,128]{1,0:T(8,128)(2,1)S(1)} collective-permute-done((bf16[768,128]{1,0:T(8,128)(2,1)S(1)}, bf16[768,128]{1,0:T(8,128)(2,1)S(1)}, u32[]{:S(2)}, u32[]{:S(2)}) %collective-permute-start.4) | collective-permute-done | bytes 196640 | tf_op jit(solution)/shard_map/ppermute | solution.py:384
  27.3 1.8 %shard_map.102 = (bf16[1,768,512]{2,1,0:T(8,128)(2,1)}, bf16[768,512]{1,0:T(8,128)(2,1)S(1)}, f32[768,512]{1,0:T(8,128)S(1)}) custom-call(bf16[768,128]{1,0:T(8,128)(2,1)S(1)} %collective-permute-done.4.refs_0_, bf16[128,512]{1,0:T(8,128)(2,1)S(1)} %get-tuple-element.26.w_conv.refs_1_, ...), custom_call_target="tpu_custom_call", output_to_operand_aliasing={{0}: (6, {}), {2}: (8, {}), {1}: (7, {})} | custom-call | flops 3221225472 | bytes 3145728 | tf_op jit(solution)/shard_map/pallas_call | solution.py:224
  29.1 0.0 collective-permute-done.2.refs_0_
  29.1 7.1 %finish.1 = (bf16[1,768,512]{2,1,0:T(8,128)(2,1)}, f32[768,512]{1,0:T(8,128)S(1)}) custom-call(bf16[768,128]{1,0:T(8,128)(2,1)S(1)} %collective-permute-done.2.refs_0_, bf16[128,512]{1,0:T(8,128)(2,1)S(1)} %get-tuple-element.26.w_conv.refs_1_, f32[1,512]{1,0:T(1,128)S(1)} %get-tuple-element.27.b_conv.refs_2_, ...), custom_call_target="tpu_custom_call", output_to_operand_aliasing={{0}: (6, {}), {1}: (9, {})} | custom-call | flops 4831838208 | bytes 3145728 | tf_op jit(solution)/shard_map/finish/pallas_call | solution.py:294
  (3 shorter events, 0.1 us)
Async XLA Ops:
  0.0 6.7 %collective-permute-start.1 = (bf16[768,128]{1,0:T(8,128)(2,1)}, bf16[768,128]{1,0:T(8,128)(2,1)S(1)}, u32[]{:S(2)}, u32[]{:S(2)}) collective-permute-start(bf16[768,128]{1,0:T(8,128)(2,1)} %bitcast.5), channel_id=1, source_target_pairs={{0,1},{2,3},{4,5},{6,7},{1,0},{3,2},{5,4},{7,6},{8,9},{10,11},{12,... | collective-permute-start | bytes 589832 | tf_op jit(solution)/shard_map/ppermute | solution.py:334
  0.0 9.9 %collective-permute-start = (bf16[768,128]{1,0:T(8,128)(2,1)}, bf16[768,128]{1,0:T(8,128)(2,1)S(1)}, u32[]{:S(2)}, u32[]{:S(2)}) collective-permute-start(bf16[768,128]{1,0:T(8,128)(2,1)} %bitcast.6), channel_id=1, source_target_pairs={{1,2},{3,4},{5,6},{2,1},{4,3},{6,5},{9,10},{11,12},{13,14},{10,9},... | collective-permute-start | bytes 589832 | tf_op jit(solution)/shard_map/ppermute | solution.py:333
  10.0 9.1 %collective-permute-start.3 = (bf16[768,128]{1,0:T(8,128)(2,1)S(1)}, bf16[768,128]{1,0:T(8,128)(2,1)S(1)}, u32[]{:S(2)}, u32[]{:S(2)}) collective-permute-start(bf16[768,128]{1,0:T(8,128)(2,1)S(1)} %aggregate.2.refs_0_), channel_id=1, source_target_pairs={{0,24},{1,25},{2,26},{3,27},{4,28},{5,29},{6,30},{7,31}} | collective-permute-start | bytes 589832 | tf_op jit(solution)/shard_map/ppermute | solution.py:350
  10.6 9.8 %collective-permute-start.5 = (bf16[768,128]{1,0:T(8,128)(2,1)S(1)}, bf16[768,128]{1,0:T(8,128)(2,1)S(1)}, u32[]{:S(2)}, u32[]{:S(2)}) collective-permute-start(bf16[768,128]{1,0:T(8,128)(2,1)S(1)} %aggregate.2.refs_0_), channel_id=1, source_target_pairs={{8,24},{9,25},{10,26},{11,27},{12,28},{13,29},{14,30},{15,31}} | collective-permute-start | bytes 589832 | tf_op jit(solution)/shard_map/ppermute | solution.py:350
  12.3 16.8 %collective-permute-start.2 = (bf16[768,128]{1,0:T(8,128)(2,1)S(1)}, bf16[768,128]{1,0:T(8,128)(2,1)S(1)}, u32[]{:S(2)}, u32[]{:S(2)}) collective-permute-start(bf16[768,128]{1,0:T(8,128)(2,1)S(1)} %aggregate.3.rows_in), channel_id=1, source_target_pairs={{0,8},{8,16},{16,24},{1,9},{9,17},{17,25},{2,10},{10,18},{18,26},{... | collective-permute-start | bytes 589832 | tf_op jit(solution)/shard_map/ppermute | solution.py:350
  19.1 8.2 %collective-permute-start.4 = (bf16[768,128]{1,0:T(8,128)(2,1)S(1)}, bf16[768,128]{1,0:T(8,128)(2,1)S(1)}, u32[]{:S(2)}, u32[]{:S(2)}) collective-permute-start(bf16[768,128]{1,0:T(8,128)(2,1)S(1)} %collective-permute-done.3.refs_0_), channel_id=1, source_target_pairs={{24,16},{25,17},{26,18},{27,19},{28,20},{29,21},{30,22},{31,23}} | collective-permute-start | bytes 589832 | tf_op jit(solution)/shard_map/ppermute | solution.py:384

commit v8 on v7

--- a/solution.py
+++ b/solution.py
@@ -165,7 +165,7 @@
     )(rows_in, w_conv, b_conv, w_input, b_gates, *([] if fresh else [out]))
 
 
-def gate_step(inner, pre, w_input, w_state, b_gates, hidden, cell, target, rows, store_cell=True):
+def gate_step(inner, pre, w_input, w_state, b_gates, hidden, held, cell, target, rows):
     width = w_state.shape[0]
     chunk = width // 2
     for low in range(0, width, chunk):
@@ -184,8 +184,8 @@
         part = slice(low, low + chunk)
         fresh = (0.5 * jnp.tanh(0.5 * gates[0]) + 0.5) * jnp.tanh(gates[2])
         if hidden is not None:
-            fresh += (0.5 * jnp.tanh(0.5 * gates[1]) + 0.5) * cell[rows, part]
-        if store_cell:
+            fresh += (0.5 * jnp.tanh(0.5 * gates[1]) + 0.5) * held[rows, part]
+        if cell is not None:
             cell[rows, part] = fresh
         shown = (0.5 * jnp.tanh(0.5 * gates[3]) + 0.5) * jnp.tanh(fresh)
         target[rows, part] = shown.astype(BF16)
@@ -193,7 +193,7 @@
 
 def step_kernel(on_first, on_later, inputs, *refs):
     rows_in, w_conv, b_conv, w_input, w_state, b_gates = refs[:6]
-    before = refs[7] if inputs > 7 else None
+    before, held = refs[7:9] if inputs > 7 else (None, None)
     _, hidden, cell, conv = refs[inputs:]
     me = lax.axis_index("snap")
     every = slice(None)
@@ -201,12 +201,18 @@
     def taken(first):
         convolve(rows_in, w_conv, b_conv, conv)
         source = None if first else before
-        gate_step(conv, None, w_input, w_state, b_gates, source, cell, hidden, every)
+        gate_step(conv, None, w_input, w_state, b_gates, source, held, cell, hidden, every)
 
     for device in on_first:
         pl.when(me == device)(functools.partial(taken, True))
     if on_later is not None:
         pl.when(me >= on_later)(functools.partial(taken, False))
+    elif before is not None:
+
+        @pl.when(me > on_first[0])
+        def _():
+            hidden[...] = before[...]
+            cell[...] = held[...]
 
 
 def step(on_first, on_later, rows_in, weights, out, state):
@@ -240,7 +246,7 @@
 def finish_kernel(snaps, offset, *refs):
     rows_in, w_conv, b_conv, w_input, w_state, b_gates, _, pre = refs[:8]
     out, cell, conv, middle, shown, sems = refs[-6:]
-    before = refs[8] if snaps >= 3 else None
+    before, held = refs[8:10] if snaps >= 3 else (None, None)
     me = lax.axis_index("snap")
     rows = shown.shape[0]
     blocks = LAST_BLOCKS if rows % (16 * LAST_BLOCKS) == 0 else 1
@@ -254,13 +260,13 @@
             sems.at[block],
         )
 
-    def run(source, begins, carried):
+    def run(source, begins, carried, kept):
         def taken(part):
             convolve(rows_in, w_conv, b_conv, conv, part)
-            gate_step(conv, None, w_input, w_state, b_gates, source, cell, middle, part)
+            gate_step(conv, None, w_input, w_state, b_gates, source, held, cell, middle, part)
 
         def last(block, part):
-            gate_step(None, pre, w_input, w_state, b_gates, carried, cell, shown, part, False)
+            gate_step(None, pre, w_input, w_state, b_gates, carried, kept, None, shown, part)
             sent(block).start()
 
         parts = [slice(block * share, (block + 1) * share) for block in range(blocks)]
@@ -271,12 +277,12 @@
                 taken(parts[block + 1])
             last(block, part)
 
-    pl.when(me == 0)(functools.partial(run, None, False, None))
+    pl.when(me == 0)(functools.partial(run, None, False, None, None))
     if snaps > 1:
-        middle_now = before if snaps == 3 else middle
-        pl.when(me == 1)(functools.partial(run, None, snaps != 3, middle_now))
+        carried, kept = (before, held) if snaps == 3 else (middle, cell)
+        pl.when(me == 1)(functools.partial(run, None, snaps != 3, carried, kept))
     if snaps > 2:
-        pl.when(me > 1)(functools.partial(run, before, True, middle))
+        pl.when(me > 1)(functools.partial(run, before, True, middle, cell))
     for block in range(blocks):
         sent(block).wait()
 

time: 36.5 us -> 36.5 us (level)
  no operation moved by 1% of the time
where the time goes in v8:
time: 36.5 us; the launch traced here: 36.3 us
  Pallas kernels  14.5 us (40%)
  starting transfers between devices  10.8 us (30%)
  waiting for transfers between devices  10.1 us (28%)
  between operations  0.93 us (3%)
    pallas_call x1, Pallas kernels, finish(): pl.pallas_call(functools.partial(finish_kernel, snaps, offset), out_shape...  7.05 us
    ppermute x1, waiting for transfers between devices, shards(): lax.ppermute(arrived[last, part], 'snap', [(last, last - 1)])  6.87 us
    ppermute x3, starting transfers between devices, shifted(): return lax.ppermute(ready if hop > 1 else whole, 'snap', routes)  6.07 us
    ppermute x1, starting transfers between devices, shards(): outer = lax.ppermute(features[0], 'vert', odd + [(b, a) for a, b in odd])  3.44 us
    ppermute x1, waiting for transfers between devices, shards(): outer = lax.ppermute(features[0], 'vert', odd + [(b, a) for a, b in odd])  3.23 us
    pallas_call x1, Pallas kernels, load(): pl.pallas_call(functools.partial(load_kernel, len(arrays)), out_shape=[ja...  2.58 us
    pallas_call x1, Pallas kernels, pregate(): pl.pallas_call(pregate_kernel, out_shape=[jax.ShapeDtypeStruct((rows, gat...  1.99 us
    pallas_call x3, Pallas kernels, step(): pl.pallas_call(functools.partial(step_kernel, on_first, on_later, len(ope...  1.81 us
  transfers between devices with their start and end apart: 6, of which 2 were waited for; matrix products, arithmetic and copies ran while one was open for 0% of the time, Pallas kernels for 20%

profile of v8, /device:TPU:20, one launch (start us, length us, event | category | flops | bytes accessed | tf_op | source)
XLA Modules:
  0.0 36.3 jit_solution(2952369330484119065)
XLA Ops:
  0.0 0.0 collective-permute-start.1
  0.0 3.4 %collective-permute-start = (bf16[768,128]{1,0:T(8,128)(2,1)}, bf16[768,128]{1,0:T(8,128)(2,1)S(1)}, u32[]{:S(2)}, u32[]{:S(2)}) collective-permute-start(bf16[768,128]{1,0:T(8,128)(2,1)} %bitcast.6), channel_id=1, source_target_pairs={{1,2},{3,4},{5,6},{2,1},{4,3},{6,5},{9,10},{11,12},{13,14},{10,9},... | collective-permute-start | bytes 589832 | tf_op jit(solution)/shard_map/ppermute | solution.py:339
  4.1 2.6 %load.1 = (bf16[768,128]{1,0:T(8,128)(2,1)S(1)}, bf16[12,128,128]{2,1,0:T(8,128)(2,1)S(1)}, bf16[128,512]{1,0:T(8,128)(2,1)S(1)}, f32[1,512]{1,0:T(1,128)S(1)}, ...) custom-call(bf16[768,128]{1,0:T(8,128)(2,1)} %bitcast.7, ...), custom_call_target="tpu_custom_call" | custom-call | bytes 9850880 | tf_op jit(solution)/shard_map/load/pallas_call | solution.py:38
  6.7 0.0 collective-permute-done.1.inner
  6.7 3.2 %collective-permute-done.outer = bf16[768,128]{1,0:T(8,128)(2,1)S(1)} collective-permute-done((bf16[768,128]{1,0:T(8,128)(2,1)}, bf16[768,128]{1,0:T(8,128)(2,1)S(1)}, u32[]{:S(2)}, u32[]{:S(2)}) %collective-permute-start) | collective-permute-done | bytes 196640 | tf_op jit(solution)/shard_map/ppermute | solution.py:339
  10.0 0.7 %collective-permute-start.3 = (bf16[768,128]{1,0:T(8,128)(2,1)S(1)}, bf16[768,128]{1,0:T(8,128)(2,1)S(1)}, u32[]{:S(2)}, u32[]{:S(2)}) collective-permute-start(bf16[768,128]{1,0:T(8,128)(2,1)S(1)} %aggregate.2.refs_0_), channel_id=1, source_target_pairs={{0,24},{1,25},{2,26},{3,27},{4,28},{5,29},{6,30},{7,31}} | collective-permute-start | bytes 589832 | tf_op jit(solution)/shard_map/ppermute | solution.py:356
  10.6 0.7 %collective-permute-start.5 = (bf16[768,128]{1,0:T(8,128)(2,1)S(1)}, bf16[768,128]{1,0:T(8,128)(2,1)S(1)}, u32[]{:S(2)}, u32[]{:S(2)}) collective-permute-start(bf16[768,128]{1,0:T(8,128)(2,1)S(1)} %aggregate.2.refs_0_), channel_id=1, source_target_pairs={{8,24},{9,25},{10,26},{11,27},{12,28},{13,29},{14,30},{15,31}} | collective-permute-start | bytes 589832 | tf_op jit(solution)/shard_map/ppermute | solution.py:356
  11.3 1.0 %aggregate.3.rows_in = bf16[768,128]{1,0:T(8,128)(2,1)S(1)} custom-call(bf16[768,128]{1,0:T(8,128)(2,1)S(1)} %get-tuple-element.24.own, bf16[768,128]{1,0:T(8,128)(2,1)S(1)} %collective-permute-done.outer, bf16[768,128]{1,0:T(8,128)(2,1)S(1)} %collective-permute-done.1.inner, bf16[12,128,128]{2,1,0:T(8,128)(2,1)S(1)} %get-tuple-element.25.tiles, ...), custom_call_target="tpu_custom_call" | custom-call | tf_op jit(solution)/shard_map/aggregate/pallas_call | solution.py:110
  12.3 4.7 %collective-permute-start.2 = (bf16[768,128]{1,0:T(8,128)(2,1)S(1)}, bf16[768,128]{1,0:T(8,128)(2,1)S(1)}, u32[]{:S(2)}, u32[]{:S(2)}) collective-permute-start(bf16[768,128]{1,0:T(8,128)(2,1)S(1)} %aggregate.3.rows_in), channel_id=1, source_target_pairs={{0,8},{8,16},{16,24},{1,9},{9,17},{17,25},{2,10},{10,18},{18,26},{... | collective-permute-start | bytes 589832 | tf_op jit(solution)/shard_map/ppermute | solution.py:356
  17.1 2.0 %pregate.1 = (f32[768,2048]{1,0:T(8,128)S(1)}, bf16[1,768,512]{2,1,0:T(8,128)(2,1)}) custom-call(bf16[768,128]{1,0:T(8,128)(2,1)S(1)} %aggregate.3.rows_in, bf16[128,512]{1,0:T(8,128)(2,1)S(1)} %get-tuple-element.26.w_conv.refs_1_, f32[1,512]{1,0:T(1,128)S(1)} %get-tuple-element.27.b_conv.refs_2_, bf16[512,2048]{1,0:T(8,128)(2,1)S(1)} %get-tuple-element.28.w_input.refs_3_, ...), custom_call_target="tpu_custom_call" | custom-call | flops 1610612736 | bytes 6291456 | tf_op jit(solution)/shard_map/pregate/pallas_call | solution.py:150
  19.1 0.0 collective-permute-done.3.refs_0_
  19.1 1.3 %collective-permute-start.4 = (bf16[768,128]{1,0:T(8,128)(2,1)S(1)}, bf16[768,128]{1,0:T(8,128)(2,1)S(1)}, u32[]{:S(2)}, u32[]{:S(2)}) collective-permute-start(bf16[768,128]{1,0:T(8,128)(2,1)S(1)} %collective-permute-done.3.refs_0_), channel_id=1, source_target_pairs={{24,16},{25,17},{26,18},{27,19},{28,20},{29,21},{30,22},{31,23}} | collective-permute-start | bytes 589832 | tf_op jit(solution)/shard_map/ppermute | solution.py:390
  20.4 0.0 collective-permute-done.5.refs_0_
  20.4 6.9 %collective-permute-done.4.refs_0_ = bf16[768,128]{1,0:T(8,128)(2,1)S(1)} collective-permute-done((bf16[768,128]{1,0:T(8,128)(2,1)S(1)}, bf16[768,128]{1,0:T(8,128)(2,1)S(1)}, u32[]{:S(2)}, u32[]{:S(2)}) %collective-permute-start.4) | collective-permute-done | bytes 196640 | tf_op jit(solution)/shard_map/ppermute | solution.py:390
  27.3 1.8 %shard_map.102 = (bf16[1,768,512]{2,1,0:T(8,128)(2,1)}, bf16[768,512]{1,0:T(8,128)(2,1)S(1)}, f32[768,512]{1,0:T(8,128)S(1)}) custom-call(bf16[768,128]{1,0:T(8,128)(2,1)S(1)} %collective-permute-done.4.refs_0_, bf16[128,512]{1,0:T(8,128)(2,1)S(1)} %get-tuple-element.26.w_conv.refs_1_, ...), custom_call_target="tpu_custom_call", output_to_operand_aliasing={{0}: (6, {}), {2}: (8, {}), {1}: (7, {})} | custom-call | flops 3221225472 | bytes 3145728 | tf_op jit(solution)/shard_map/pallas_call | solution.py:230
  29.1 0.0 collective-permute-done.2.refs_0_
  29.1 7.1 %finish.1 = (bf16[1,768,512]{2,1,0:T(8,128)(2,1)}, f32[768,512]{1,0:T(8,128)S(1)}) custom-call(bf16[768,128]{1,0:T(8,128)(2,1)S(1)} %collective-permute-done.2.refs_0_, bf16[128,512]{1,0:T(8,128)(2,1)S(1)} %get-tuple-element.26.w_conv.refs_1_, f32[1,512]{1,0:T(1,128)S(1)} %get-tuple-element.27.b_conv.refs_2_, ...), custom_call_target="tpu_custom_call", output_to_operand_aliasing={{0}: (6, {}), {1}: (9, {})} | custom-call | flops 4831838208 | bytes 3145728 | tf_op jit(solution)/shard_map/finish/pallas_call | solution.py:300
  (3 shorter events, 0.1 us)
Async XLA Ops:
  0.0 6.7 %collective-permute-start.1 = (bf16[768,128]{1,0:T(8,128)(2,1)}, bf16[768,128]{1,0:T(8,128)(2,1)S(1)}, u32[]{:S(2)}, u32[]{:S(2)}) collective-permute-start(bf16[768,128]{1,0:T(8,128)(2,1)} %bitcast.5), channel_id=1, source_target_pairs={{0,1},{2,3},{4,5},{6,7},{1,0},{3,2},{5,4},{7,6},{8,9},{10,11},{12,... | collective-permute-start | bytes 589832 | tf_op jit(solution)/shard_map/ppermute | solution.py:340
  0.0 9.9 %collective-permute-start = (bf16[768,128]{1,0:T(8,128)(2,1)}, bf16[768,128]{1,0:T(8,128)(2,1)S(1)}, u32[]{:S(2)}, u32[]{:S(2)}) collective-permute-start(bf16[768,128]{1,0:T(8,128)(2,1)} %bitcast.6), channel_id=1, source_target_pairs={{1,2},{3,4},{5,6},{2,1},{4,3},{6,5},{9,10},{11,12},{13,14},{10,9},... | collective-permute-start | bytes 589832 | tf_op jit(solution)/shard_map/ppermute | solution.py:339
  10.0 9.1 %collective-permute-start.3 = (bf16[768,128]{1,0:T(8,128)(2,1)S(1)}, bf16[768,128]{1,0:T(8,128)(2,1)S(1)}, u32[]{:S(2)}, u32[]{:S(2)}) collective-permute-start(bf16[768,128]{1,0:T(8,128)(2,1)S(1)} %aggregate.2.refs_0_), channel_id=1, source_target_pairs={{0,24},{1,25},{2,26},{3,27},{4,28},{5,29},{6,30},{7,31}} | collective-permute-start | bytes 589832 | tf_op jit(solution)/shard_map/ppermute | solution.py:356
  10.6 9.8 %collective-permute-start.5 = (bf16[768,128]{1,0:T(8,128)(2,1)S(1)}, bf16[768,128]{1,0:T(8,128)(2,1)S(1)}, u32[]{:S(2)}, u32[]{:S(2)}) collective-permute-start(bf16[768,128]{1,0:T(8,128)(2,1)S(1)} %aggregate.2.refs_0_), channel_id=1, source_target_pairs={{8,24},{9,25},{10,26},{11,27},{12,28},{13,29},{14,30},{15,31}} | collective-permute-start | bytes 589832 | tf_op jit(solution)/shard_map/ppermute | solution.py:356
  12.3 16.8 %collective-permute-start.2 = (bf16[768,128]{1,0:T(8,128)(2,1)S(1)}, bf16[768,128]{1,0:T(8,128)(2,1)S(1)}, u32[]{:S(2)}, u32[]{:S(2)}) collective-permute-start(bf16[768,128]{1,0:T(8,128)(2,1)S(1)} %aggregate.3.rows_in), channel_id=1, source_target_pairs={{0,8},{8,16},{16,24},{1,9},{9,17},{17,25},{2,10},{10,18},{18,26},{... | collective-permute-start | bytes 589832 | tf_op jit(solution)/shard_map/ppermute | solution.py:356
  19.1 8.2 %collective-permute-start.4 = (bf16[768,128]{1,0:T(8,128)(2,1)S(1)}, bf16[768,128]{1,0:T(8,128)(2,1)S(1)}, u32[]{:S(2)}, u32[]{:S(2)}) collective-permute-start(bf16[768,128]{1,0:T(8,128)(2,1)S(1)} %collective-permute-done.3.refs_0_), channel_id=1, source_target_pairs={{24,16},{25,17},{26,18},{27,19},{28,20},{29,21},{30,22},{31,23}} | collective-permute-start | bytes 589832 | tf_op jit(solution)/shard_map/ppermute | solution.py:390
